TPU v7x, 32 devices: a whole 2x2x4 slice. The times are simulated.
32 devices in a mesh: shot: 2 (over y), depth: 2 (over core), lat: 8 (over z, x).
Axes of the slice: x: 2, y: 2, z: 4, core: 2. Of those that a mesh axis runs over, the one named last changes fastest.
Arguments:
- sources: float32 [6, 2, 32, 4096], P('shot', None, 'depth', 'lat'), parts along dimension 0, may hold values from -6 to 6
- blocks: float32 [4, 32, 7, 2, 128, 128], P(('shot', 'depth'), 'lat'), parts along dimension 0, may hold values from -0.125 to 0.125
- block_cols: int32 [2, 32, 7], P('depth', 'lat'), may hold values from 0 to 31, as said below
- refl_level: int32 [4096], P('lat'), may hold values from 0 to 1
- refl_coef: float32 [2, 4096], P(None, 'lat'), may hold values from -0.5 to 0.5
Outputs:
- bottom: float32 [6, 2, 32, 4096], P('shot', None, 'depth', 'lat'), parts along dimension 0
There are 2 independent parts, one for each index of `shot`. A program takes and returns all parts, laid end to end along the dimension named above; an argument that names none is the same for every part. Nothing has to cross between parts.
Inputs may be any that keep to these rules, and one draw needn't show every extreme that they name: block_cols[l, b, 0] = b, and every entry of row b lies within 4 block rows of b; a row may name a column twice.
All inputs are finite; a program needn't handle non-finite values.
Results may differ from a plain program's by a relative error of at most 0.0001.
Values sent between devices are 32-bit elements; how exact they have to be, the bound alone decides.
No kernel may reach another device: no remote copies, remote signals or barrier semaphores. Data moves between devices by JAX's collectives and lax.ppermute only.
A program may use at most 64 MiB of HBM per device.

v0:
```python
import functools

import jax
import jax.numpy as jnp
from jax import lax
from jax.experimental import pallas as pl
from jax.experimental.pallas import tpu as pltpu
from jax.sharding import PartitionSpec as P

VMEM = pl.BlockSpec(memory_space=pltpu.VMEM)
SMEM = pl.BlockSpec(memory_space=pltpu.SMEM)
HBM = pl.BlockSpec(memory_space=pltpu.HBM)
MIB = 1 << 20


def reflected(field_re, field_im, coef_re, coef_im):
    return (
        field_re + coef_re * field_re - coef_im * field_im,
        field_im + coef_re * field_im + coef_im * field_re,
    )


def entered(sources, coef):
    panels = [
        reflected(sources[k, 0], sources[k, 1], coef[0:1, :], coef[1:2, :])
        for k in range(sources.shape[0])
    ]
    return jnp.concatenate([re for re, _ in panels] + [im for _, im in panels], axis=0)


def enter_kernel(
    sources, refl_level, refl_coef, total, first_coef, next_coef, held, level_held, coef_held, sems
):
    copies = [
        pltpu.make_async_copy(a, b, sems.at[i])
        for i, (a, b) in enumerate(
            ((sources, held), (refl_level, level_held), (refl_coef, coef_held))
        )
    ]
    for copy in copies:
        copy.start()
    for copy in copies:
        copy.wait()
    first_coef[...] = jnp.where(level_held[...] == 0, coef_held[...], 0.0)
    next_coef[...] = jnp.where(level_held[...] == 1, coef_held[...], 0.0)
    total[...] = entered(held, first_coef)


def head_and_tail(value):
    head = value.astype(jnp.bfloat16)
    return head, (value - head.astype(jnp.float32)).astype(jnp.bfloat16)


def pieces(value):
    return jnp.concatenate(head_and_tail(value), axis=0)


def product(left, high, low):
    rows = left.shape[0] // 2
    high = high.reshape(high.shape[0] * high.shape[1], high.shape[2])
    low = low.reshape(high.shape)
    both = jnp.dot(left, high, preferred_element_type=jnp.float32)
    cross = jnp.dot(left[:rows], low, preferred_element_type=jnp.float32)
    return both[:rows] + both[rows:] + cross


def prepare_kernel(
    level, own_cols, other_cols, own, received, field, high, low, sums, held, left, sems
):
    block_rows, per_row, _, size, _ = held.shape
    here = lax.axis_index("depth") == level
    first_row = lax.axis_index("lat") * block_rows
    for b in range(block_rows):

        @pl.when(here)
        def _():
            pltpu.make_async_copy(own.at[0, b], held.at[b], sems.at[b]).start()

        @pl.when(jnp.logical_not(here))
        def _():
            pltpu.make_async_copy(received.at[0, b], held.at[b], sems.at[b]).start()

    span = 2 * block_rows + 1
    zeros = jnp.zeros((size, 2 * size), jnp.bfloat16)

    def clear(b, o):
        high[b, o] = zeros
        low[b, o] = zeros

    rows_at, rows_repeated = [], []
    for b in range(block_rows):
        first = first_row + b - block_rows
        at = [
            jnp.where(here, own_cols[0, b, j], other_cols[0, b, j]) - first
            for j in range(per_row)
        ]
        bits = [jnp.left_shift(1, a) for a in at]
        present = functools.reduce(jnp.bitwise_or, bits)
        repeated = sum(bits) != present
        rows_at.append(at)
        rows_repeated.append(repeated)
        absent = (1 << span) - 1 - present
        if span - per_row == 2:
            clear(b, sum(jnp.where(absent % (2 << o) == 0, 1, 0) for o in range(span - 1)))
            clear(b, sum(jnp.where(absent >= (2 << o), 1, 0) for o in range(span - 1)))
        else:
            repeated = True

        @pl.when(repeated)
        def _():
            def clear_one(o, carry):
                @pl.when(jnp.bitwise_and(jnp.right_shift(absent, o), 1) == 1)
                def _():
                    clear(b, o)

                return carry

            lax.fori_loop(0, span, clear_one, 0)

    left[...] = pieces(field[...])
    for b in range(block_rows):
        at = rows_at[b]
        pltpu.make_async_copy(own.at[0, b], held.at[b], sems.at[b]).wait()

        @pl.when(rows_repeated[b])
        def _():
            for j in reversed(range(1, per_row)):
                target = jnp.int32(per_row)
                for i in range(j):
                    target = jnp.where(at[i] == at[j], i, target)

                @pl.when(target < per_row)
                def _():
                    held[b, target] = held[b, target] + held[b, j]

        def split(n, carry):
            rows = pl.ds(pl.multiple_of(n * 16, 16), 16)
            for j in reversed(range(per_row)):
                head, tail = head_and_tail(
                    jnp.concatenate([held[b, j, 0, rows], held[b, j, 1, rows]], axis=1)
                )
                high[b, at[j], rows] = head
                low[b, at[j], rows] = tail
            return carry

        lax.fori_loop(0, size // 16, split, 0)
    for b in range(block_rows):
        band = slice(block_rows - b, 2 * block_rows - b)
        sums[b] = product(left[...], high[b, band], low[b, band])


def add_halos(swapped, diagonal, high, low, sums, finish):
    block_rows, span, size, _ = high.shape

    def both(before, after):
        for b in range(block_rows):
            ahead = slice(0, block_rows - b)
            behind = slice(span - 1 - b, span)
            finish(
                b,
                sums[b]
                + product(before[:, b * size :], high[b, ahead], low[b, ahead])
                + product(after[:, : (b + 1) * size], high[b, behind], low[b, behind]),
            )

    swapped, diagonal = pieces(swapped), pieces(diagonal)
    even = lax.axis_index("lat") % 2 == 0

    @pl.when(even)
    def _():
        both(diagonal, swapped)

    @pl.when(jnp.logical_not(even))
    def _():
        both(swapped, diagonal)


def leaving(value):
    channels, size = value.shape[0] // 2, value.shape[1] // 2
    return (
        value[:channels, :size] - value[channels:, size:],
        value[:channels, size:] + value[channels:, :size],
    )


def first_level_kernel(
    swapped, diagonal, swapped_coef, diagonal_coef, high, low, sums, next_coef, out
):
    def finish(b, value):
        re, im = leaving(value)
        channels, size = re.shape
        lanes = slice(b * size, (b + 1) * size)
        re, im = reflected(re, im, next_coef[0:1, lanes], next_coef[1:2, lanes])
        out[:channels, lanes] = re
        out[channels:, lanes] = im

    add_halos(
        entered(swapped, swapped_coef),
        entered(diagonal, diagonal_coef),
        high,
        low,
        sums,
        finish,
    )


def bottom_kernel(swapped, diagonal, high, low, sums, out, held, sems):
    panels, _, part, _ = out.shape
    block_rows, _, size, _ = high.shape

    def copy_out(b):
        lanes = pl.ds(b * size, size)
        return pltpu.make_async_copy(
            held.at[b], out.at[:, :, :, lanes], sems.at[b]
        )

    def finish(b, value):
        re, im = leaving(value)
        held[b, :, 0] = re.reshape(panels, part, size)
        held[b, :, 1] = im.reshape(panels, part, size)
        copy_out(b).start()

    add_halos(swapped[...], diagonal[...], high, low, sums, finish)
    for b in range(block_rows):
        copy_out(b).wait()


def in_hbm(value):
    return pltpu.with_memory_space_constraint(value, pltpu.HBM)


def params(mib):
    return pltpu.CompilerParams(vmem_limit_bytes=mib * MIB)


def cost(flops, transferred):
    return pl.CostEstimate(flops=flops, bytes_accessed=transferred, transcendentals=0)


def per_device(sources, blocks, block_cols, refl_level, refl_coef):
    lat_count = lax.axis_size("lat")
    panels, _, part, points = sources.shape
    _, block_rows, per_row, _, size, _ = blocks.shape
    channels = panels * part
    f32, bf16 = jnp.float32, jnp.bfloat16
    axes = ("depth", "lat")
    over_depth = [(0, 1), (1, 0)]
    even = range(0, lat_count - 1, 2)
    uneven = range(1, lat_count - 1, 2)
    alone_even = range(lat_count - lat_count % 2, lat_count)
    alone_uneven = [0] + list(range(lat_count - 1 + lat_count % 2, lat_count))

    def over_lat(firsts, alone):
        pairs = [(d * lat_count + i, d * lat_count + i + 1) for d in range(2) for i in firsts]
        pairs += [(i, lat_count + i) for i in alone]
        return pairs + [(j, i) for i, j in pairs]

    across = over_lat(uneven, alone_uneven)
    beside = over_lat(even, alone_even)
    other_blocks = lax.ppermute(blocks, "depth", over_depth)
    diagonal = lax.ppermute(sources, axes, across)
    swapped = lax.ppermute(sources, axes, beside)
    other_cols = lax.ppermute(block_cols, "depth", over_depth)
    field_shape = jax.ShapeDtypeStruct((2 * channels, points), f32)
    coef_shape = jax.ShapeDtypeStruct((2, points), f32)
    total, first_coef, next_coef = pl.pallas_call(
        enter_kernel,
        out_shape=[field_shape, coef_shape, coef_shape],
        in_specs=[HBM] * 3,
        out_specs=[VMEM] * 3,
        scratch_shapes=[
            pltpu.VMEM(sources.shape, f32),
            pltpu.VMEM((1, points), jnp.int32),
            pltpu.VMEM((2, points), f32),
            pltpu.SemaphoreType.DMA((3,)),
        ],
        compiler_params=params(4),
        name="enter",
    )(in_hbm(sources), in_hbm(refl_level.reshape(1, points)), in_hbm(refl_coef))
    diagonal_coef = lax.ppermute(first_coef, axes, across)
    swapped_coef = lax.ppermute(first_coef, axes, beside)

    band_shape = jax.ShapeDtypeStruct((block_rows, 2 * block_rows + 1, size, 2 * size), bf16)
    sums_shape = jax.ShapeDtypeStruct((block_rows, 2 * channels, 2 * size), f32)
    macs = 6 * channels * points * 2 * size

    def prepare(level, total):
        return pl.pallas_call(
            functools.partial(prepare_kernel, level),
            out_shape=[band_shape, band_shape, sums_shape],
            in_specs=[SMEM, SMEM, HBM, HBM, VMEM],
            out_specs=[VMEM] * 3,
            scratch_shapes=[
                pltpu.VMEM(blocks.shape[1:], f32),
                pltpu.VMEM((4 * channels, points), bf16),
                pltpu.SemaphoreType.DMA((block_rows,)),
            ],
            compiler_params=params(16),
            cost_estimate=cost(4 * macs, 8 * blocks.size),
            name="prepare",
        )(in_hbm(block_cols), other_cols, in_hbm(blocks), other_blocks, total)

    high, low, sums = prepare(0, total)
    total = pl.pallas_call(
        first_level_kernel,
        out_shape=field_shape,
        in_specs=[VMEM] * 8,
        out_specs=VMEM,
        compiler_params=params(12),
        cost_estimate=cost(2 * macs, blocks.size),
        name="first_level",
    )(swapped, diagonal, swapped_coef, diagonal_coef, high, low, sums, next_coef)
    diagonal = lax.ppermute(total, axes, across)
    swapped = lax.ppermute(total, axes, beside)
    high, low, sums = prepare(1, total)
    return pl.pallas_call(
        bottom_kernel,
        out_shape=jax.ShapeDtypeStruct(sources.shape, f32),
        in_specs=[VMEM] * 5,
        out_specs=HBM,
        scratch_shapes=[
            pltpu.VMEM((block_rows, panels, 2, part, size), f32),
            pltpu.SemaphoreType.DMA((block_rows,)),
        ],
        compiler_params=params(12),
        cost_estimate=cost(2 * macs, blocks.size),
        name="bottom",
    )(swapped, diagonal, high, low, sums)


def solution(mesh):
    placed = (
        P("shot", None, "depth", "lat"),
        P(("shot", "depth"), "lat", None, None, None, None),
        P("depth", "lat", None),
        P("lat"),
        P(None, "lat"),
    )
    return jax.shard_map(
        per_device,
        mesh=mesh,
        in_specs=placed,
        out_specs=P("shot", None, "depth", "lat"),
        check_vma=False,
    )
```

profile of v0, /device:TPU:0, one launch (start us, length us, event | category | flops | bytes accessed | tf_op | source)
XLA Modules:
  0.0 25.4 jit_solution(3516098191110448725)
XLA Ops:
  0.0 0.5 %collective-permute-start.5 = (f32[1,4,7,2,128,128]{5,4,3,2,1,0:T(8,128)}, f32[1,4,7,2,128,128]{5,4,3,2,1,0:T(8,128)S(1)}, u32[]{:S(2)}, u32[]{:S(2)}) collective-permute-start(f32[1,4,7,2,128,128]{5,4,3,2,1,0:T(8,128)} %own.3), channel_id=1, source_target_pairs={{0,8},{8,0},{1,9},{9,1},{2,10},{10,2},{3,11},{11,3},{4,12},{12,4},... | collective-permute-start | bytes 11010056 | tf_op jit(solution)/shard_map/ppermute | solution.py:260
  0.5 2.5 %collective-permute-start = (f32[3,2,16,512]{3,2,1,0:T(8,128)}, f32[3,2,16,512]{3,2,1,0:T(8,128)S(1)}, u32[]{:S(2)}, u32[]{:S(2)}) collective-permute-start(f32[3,2,16,512]{3,2,1,0:T(8,128)} %sources.1), channel_id=1, source_target_pairs={{0,1},{2,3},{4,5},{6,7},{8,9},{10,11},{12,13},{14,15},{1,0},{3,2},... | collective-permute-start | bytes 589832 | tf_op jit(solution)/shard_map/ppermute | solution.py:262
  3.0 0.2 collective-permute-start.1
  3.2 0.3 %collective-permute-start.4 = (s32[1,4,7]{2,1,0:T(4,128)}, s32[1,4,7]{2,1,0:T(4,128)S(1)}, u32[]{:S(2)}, u32[]{:S(2)}) collective-permute-start(s32[1,4,7]{2,1,0:T(4,128)} %own_cols.3), channel_id=1, source_target_pairs={{0,8},{8,0},{1,9},{9,1},{2,10},{10,2},{3,11},{11,3},{4,12},{12,4},... | collective-permute-start | bytes 344 | tf_op jit(solution)/shard_map/ppermute | solution.py:263
  3.5 1.0 %enter.1 = (f32[96,512]{1,0:T(8,128)S(1)}, f32[2,512]{1,0:T(2,128)S(1)}, f32[2,512]{1,0:T(2,128)S(1)}) custom-call(f32[3,2,16,512]{3,2,1,0:T(8,128)} %sources.1, s32[1,512]{1,0:T(1,128)} %bitcast.1, f32[2,512]{1,0:T(2,128)} %refl_coef.1), custom_call_target="tpu_custom_call" | custom-call | tf_op jit(solution)/shard_map/enter/pallas_call | solution.py:266
  4.5 2.6 %collective-permute-start.2 = (f32[2,512]{1,0:T(2,128)S(1)}, f32[2,512]{1,0:T(2,128)S(1)}, u32[]{:S(2)}, u32[]{:S(2)}) collective-permute-start(f32[2,512]{1,0:T(2,128)S(1)} %get-tuple-element.14), channel_id=1, source_target_pairs={{0,1},{2,3},{4,5},{6,7},{8,9},{10,11},{12,13},{14,15},{1,0},{3,2},... | collective-permute-start | bytes 12296 | tf_op jit(solution)/shard_map/ppermute | solution.py:281
  7.1 0.0 collective-permute-done.4.other_cols
  7.1 0.3 %collective-permute-start.3 = (f32[2,512]{1,0:T(2,128)S(1)}, f32[2,512]{1,0:T(2,128)S(1)}, u32[]{:S(2)}, u32[]{:S(2)}) collective-permute-start(f32[2,512]{1,0:T(2,128)S(1)} %get-tuple-element.14), channel_id=1, source_target_pairs={{1,2},{3,4},{5,6},{9,10},{11,12},{13,14},{0,8},{7,15},{2,1},{4,3},... | collective-permute-start | bytes 12296 | tf_op jit(solution)/shard_map/ppermute | solution.py:280
  7.4 0.0 collective-permute-done.5.received
  7.4 3.5 %prepare.2 = (bf16[4,9,128,256]{3,2,1,0:T(8,128)(2,1)S(1)}, bf16[4,9,128,256]{3,2,1,0:T(8,128)(2,1)S(1)}, f32[4,96,256]{2,1,0:T(8,128)S(1)}) custom-call(s32[1,4,7]{2,1,0:T(4,128)} %own_cols.3, s32[1,4,7]{2,1,0:T(4,128)S(1)} %collective-permute-done.4.other_cols, f32[1,4,7,2,128,128]{5,4,3,2,1,0:T(8,128)} %own.3, ...), custom_call_target="tpu_custom_call" | custom-call | flops 150994944 | bytes 7340032 | tf_op jit(solution)/shard_map/prepare/pallas_call | solution.py:288
  10.9 1.6 %collective-permute-done.2.swapped_coef = f32[2,512]{1,0:T(2,128)S(1)} collective-permute-done((f32[2,512]{1,0:T(2,128)S(1)}, f32[2,512]{1,0:T(2,128)S(1)}, u32[]{:S(2)}, u32[]{:S(2)}) %collective-permute-start.2) | collective-permute-done | bytes 4128 | tf_op jit(solution)/shard_map/ppermute | solution.py:281
  12.5 0.0 collective-permute-done.3.diagonal_coef
  12.5 0.0 collective-permute-done.swapped
  12.5 0.0 collective-permute-done.1.diagonal
  12.5 0.8 %first_level.1.field = f32[96,512]{1,0:T(8,128)S(1)} custom-call(f32[3,2,16,512]{3,2,1,0:T(8,128)S(1)} %collective-permute-done.swapped, f32[3,2,16,512]{3,2,1,0:T(8,128)S(1)} %collective-permute-done.1.diagonal, f32[2,512]{1,0:T(2,128)S(1)} %collective-permute-done.2.swapped_coef, f32[2,512]{1,0:T(2,128)S(1)} %collective-permute-done.3.diagonal_coef, ...), custom_call_target="tpu_custom_call" | custom-call | flops 75497472 | bytes 917504 | tf_op jit(solution)/shard_map/first_level/pallas_call | solution.py:304
  13.3 2.5 %collective-permute-start.6 = (f32[96,512]{1,0:T(8,128)S(1)}, f32[96,512]{1,0:T(8,128)S(1)}, u32[]{:S(2)}, u32[]{:S(2)}) collective-permute-start(f32[96,512]{1,0:T(8,128)S(1)} %first_level.1.field), channel_id=1, source_target_pairs={{0,1},{2,3},{4,5},{6,7},{8,9},{10,11},{12,13},{14,15},{1,0},{3,2},... | collective-permute-start | bytes 589832 | tf_op jit(solution)/shard_map/ppermute | solution.py:314
  15.8 0.0 collective-permute-start.7
  15.8 3.7 %prepare.3 = (bf16[4,9,128,256]{3,2,1,0:T(8,128)(2,1)S(1)}, bf16[4,9,128,256]{3,2,1,0:T(8,128)(2,1)S(1)}, f32[4,96,256]{2,1,0:T(8,128)S(1)}) custom-call(s32[1,4,7]{2,1,0:T(4,128)} %own_cols.3, s32[1,4,7]{2,1,0:T(4,128)S(1)} %collective-permute-done.4.other_cols, f32[1,4,7,2,128,128]{5,4,3,2,1,0:T(8,128)} %own.3, ...), custom_call_target="tpu_custom_call" | custom-call | flops 150994944 | bytes 7340032 | tf_op jit(solution)/shard_map/prepare/pallas_call | solution.py:288
  19.5 4.4 %collective-permute-done.6.swapped = f32[96,512]{1,0:T(8,128)S(1)} collective-permute-done((f32[96,512]{1,0:T(8,128)S(1)}, f32[96,512]{1,0:T(8,128)S(1)}, u32[]{:S(2)}, u32[]{:S(2)}) %collective-permute-start.6) | collective-permute-done | bytes 196640 | tf_op jit(solution)/shard_map/ppermute | solution.py:314
  23.9 0.0 collective-permute-done.7.diagonal
  23.9 1.4 %bottom.1 = f32[3,2,16,512]{3,2,1,0:T(8,128)} custom-call(f32[96,512]{1,0:T(8,128)S(1)} %collective-permute-done.6.swapped, f32[96,512]{1,0:T(8,128)S(1)} %collective-permute-done.7.diagonal, bf16[4,9,128,256]{3,2,1,0:T(8,128)(2,1)S(1)} %get-tuple-element.20.high, bf16[4,9,128,256]{3,2,1,0:T(8,128)(2,1)S(1)} %get-tuple-element.21.low, ...), custom_call_target="tpu_custom_call" | custom-call | flops 75497472 | bytes 917504 | tf_op jit(solution)/shard_map/bottom/pallas_call | solution.py:316
Async XLA Ops:
  0.0 7.4 %collective-permute-start.5 = (f32[1,4,7,2,128,128]{5,4,3,2,1,0:T(8,128)}, f32[1,4,7,2,128,128]{5,4,3,2,1,0:T(8,128)S(1)}, u32[]{:S(2)}, u32[]{:S(2)}) collective-permute-start(f32[1,4,7,2,128,128]{5,4,3,2,1,0:T(8,128)} %own.3), channel_id=1, source_target_pairs={{0,8},{8,0},{1,9},{9,1},{2,10},{10,2},{3,11},{11,3},{4,12},{12,4},... | collective-permute-start | bytes 11010056 | tf_op jit(solution)/shard_map/ppermute | solution.py:260
  0.5 12.0 %collective-permute-start = (f32[3,2,16,512]{3,2,1,0:T(8,128)}, f32[3,2,16,512]{3,2,1,0:T(8,128)S(1)}, u32[]{:S(2)}, u32[]{:S(2)}) collective-permute-start(f32[3,2,16,512]{3,2,1,0:T(8,128)} %sources.1), channel_id=1, source_target_pairs={{0,1},{2,3},{4,5},{6,7},{8,9},{10,11},{12,13},{14,15},{1,0},{3,2},... | collective-permute-start | bytes 589832 | tf_op jit(solution)/shard_map/ppermute | solution.py:262
  3.0 9.5 %collective-permute-start.1 = (f32[3,2,16,512]{3,2,1,0:T(8,128)}, f32[3,2,16,512]{3,2,1,0:T(8,128)S(1)}, u32[]{:S(2)}, u32[]{:S(2)}) collective-permute-start(f32[3,2,16,512]{3,2,1,0:T(8,128)} %sources.1), channel_id=1, source_target_pairs={{1,2},{3,4},{5,6},{9,10},{11,12},{13,14},{0,8},{7,15},{2,1},{4,3},... | collective-permute-start | bytes 589832 | tf_op jit(solution)/shard_map/ppermute | solution.py:261
  3.2 3.9 %collective-permute-start.4 = (s32[1,4,7]{2,1,0:T(4,128)}, s32[1,4,7]{2,1,0:T(4,128)S(1)}, u32[]{:S(2)}, u32[]{:S(2)}) collective-permute-start(s32[1,4,7]{2,1,0:T(4,128)} %own_cols.3), channel_id=1, source_target_pairs={{0,8},{8,0},{1,9},{9,1},{2,10},{10,2},{3,11},{11,3},{4,12},{12,4},... | collective-permute-start | bytes 344 | tf_op jit(solution)/shard_map/ppermute | solution.py:263
  4.5 8.0 %collective-permute-start.2 = (f32[2,512]{1,0:T(2,128)S(1)}, f32[2,512]{1,0:T(2,128)S(1)}, u32[]{:S(2)}, u32[]{:S(2)}) collective-permute-start(f32[2,512]{1,0:T(2,128)S(1)} %get-tuple-element.14), channel_id=1, source_target_pairs={{0,1},{2,3},{4,5},{6,7},{8,9},{10,11},{12,13},{14,15},{1,0},{3,2},... | collective-permute-start | bytes 12296 | tf_op jit(solution)/shard_map/ppermute | solution.py:281
  7.1 5.3 %collective-permute-start.3 = (f32[2,512]{1,0:T(2,128)S(1)}, f32[2,512]{1,0:T(2,128)S(1)}, u32[]{:S(2)}, u32[]{:S(2)}) collective-permute-start(f32[2,512]{1,0:T(2,128)S(1)} %get-tuple-element.14), channel_id=1, source_target_pairs={{1,2},{3,4},{5,6},{9,10},{11,12},{13,14},{0,8},{7,15},{2,1},{4,3},... | collective-permute-start | bytes 12296 | tf_op jit(solution)/shard_map/ppermute | solution.py:280
  13.3 10.7 %collective-permute-start.6 = (f32[96,512]{1,0:T(8,128)S(1)}, f32[96,512]{1,0:T(8,128)S(1)}, u32[]{:S(2)}, u32[]{:S(2)}) collective-permute-start(f32[96,512]{1,0:T(8,128)S(1)} %first_level.1.field), channel_id=1, source_target_pairs={{0,1},{2,3},{4,5},{6,7},{8,9},{10,11},{12,13},{14,15},{1,0},{3,2},... | collective-permute-start | bytes 589832 | tf_op jit(solution)/shard_map/ppermute | solution.py:314
  15.8 8.2 %collective-permute-start.7 = (f32[96,512]{1,0:T(8,128)S(1)}, f32[96,512]{1,0:T(8,128)S(1)}, u32[]{:S(2)}, u32[]{:S(2)}) collective-permute-start(f32[96,512]{1,0:T(8,128)S(1)} %first_level.1.field), channel_id=1, source_target_pairs={{1,2},{3,4},{5,6},{9,10},{11,12},{13,14},{0,8},{7,15},{2,1},{4,3},... | collective-permute-start | bytes 589832 | tf_op jit(solution)/shard_map/ppermute | solution.py:313
where the time goes:
time: 25.6 us; the launch traced here: 25.4 us
  Pallas kernels  10.4 us (41%)
  starting transfers between devices  8.87 us (35%)
  waiting for transfers between devices  6.01 us (23%)
    pallas_call x2, Pallas kernels, prepare(): pl.pallas_call(functools.partial(prepare_kernel, level), out_shape=[band_...  7.23 us
    ppermute x1, waiting for transfers between devices, per_device(): swapped = lax.ppermute(total, axes, beside)  4.44 us
    ppermute x1, starting transfers between devices, per_device(): swapped_coef = lax.ppermute(first_coef, axes, beside)  2.63 us
    ppermute x1, starting transfers between devices, per_device(): swapped = lax.ppermute(total, axes, beside)  2.48 us
    ppermute x1, starting transfers between devices, per_device(): swapped = lax.ppermute(sources, axes, beside)  2.48 us
    ppermute x1, waiting for transfers between devices, per_device(): swapped_coef = lax.ppermute(first_coef, axes, beside)  1.56 us
    pallas_call x1, Pallas kernels, per_device(): pl.pallas_call(bottom_kernel, out_shape=jax.ShapeDtypeStruct(sources.shap...  1.42 us
    pallas_call x1, Pallas kernels, per_device(): pl.pallas_call(enter_kernel, out_shape=[field_shape, coef_shape, coef_sha...  1 us
  transfers between devices with their start and end apart: 8, of which 2 were waited for; matrix products, arithmetic and copies ran while one was open for 0% of the time, Pallas kernels for 32%

commit v1 on v0

--- a/solution.py
+++ b/solution.py
@@ -149,30 +149,37 @@
         sums[b] = product(left[...], high[b, band], low[b, band])
 
 
-def add_halos(swapped, diagonal, high, low, sums, finish):
+def add_halo(value, is_left, left, high, low, sums, finish):
     block_rows, span, size, _ = high.shape
-
-    def both(before, after):
+    left[...] = pieces(value)
+
+    @pl.when(is_left)
+    def _():
         for b in range(block_rows):
-            ahead = slice(0, block_rows - b)
-            behind = slice(span - 1 - b, span)
-            finish(
-                b,
-                sums[b]
-                + product(before[:, b * size :], high[b, ahead], low[b, ahead])
-                + product(after[:, : (b + 1) * size], high[b, behind], low[b, behind]),
-            )
-
-    swapped, diagonal = pieces(swapped), pieces(diagonal)
-    even = lax.axis_index("lat") % 2 == 0
-
-    @pl.when(even)
+            band = slice(0, block_rows - b)
+            part = product(left[:, b * size :], high[b, band], low[b, band])
+            finish(b, sums[b] + part)
+
+    @pl.when(jnp.logical_not(is_left))
     def _():
-        both(diagonal, swapped)
-
-    @pl.when(jnp.logical_not(even))
-    def _():
-        both(swapped, diagonal)
+        for b in range(block_rows):
+            band = slice(span - 1 - b, span)
+            part = product(left[:, : (b + 1) * size], high[b, band], low[b, band])
+            finish(b, sums[b] + part)
+
+
+def odd_position():
+    return lax.axis_index("lat") % 2 == 1
+
+
+def swapped_kernel(reflects, halo, *refs):
+    coef, (high, low, sums, out, left) = refs[:reflects], refs[reflects:]
+
+    def finish(b, value):
+        out[b] = value
+
+    value = entered(halo, coef[0]) if reflects else halo[...]
+    add_halo(value, odd_position(), left, high, low, sums, finish)
 
 
 def leaving(value):
@@ -183,9 +190,7 @@
     )
 
 
-def first_level_kernel(
-    swapped, diagonal, swapped_coef, diagonal_coef, high, low, sums, next_coef, out
-):
+def first_level_kernel(halo, coef, high, low, sums, next_coef, out, left):
     def finish(b, value):
         re, im = leaving(value)
         channels, size = re.shape
@@ -194,17 +199,11 @@
         out[:channels, lanes] = re
         out[channels:, lanes] = im
 
-    add_halos(
-        entered(swapped, swapped_coef),
-        entered(diagonal, diagonal_coef),
-        high,
-        low,
-        sums,
-        finish,
-    )
-
-
-def bottom_kernel(swapped, diagonal, high, low, sums, out, held, sems):
+    is_left = jnp.logical_not(odd_position())
+    add_halo(entered(halo, coef), is_left, left, high, low, sums, finish)
+
+
+def bottom_kernel(halo, high, low, sums, out, held, left, sems):
     panels, _, part, _ = out.shape
     block_rows, _, size, _ = high.shape
 
@@ -220,7 +219,8 @@
         held[b, :, 1] = im.reshape(panels, part, size)
         copy_out(b).start()
 
-    add_halos(swapped[...], diagonal[...], high, low, sums, finish)
+    is_left = jnp.logical_not(odd_position())
+    add_halo(halo[...], is_left, left, high, low, sums, finish)
     for b in range(block_rows):
         copy_out(b).wait()
 
@@ -258,7 +258,6 @@
     across = over_lat(uneven, alone_uneven)
     beside = over_lat(even, alone_even)
     other_blocks = lax.ppermute(blocks, "depth", over_depth)
-    diagonal = lax.ppermute(sources, axes, across)
     swapped = lax.ppermute(sources, axes, beside)
     other_cols = lax.ppermute(block_cols, "depth", over_depth)
     field_shape = jax.ShapeDtypeStruct((2 * channels, points), f32)
@@ -277,6 +276,8 @@
         compiler_params=params(4),
         name="enter",
     )(in_hbm(sources), in_hbm(refl_level.reshape(1, points)), in_hbm(refl_coef))
+    late_sources, first_coef = lax.optimization_barrier((sources, first_coef))
+    diagonal = lax.ppermute(late_sources, axes, across)
     diagonal_coef = lax.ppermute(first_coef, axes, across)
     swapped_coef = lax.ppermute(first_coef, axes, beside)
 
@@ -300,32 +301,51 @@
             name="prepare",
         )(in_hbm(block_cols), other_cols, in_hbm(blocks), other_blocks, total)
 
+    left_scratch = pltpu.VMEM((4 * channels, points), bf16)
+
+    def add_swapped(*operands):
+        return pl.pallas_call(
+            functools.partial(swapped_kernel, len(operands) - 4),
+            out_shape=sums_shape,
+            in_specs=[VMEM] * len(operands),
+            out_specs=VMEM,
+            scratch_shapes=[left_scratch],
+            compiler_params=params(12),
+            cost_estimate=cost(macs, blocks.size),
+            name="swapped",
+        )(*operands)
+
     high, low, sums = prepare(0, total)
+    sums = add_swapped(swapped, swapped_coef, high, low, sums)
     total = pl.pallas_call(
         first_level_kernel,
         out_shape=field_shape,
-        in_specs=[VMEM] * 8,
+        in_specs=[VMEM] * 6,
         out_specs=VMEM,
+        scratch_shapes=[left_scratch],
         compiler_params=params(12),
-        cost_estimate=cost(2 * macs, blocks.size),
+        cost_estimate=cost(macs, blocks.size),
         name="first_level",
-    )(swapped, diagonal, swapped_coef, diagonal_coef, high, low, sums, next_coef)
-    diagonal = lax.ppermute(total, axes, across)
+    )(diagonal, diagonal_coef, high, low, sums, next_coef)
     swapped = lax.ppermute(total, axes, beside)
     high, low, sums = prepare(1, total)
+    late_total, sums = lax.optimization_barrier((total, sums))
+    diagonal = lax.ppermute(late_total, axes, across)
+    sums = add_swapped(swapped, high, low, sums)
     return pl.pallas_call(
         bottom_kernel,
         out_shape=jax.ShapeDtypeStruct(sources.shape, f32),
-        in_specs=[VMEM] * 5,
+        in_specs=[VMEM] * 4,
         out_specs=HBM,
         scratch_shapes=[
             pltpu.VMEM((block_rows, panels, 2, part, size), f32),
+            left_scratch,
             pltpu.SemaphoreType.DMA((block_rows,)),
         ],
         compiler_params=params(12),
-        cost_estimate=cost(2 * macs, blocks.size),
+        cost_estimate=cost(macs, blocks.size),
         name="bottom",
-    )(swapped, diagonal, high, low, sums)
+    )(diagonal, high, low, sums)
 
 
 def solution(mesh):

time: 25.6 us -> 26.3 us (1.027)
  the two profiles are of different devices: /device:TPU:0 before, /device:TPU:16 now
where the time goes in v1:
time: 26.3 us; the launch traced here: 26.2 us
  Pallas kernels  10 us (38%)
  waiting for transfers between devices  8.05 us (31%)
  starting transfers between devices  8.02 us (30%)
    pallas_call x2, Pallas kernels, prepare(): pl.pallas_call(functools.partial(prepare_kernel, level), out_shape=[band_...  6.49 us
    ppermute x1, waiting for transfers between devices, per_device(): diagonal = lax.ppermute(late_total, axes, across)  5.17 us
    ppermute x1, starting transfers between devices, per_device(): swapped_coef = lax.ppermute(first_coef, axes, beside)  2.62 us
    ppermute x1, starting transfers between devices, per_device(): swapped = lax.ppermute(total, axes, beside)  1.56 us
    ppermute x1, starting transfers between devices, per_device(): swapped = lax.ppermute(sources, axes, beside)  1.49 us
    ppermute x1, waiting for transfers between devices, per_device(): swapped = lax.ppermute(total, axes, beside)  1.41 us
    ppermute x1, starting transfers between devices, per_device(): diagonal_coef = lax.ppermute(first_coef, axes, across)  1.38 us
    pallas_call x1, Pallas kernels, per_device(): pl.pallas_call(bottom_kernel, out_shape=jax.ShapeDtypeStruct(sources.shap...  1.13 us
  transfers between devices with their start and end apart: 8, of which 4 were waited for; matrix products, arithmetic and copies ran while one was open for 0% of the time, Pallas kernels for 32%

profile of v1, /device:TPU:16, one launch (start us, length us, event | category | flops | bytes accessed | tf_op | source)
XLA Modules:
  0.0 26.2 jit_solution(52566491435043878)
XLA Ops:
  0.0 0.0 collective-permute-start.3
  0.0 1.5 %collective-permute-start.4 = (f32[3,2,16,512]{3,2,1,0:T(8,128)}, f32[3,2,16,512]{3,2,1,0:T(8,128)S(1)}, u32[]{:S(2)}, u32[]{:S(2)}) collective-permute-start(f32[3,2,16,512]{3,2,1,0:T(8,128)} %sources.1), channel_id=1, source_target_pairs={{0,1},{2,3},{4,5},{6,7},{8,9},{10,11},{12,13},{14,15},{1,0},{3,2},... | collective-permute-start | bytes 589832 | tf_op jit(solution)/shard_map/ppermute | solution.py:261
  1.5 1.0 %enter.1 = (f32[96,512]{1,0:T(8,128)S(1)}, f32[2,512]{1,0:T(2,128)S(1)}, f32[2,512]{1,0:T(2,128)S(1)}) custom-call(f32[3,2,16,512]{3,2,1,0:T(8,128)} %sources.1, s32[1,512]{1,0:T(1,128)} %bitcast.1, f32[2,512]{1,0:T(2,128)} %refl_coef.1), custom_call_target="tpu_custom_call" | custom-call | tf_op jit(solution)/shard_map/enter/pallas_call | solution.py:265
  2.5 0.5 %collective-permute-start = (f32[3,2,16,512]{3,2,1,0:T(8,128)}, f32[3,2,16,512]{3,2,1,0:T(8,128)S(1)}, u32[]{:S(2)}, u32[]{:S(2)}) collective-permute-start(f32[3,2,16,512]{3,2,1,0:T(8,128)} %sources.1), channel_id=1, source_target_pairs={{1,2},{3,4},{5,6},{9,10},{11,12},{13,14},{0,8},{7,15},{2,1},{4,3},... | collective-permute-start | bytes 589832 | tf_op jit(solution)/shard_map/ppermute | solution.py:280
  3.0 0.0 collective-permute-start.2
  3.0 2.6 %collective-permute-start.5 = (f32[2,512]{1,0:T(2,128)S(1)}, f32[2,512]{1,0:T(2,128)S(1)}, u32[]{:S(2)}, u32[]{:S(2)}) collective-permute-start(f32[2,512]{1,0:T(2,128)S(1)} %get-tuple-element.20), channel_id=1, source_target_pairs={{0,1},{2,3},{4,5},{6,7},{8,9},{10,11},{12,13},{14,15},{1,0},{3,2},... | collective-permute-start | bytes 12296 | tf_op jit(solution)/shard_map/ppermute | solution.py:282
  5.6 1.0 %collective-permute-done.2.other_cols = s32[1,4,7]{2,1,0:T(4,128)S(1)} collective-permute-done((s32[1,4,7]{2,1,0:T(4,128)}, s32[1,4,7]{2,1,0:T(4,128)S(1)}, u32[]{:S(2)}, u32[]{:S(2)}) %collective-permute-start.2) | collective-permute-done | bytes 144 | tf_op jit(solution)/shard_map/ppermute | solution.py:262
  6.6 1.4 %collective-permute-start.1 = (f32[2,512]{1,0:T(2,128)S(1)}, f32[2,512]{1,0:T(2,128)S(1)}, u32[]{:S(2)}, u32[]{:S(2)}) collective-permute-start(f32[2,512]{1,0:T(2,128)S(1)} %get-tuple-element.20), channel_id=1, source_target_pairs={{1,2},{3,4},{5,6},{9,10},{11,12},{13,14},{0,8},{7,15},{2,1},{4,3},... | collective-permute-start | bytes 12296 | tf_op jit(solution)/shard_map/ppermute | solution.py:281
  8.0 0.0 collective-permute-done.3.received
  8.0 3.4 %prepare.2 = (bf16[4,9,128,256]{3,2,1,0:T(8,128)(2,1)S(1)}, bf16[4,9,128,256]{3,2,1,0:T(8,128)(2,1)S(1)}, f32[4,96,256]{2,1,0:T(8,128)S(1)}) custom-call(s32[1,4,7]{2,1,0:T(4,128)} %own_cols.3, s32[1,4,7]{2,1,0:T(4,128)S(1)} %collective-permute-done.2.other_cols, f32[1,4,7,2,128,128]{5,4,3,2,1,0:T(8,128)} %own.3, ...), custom_call_target="tpu_custom_call" | custom-call | flops 150994944 | bytes 7340032 | tf_op jit(solution)/shard_map/prepare/pallas_call | solution.py:289
  11.4 0.5 %collective-permute-done.5.refs_0_ = f32[2,512]{1,0:T(2,128)S(1)} collective-permute-done((f32[2,512]{1,0:T(2,128)S(1)}, f32[2,512]{1,0:T(2,128)S(1)}, u32[]{:S(2)}, u32[]{:S(2)}) %collective-permute-start.5) | collective-permute-done | bytes 4128 | tf_op jit(solution)/shard_map/ppermute | solution.py:282
  11.9 0.0 collective-permute-done.4.halo
  11.9 0.5 %swapped.2.sums = f32[4,96,256]{2,1,0:T(8,128)S(1)} custom-call(f32[3,2,16,512]{3,2,1,0:T(8,128)S(1)} %collective-permute-done.4.halo, f32[2,512]{1,0:T(2,128)S(1)} %collective-permute-done.5.refs_0_, bf16[4,9,128,256]{3,2,1,0:T(8,128)(2,1)S(1)} %get-tuple-element.22.refs_1_.high, bf16[4,9,128,256]{3,2,1,0:T(8,128)(2,1)S(1)} %get-tuple-element.23.refs_2_.low, ...), custom_call_target="tpu_custom_call" | custom-call | flops 37748736 | bytes 917504 | tf_op jit(solution)/shard_map/swapped/pallas_call | solution.py:307
  12.4 0.0 collective-permute-done.1.coef
  12.4 0.0 collective-permute-done.halo
  12.4 0.5 %first_level.1.field = f32[96,512]{1,0:T(8,128)S(1)} custom-call(f32[3,2,16,512]{3,2,1,0:T(8,128)S(1)} %collective-permute-done.halo, f32[2,512]{1,0:T(2,128)S(1)} %collective-permute-done.1.coef, bf16[4,9,128,256]{3,2,1,0:T(8,128)(2,1)S(1)} %get-tuple-element.22.refs_1_.high, bf16[4,9,128,256]{3,2,1,0:T(8,128)(2,1)S(1)} %get-tuple-element.23.refs_2_.low, ...), custom_call_target="tpu_custom_call" | custom-call | flops 37748736 | bytes 917504 | tf_op jit(solution)/shard_map/first_level/pallas_call | solution.py:320
  12.9 1.6 %collective-permute-start.7 = (f32[96,512]{1,0:T(8,128)S(1)}, f32[96,512]{1,0:T(8,128)S(1)}, u32[]{:S(2)}, u32[]{:S(2)}) collective-permute-start(f32[96,512]{1,0:T(8,128)S(1)} %first_level.1.field), channel_id=1, source_target_pairs={{0,1},{2,3},{4,5},{6,7},{8,9},{10,11},{12,13},{14,15},{1,0},{3,2},... | collective-permute-start | bytes 589832 | tf_op jit(solution)/shard_map/ppermute | solution.py:330
  14.4 3.1 %prepare.3 = (bf16[4,9,128,256]{3,2,1,0:T(8,128)(2,1)S(1)}, bf16[4,9,128,256]{3,2,1,0:T(8,128)(2,1)S(1)}, f32[4,96,256]{2,1,0:T(8,128)S(1)}) custom-call(s32[1,4,7]{2,1,0:T(4,128)} %own_cols.3, s32[1,4,7]{2,1,0:T(4,128)S(1)} %collective-permute-done.2.other_cols, f32[1,4,7,2,128,128]{5,4,3,2,1,0:T(8,128)} %own.3, ...), custom_call_target="tpu_custom_call" | custom-call | flops 150994944 | bytes 7340032 | tf_op jit(solution)/shard_map/prepare/pallas_call | solution.py:289
  17.5 0.5 %collective-permute-start.6 = (f32[96,512]{1,0:T(8,128)S(1)}, f32[96,512]{1,0:T(8,128)S(1)}, u32[]{:S(2)}, u32[]{:S(2)}) collective-permute-start(f32[96,512]{1,0:T(8,128)S(1)} %first_level.1.field), channel_id=1, source_target_pairs={{1,2},{3,4},{5,6},{9,10},{11,12},{13,14},{0,8},{7,15},{2,1},{4,3},... | collective-permute-start | bytes 589832 | tf_op jit(solution)/shard_map/ppermute | solution.py:333
  18.0 1.4 %collective-permute-done.7.halo = f32[96,512]{1,0:T(8,128)S(1)} collective-permute-done((f32[96,512]{1,0:T(8,128)S(1)}, f32[96,512]{1,0:T(8,128)S(1)}, u32[]{:S(2)}, u32[]{:S(2)}) %collective-permute-start.7) | collective-permute-done | bytes 196640 | tf_op jit(solution)/shard_map/ppermute | solution.py:330
  19.4 0.4 %swapped.3.sums = f32[4,96,256]{2,1,0:T(8,128)S(1)} custom-call(f32[96,512]{1,0:T(8,128)S(1)} %collective-permute-done.7.halo, bf16[4,9,128,256]{3,2,1,0:T(8,128)(2,1)S(1)} %get-tuple-element.28.refs_0_.high, bf16[4,9,128,256]{3,2,1,0:T(8,128)(2,1)S(1)} %get-tuple-element.29.refs_1_.low, f32[4,96,256]{2,1,0:T(8,128)S(1)} %get-tuple-element.30.refs_2_), custom_call_target="tpu_custom_call" | custom-call | flops 37748736 | bytes 917504 | tf_op jit(solution)/shard_map/swapped/pallas_call | solution.py:307
  19.8 5.2 %collective-permute-done.6.halo = f32[96,512]{1,0:T(8,128)S(1)} collective-permute-done((f32[96,512]{1,0:T(8,128)S(1)}, f32[96,512]{1,0:T(8,128)S(1)}, u32[]{:S(2)}, u32[]{:S(2)}) %collective-permute-start.6) | collective-permute-done | bytes 196640 | tf_op jit(solution)/shard_map/ppermute | solution.py:333
  25.0 1.1 %bottom.1 = f32[3,2,16,512]{3,2,1,0:T(8,128)} custom-call(f32[96,512]{1,0:T(8,128)S(1)} %collective-permute-done.6.halo, bf16[4,9,128,256]{3,2,1,0:T(8,128)(2,1)S(1)} %get-tuple-element.28.refs_0_.high, bf16[4,9,128,256]{3,2,1,0:T(8,128)(2,1)S(1)} %get-tuple-element.29.refs_1_.low, f32[4,96,256]{2,1,0:T(8,128)S(1)} %swapped.3.sums), custom_call_target="tpu_custom_call" | custom-call | flops 37748736 | bytes 917504 | tf_op jit(solution)/shard_map/bottom/pallas_call | solution.py:335
Async XLA Ops:
  0.0 8.0 %collective-permute-start.3 = (f32[1,4,7,2,128,128]{5,4,3,2,1,0:T(8,128)}, f32[1,4,7,2,128,128]{5,4,3,2,1,0:T(8,128)S(1)}, u32[]{:S(2)}, u32[]{:S(2)}) collective-permute-start(f32[1,4,7,2,128,128]{5,4,3,2,1,0:T(8,128)} %own.3), channel_id=1, source_target_pairs={{0,8},{8,0},{1,9},{9,1},{2,10},{10,2},{3,11},{11,3},{4,12},{12,4},... | collective-permute-start | bytes 11010056 | tf_op jit(solution)/shard_map/ppermute | solution.py:260
  0.0 11.9 %collective-permute-start.4 = (f32[3,2,16,512]{3,2,1,0:T(8,128)}, f32[3,2,16,512]{3,2,1,0:T(8,128)S(1)}, u32[]{:S(2)}, u32[]{:S(2)}) collective-permute-start(f32[3,2,16,512]{3,2,1,0:T(8,128)} %sources.1), channel_id=1, source_target_pairs={{0,1},{2,3},{4,5},{6,7},{8,9},{10,11},{12,13},{14,15},{1,0},{3,2},... | collective-permute-start | bytes 589832 | tf_op jit(solution)/shard_map/ppermute | solution.py:261
  2.5 9.9 %collective-permute-start = (f32[3,2,16,512]{3,2,1,0:T(8,128)}, f32[3,2,16,512]{3,2,1,0:T(8,128)S(1)}, u32[]{:S(2)}, u32[]{:S(2)}) collective-permute-start(f32[3,2,16,512]{3,2,1,0:T(8,128)} %sources.1), channel_id=1, source_target_pairs={{1,2},{3,4},{5,6},{9,10},{11,12},{13,14},{0,8},{7,15},{2,1},{4,3},... | collective-permute-start | bytes 589832 | tf_op jit(solution)/shard_map/ppermute | solution.py:280
  3.0 3.6 %collective-permute-start.2 = (s32[1,4,7]{2,1,0:T(4,128)}, s32[1,4,7]{2,1,0:T(4,128)S(1)}, u32[]{:S(2)}, u32[]{:S(2)}) collective-permute-start(s32[1,4,7]{2,1,0:T(4,128)} %own_cols.3), channel_id=1, source_target_pairs={{0,8},{8,0},{1,9},{9,1},{2,10},{10,2},{3,11},{11,3},{4,12},{12,4},... | collective-permute-start | bytes 344 | tf_op jit(solution)/shard_map/ppermute | solution.py:262
  3.0 8.9 %collective-permute-start.5 = (f32[2,512]{1,0:T(2,128)S(1)}, f32[2,512]{1,0:T(2,128)S(1)}, u32[]{:S(2)}, u32[]{:S(2)}) collective-permute-start(f32[2,512]{1,0:T(2,128)S(1)} %get-tuple-element.20), channel_id=1, source_target_pairs={{0,1},{2,3},{4,5},{6,7},{8,9},{10,11},{12,13},{14,15},{1,0},{3,2},... | collective-permute-start | bytes 12296 | tf_op jit(solution)/shard_map/ppermute | solution.py:282
  6.6 5.8 %collective-permute-start.1 = (f32[2,512]{1,0:T(2,128)S(1)}, f32[2,512]{1,0:T(2,128)S(1)}, u32[]{:S(2)}, u32[]{:S(2)}) collective-permute-start(f32[2,512]{1,0:T(2,128)S(1)} %get-tuple-element.20), channel_id=1, source_target_pairs={{1,2},{3,4},{5,6},{9,10},{11,12},{13,14},{0,8},{7,15},{2,1},{4,3},... | collective-permute-start | bytes 12296 | tf_op jit(solution)/shard_map/ppermute | solution.py:281
  12.9 6.5 %collective-permute-start.7 = (f32[96,512]{1,0:T(8,128)S(1)}, f32[96,512]{1,0:T(8,128)S(1)}, u32[]{:S(2)}, u32[]{:S(2)}) collective-permute-start(f32[96,512]{1,0:T(8,128)S(1)} %first_level.1.field), channel_id=1, source_target_pairs={{0,1},{2,3},{4,5},{6,7},{8,9},{10,11},{12,13},{14,15},{1,0},{3,2},... | collective-permute-start | bytes 589832 | tf_op jit(solution)/shard_map/ppermute | solution.py:330
  17.5 7.5 %collective-permute-start.6 = (f32[96,512]{1,0:T(8,128)S(1)}, f32[96,512]{1,0:T(8,128)S(1)}, u32[]{:S(2)}, u32[]{:S(2)}) collective-permute-start(f32[96,512]{1,0:T(8,128)S(1)} %first_level.1.field), channel_id=1, source_target_pairs={{1,2},{3,4},{5,6},{9,10},{11,12},{13,14},{0,8},{7,15},{2,1},{4,3},... | collective-permute-start | bytes 589832 | tf_op jit(solution)/shard_map/ppermute | solution.py:333

commit v2 on v0

--- a/solution.py
+++ b/solution.py
@@ -7,6 +7,7 @@
 from jax.experimental.pallas import tpu as pltpu
 from jax.sharding import PartitionSpec as P
 
+
 VMEM = pl.BlockSpec(memory_space=pltpu.VMEM)
 SMEM = pl.BlockSpec(memory_space=pltpu.SMEM)
 HBM = pl.BlockSpec(memory_space=pltpu.HBM)
@@ -29,21 +30,26 @@
 
 
 def enter_kernel(
-    sources, refl_level, refl_coef, total, first_coef, next_coef, held, level_held, coef_held, sems
+    first, sources, refl_level, refl_coef, total, next_coef, held, level_held, coef_held, coef, sems
 ):
+    lanes = pl.ds(first, total.shape[1])
     copies = [
         pltpu.make_async_copy(a, b, sems.at[i])
         for i, (a, b) in enumerate(
-            ((sources, held), (refl_level, level_held), (refl_coef, coef_held))
+            (
+                (sources.at[:, :, :, lanes], held),
+                (refl_level.at[:, lanes], level_held),
+                (refl_coef.at[:, lanes], coef_held),
+            )
         )
     ]
     for copy in copies:
         copy.start()
     for copy in copies:
         copy.wait()
-    first_coef[...] = jnp.where(level_held[...] == 0, coef_held[...], 0.0)
+    coef[...] = jnp.where(level_held[...] == 0, coef_held[...], 0.0)
     next_coef[...] = jnp.where(level_held[...] == 1, coef_held[...], 0.0)
-    total[...] = entered(held, first_coef)
+    total[...] = entered(held, coef)
 
 
 def head_and_tail(value):
@@ -64,9 +70,8 @@
     return both[:rows] + both[rows:] + cross
 
 
-def prepare_kernel(
-    level, own_cols, other_cols, own, received, field, high, low, sums, held, left, sems
-):
+def prepare_kernel(level, own_cols, other_cols, own, received, *refs):
+    fields, (high, low, sums, held, left, sems) = refs[:-6], refs[-6:]
     block_rows, per_row, _, size, _ = held.shape
     here = lax.axis_index("depth") == level
     first_row = lax.axis_index("lat") * block_rows
@@ -117,7 +122,10 @@
 
             lax.fori_loop(0, span, clear_one, 0)
 
-    left[...] = pieces(field[...])
+    at_lane = 0
+    for field in fields:
+        left[:, at_lane : at_lane + field.shape[1]] = pieces(field[...])
+        at_lane += field.shape[1]
     for b in range(block_rows):
         at = rows_at[b]
         pltpu.make_async_copy(own.at[0, b], held.at[b], sems.at[b]).wait()
@@ -149,30 +157,57 @@
         sums[b] = product(left[...], high[b, band], low[b, band])
 
 
-def add_halos(swapped, diagonal, high, low, sums, finish):
-    block_rows, span, size, _ = high.shape
-
-    def both(before, after):
-        for b in range(block_rows):
-            ahead = slice(0, block_rows - b)
-            behind = slice(span - 1 - b, span)
+def side_product(b, first, piece, is_before, high, low):
+    block_rows, _, size, _ = high.shape
+    last = first + piece.shape[1] // size
+    if is_before:
+        low_col, high_col, shift = max(b, first), last, -b
+    else:
+        low_col, high_col, shift = first, min(b + 1, last), 2 * block_rows - b
+    if low_col >= high_col:
+        return 0.0
+    lanes = slice((low_col - first) * size, (high_col - first) * size)
+    band = slice(low_col + shift, high_col + shift)
+    return product(piece[:, lanes], high[b, band], low[b, band])
+
+
+def by_side(run):
+    even = lax.axis_index("lat") % 2 == 0
+    pl.when(even)(functools.partial(run, False))
+    pl.when(jnp.logical_not(even))(functools.partial(run, True))
+
+
+def early_kernel(halo, high, low, sums, out, left):
+    left[...] = pieces(halo[...])
+
+    def run(swapped_before):
+        for b in range(high.shape[0]):
+            out[b] = sums[b] + side_product(b, 0, left, swapped_before, high, low)
+
+    by_side(run)
+
+
+def late_products(rows, swapped, diagonal, high, low, sums, finish):
+    first = (diagonal.shape[1] - swapped.shape[1]) // high.shape[2]
+
+    def run(swapped_before):
+        for i, b in enumerate(rows):
             finish(
+                i,
                 b,
                 sums[b]
-                + product(before[:, b * size :], high[b, ahead], low[b, ahead])
-                + product(after[:, : (b + 1) * size], high[b, behind], low[b, behind]),
+                + side_product(b, 0, diagonal, not swapped_before, high, low)
+                + side_product(b, first, swapped, swapped_before, high, low),
             )
 
-    swapped, diagonal = pieces(swapped), pieces(diagonal)
-    even = lax.axis_index("lat") % 2 == 0
-
-    @pl.when(even)
-    def _():
-        both(diagonal, swapped)
-
-    @pl.when(jnp.logical_not(even))
-    def _():
-        both(swapped, diagonal)
+    by_side(run)
+
+
+def take_late(swapped, relayed, diagonal, swapped_left, diagonal_left):
+    points = relayed.shape[1]
+    swapped_left[...] = pieces(swapped[...])
+    diagonal_left[:, :points] = pieces(relayed[...])
+    diagonal_left[:, points:] = pieces(diagonal[...])
 
 
 def leaving(value):
@@ -183,30 +218,41 @@
     )
 
 
-def first_level_kernel(
-    swapped, diagonal, swapped_coef, diagonal_coef, high, low, sums, next_coef, out
-):
-    def finish(b, value):
+def level_rows(rows, swapped, diagonal, high, low, sums, next_coef, out):
+    def finish(i, b, value):
         re, im = leaving(value)
         channels, size = re.shape
-        lanes = slice(b * size, (b + 1) * size)
+        lanes = slice(i * size, (i + 1) * size)
         re, im = reflected(re, im, next_coef[0:1, lanes], next_coef[1:2, lanes])
         out[:channels, lanes] = re
         out[channels:, lanes] = im
 
-    add_halos(
-        entered(swapped, swapped_coef),
-        entered(diagonal, diagonal_coef),
-        high,
-        low,
-        sums,
-        finish,
-    )
-
-
-def bottom_kernel(swapped, diagonal, high, low, sums, out, held, sems):
+    late_products(rows, swapped, diagonal, high, low, sums, finish)
+
+
+def first_rows_kernel(
+    rows, swapped, relayed, diagonal, high, low, sums, next_coef, out, swapped_left, diagonal_left
+):
+    take_late(swapped, relayed, diagonal, swapped_left, diagonal_left)
+    level_rows(rows, swapped_left, diagonal_left, high, low, sums, next_coef, out)
+
+
+def bottom_kernel(
+    swapped,
+    relayed,
+    diagonal,
+    high,
+    low,
+    sums,
+    out,
+    held,
+    swapped_left,
+    diagonal_left,
+    sems,
+):
     panels, _, part, _ = out.shape
     block_rows, _, size, _ = high.shape
+    take_late(swapped, relayed, diagonal, swapped_left, diagonal_left)
 
     def copy_out(b):
         lanes = pl.ds(b * size, size)
@@ -214,13 +260,13 @@
             held.at[b], out.at[:, :, :, lanes], sems.at[b]
         )
 
-    def finish(b, value):
+    def finish(i, b, value):
         re, im = leaving(value)
         held[b, :, 0] = re.reshape(panels, part, size)
         held[b, :, 1] = im.reshape(panels, part, size)
         copy_out(b).start()
 
-    add_halos(swapped[...], diagonal[...], high, low, sums, finish)
+    late_products(range(block_rows), swapped_left, diagonal_left, high, low, sums, finish)
     for b in range(block_rows):
         copy_out(b).wait()
 
@@ -240,7 +286,7 @@
 def per_device(sources, blocks, block_cols, refl_level, refl_coef):
     lat_count = lax.axis_size("lat")
     panels, _, part, points = sources.shape
-    _, block_rows, per_row, _, size, _ = blocks.shape
+    _, block_rows, _, _, size, _ = blocks.shape
     channels = panels * part
     f32, bf16 = jnp.float32, jnp.bfloat16
     axes = ("depth", "lat")
@@ -257,38 +303,70 @@
 
     across = over_lat(uneven, alone_uneven)
     beside = over_lat(even, alone_even)
+    onward = [(i, i + 2) for i in range(0, lat_count - 2, 2)]
+    onward += [(i + 2, i) for i in range(1, lat_count - 2, 2)]
+    top = lat_count - 1
+    onward += [(top, top - 1) if top % 2 == 0 else (top - 1, top), (1, 0)]
+    onward = [(d * lat_count + i, d * lat_count + j) for d in range(2) for i, j in onward]
+    half = block_rows // 2
+    first_rows, second_rows = range(half), range(half, block_rows)
+
+    def part_shape(rows):
+        return jax.ShapeDtypeStruct((2 * channels, len(rows) * size), f32)
+
+    def piece_shape(rows):
+        return (4 * channels, len(rows) * size), bf16
+
+    def exchange(first, second):
+        first_swapped = lax.ppermute(first, axes, beside)
+        second = second()
+        second_swapped = lax.ppermute(second, axes, beside)
+        second_diagonal = lax.ppermute(second, axes, across)
+        relayed = lax.ppermute(first_swapped, axes, onward)
+        return second, first_swapped, (second_swapped, relayed, second_diagonal)
+
     other_blocks = lax.ppermute(blocks, "depth", over_depth)
-    diagonal = lax.ppermute(sources, axes, across)
-    swapped = lax.ppermute(sources, axes, beside)
     other_cols = lax.ppermute(block_cols, "depth", over_depth)
-    field_shape = jax.ShapeDtypeStruct((2 * channels, points), f32)
-    coef_shape = jax.ShapeDtypeStruct((2, points), f32)
-    total, first_coef, next_coef = pl.pallas_call(
-        enter_kernel,
-        out_shape=[field_shape, coef_shape, coef_shape],
-        in_specs=[HBM] * 3,
-        out_specs=[VMEM] * 3,
-        scratch_shapes=[
-            pltpu.VMEM(sources.shape, f32),
-            pltpu.VMEM((1, points), jnp.int32),
-            pltpu.VMEM((2, points), f32),
-            pltpu.SemaphoreType.DMA((3,)),
-        ],
-        compiler_params=params(4),
-        name="enter",
-    )(in_hbm(sources), in_hbm(refl_level.reshape(1, points)), in_hbm(refl_coef))
-    diagonal_coef = lax.ppermute(first_coef, axes, across)
-    swapped_coef = lax.ppermute(first_coef, axes, beside)
+    refl_level = refl_level.reshape(1, points)
+
+    def enter(rows):
+        width = len(rows) * size
+        return pl.pallas_call(
+            functools.partial(enter_kernel, rows[0] * size),
+            out_shape=[part_shape(rows), jax.ShapeDtypeStruct((2, width), f32)],
+            in_specs=[HBM] * 3,
+            out_specs=[VMEM] * 2,
+            scratch_shapes=[
+                pltpu.VMEM((panels, 2, part, width), f32),
+                pltpu.VMEM((1, width), jnp.int32),
+                pltpu.VMEM((2, width), f32),
+                pltpu.VMEM((2, width), f32),
+                pltpu.SemaphoreType.DMA((3,)),
+            ],
+            compiler_params=params(4),
+            name="enter",
+        )(in_hbm(sources), in_hbm(refl_level), in_hbm(refl_coef))
+
+    coefs = []
+
+    def enter_second():
+        part_total, coef = enter(second_rows)
+        coefs.append(coef)
+        return part_total
+
+    first_total, coef = enter(first_rows)
+    coefs.append(coef)
+    second_total, early, late = exchange(first_total, enter_second)
 
     band_shape = jax.ShapeDtypeStruct((block_rows, 2 * block_rows + 1, size, 2 * size), bf16)
     sums_shape = jax.ShapeDtypeStruct((block_rows, 2 * channels, 2 * size), f32)
     macs = 6 * channels * points * 2 * size
 
-    def prepare(level, total):
+    def prepare(level, *fields):
         return pl.pallas_call(
             functools.partial(prepare_kernel, level),
             out_shape=[band_shape, band_shape, sums_shape],
-            in_specs=[SMEM, SMEM, HBM, HBM, VMEM],
+            in_specs=[SMEM, SMEM, HBM, HBM] + [VMEM] * len(fields),
             out_specs=[VMEM] * 3,
             scratch_shapes=[
                 pltpu.VMEM(blocks.shape[1:], f32),
@@ -298,34 +376,66 @@
             compiler_params=params(16),
             cost_estimate=cost(4 * macs, 8 * blocks.size),
             name="prepare",
-        )(in_hbm(block_cols), other_cols, in_hbm(blocks), other_blocks, total)
-
-    high, low, sums = prepare(0, total)
-    total = pl.pallas_call(
-        first_level_kernel,
-        out_shape=field_shape,
-        in_specs=[VMEM] * 8,
-        out_specs=VMEM,
+        )(in_hbm(block_cols), other_cols, in_hbm(blocks), other_blocks, *fields)
+
+    def early_products(level, halo, *fields):
+        high, low, sums = prepare(level, *fields)
+        sums = pl.pallas_call(
+            early_kernel,
+            out_shape=sums_shape,
+            in_specs=[VMEM] * 4,
+            out_specs=VMEM,
+            scratch_shapes=[pltpu.VMEM(*piece_shape(first_rows))],
+            compiler_params=params(12),
+            cost_estimate=cost(macs, blocks.size),
+            name="early",
+        )(halo, high, low, sums)
+        return high, low, sums
+
+    every_row = range(block_rows)
+    high, low, sums = early_products(0, early, first_total, second_total)
+    first_part, swapped_left, diagonal_left = pl.pallas_call(
+        functools.partial(first_rows_kernel, first_rows),
+        out_shape=[
+            part_shape(first_rows),
+            jax.ShapeDtypeStruct(*piece_shape(second_rows)),
+            jax.ShapeDtypeStruct(*piece_shape(every_row)),
+        ],
+        in_specs=[VMEM] * 7,
+        out_specs=[VMEM] * 3,
         compiler_params=params(12),
-        cost_estimate=cost(2 * macs, blocks.size),
-        name="first_level",
-    )(swapped, diagonal, swapped_coef, diagonal_coef, high, low, sums, next_coef)
-    diagonal = lax.ppermute(total, axes, across)
-    swapped = lax.ppermute(total, axes, beside)
-    high, low, sums = prepare(1, total)
+        cost_estimate=cost(macs, blocks.size),
+        name="first_rows",
+    )(*late, high, low, sums, coefs[0])
+
+    def level_second():
+        return pl.pallas_call(
+            functools.partial(level_rows, second_rows),
+            out_shape=part_shape(second_rows),
+            in_specs=[VMEM] * 6,
+            out_specs=VMEM,
+            compiler_params=params(12),
+            cost_estimate=cost(macs, blocks.size),
+            name="second_rows",
+        )(swapped_left, diagonal_left, high, low, sums, coefs[1])
+
+    second_part, early, late = exchange(first_part, level_second)
+    last_high, last_low, last_sums = early_products(1, early, first_part, second_part)
     return pl.pallas_call(
         bottom_kernel,
         out_shape=jax.ShapeDtypeStruct(sources.shape, f32),
-        in_specs=[VMEM] * 5,
+        in_specs=[VMEM] * 6,
         out_specs=HBM,
         scratch_shapes=[
             pltpu.VMEM((block_rows, panels, 2, part, size), f32),
+            pltpu.VMEM(*piece_shape(second_rows)),
+            pltpu.VMEM(*piece_shape(every_row)),
             pltpu.SemaphoreType.DMA((block_rows,)),
         ],
         compiler_params=params(12),
-        cost_estimate=cost(2 * macs, blocks.size),
+        cost_estimate=cost(macs, blocks.size),
         name="bottom",
-    )(swapped, diagonal, high, low, sums)
+    )(*late, last_high, last_low, last_sums)
 
 
 def solution(mesh):

time: 25.6 us -> 28.4 us (1.11)
  starting transfers between devices: 8.87 us -> 10 us
  Pallas kernels: 10.4 us -> 11.4 us
  waiting for transfers between devices: 6.01 us -> 6.68 us
    pallas_call x2 -> x6, Pallas kernels: 1.79 us -> 3.26 us  [the longest x2 1.89 us: enter(): pl.pallas_call(functools.partial(enter_kernel, rows[0] * size), out_shape...]
    ppermute x6 -> x8, starting transfers between devices: 8.1 us -> 9.52 us  [the longest x2 4.35 us: exchange(): relayed = lax.ppermute(first_swapped, axes, onward)]
    ppermute x1, waiting for transfers between devices: 0.01 us -> 1.37 us  [per_device(): other_cols = lax.ppermute(block_cols, 'depth', over_depth)]
    ppermute x6 -> x8, waiting for transfers between devices: 6.01 us -> 5.3 us  [the longest x2 5.29 us: exchange(): first_swapped = lax.ppermute(first, axes, beside)]
    pallas_call x2, Pallas kernels: 7.23 us -> 6.92 us  [prepare(): pl.pallas_call(functools.partial(prepare_kernel, level), out_shape=[band_...]
  transfers between devices with their start and end apart: 8 -> 10, of which waited for: 2 -> 3; matrix products, arithmetic and copies ran while one was open for 0% -> 0% of each run, Pallas kernels for 32% -> 35%
where the time goes in v2:
time: 28.4 us; the launch traced here: 28.2 us
  Pallas kernels  11.4 us (40%)
  starting transfers between devices  10 us (35%)
  waiting for transfers between devices  6.68 us (24%)
    pallas_call x2, Pallas kernels, prepare(): pl.pallas_call(functools.partial(prepare_kernel, level), out_shape=[band_...  6.92 us
    ppermute x2, waiting for transfers between devices, exchange(): first_swapped = lax.ppermute(first, axes, beside)  5.29 us
    ppermute x2, starting transfers between devices, exchange(): relayed = lax.ppermute(first_swapped, axes, onward)  4.35 us
    ppermute x2, starting transfers between devices, exchange(): first_swapped = lax.ppermute(first, axes, beside)  2.9 us
    ppermute x2, starting transfers between devices, exchange(): second_swapped = lax.ppermute(second, axes, beside)  1.98 us
    pallas_call x2, Pallas kernels, enter(): pl.pallas_call(functools.partial(enter_kernel, rows[0] * size), out_shape...  1.89 us
    ppermute x1, waiting for transfers between devices, per_device(): other_cols = lax.ppermute(block_cols, 'depth', over_depth)  1.37 us
    pallas_call x1, Pallas kernels, per_device(): pl.pallas_call(bottom_kernel, out_shape=jax.ShapeDtypeStruct(sources.shap...  1.21 us
  transfers between devices with their start and end apart: 10, of which 3 were waited for; matrix products, arithmetic and copies ran while one was open for 0% of the time, Pallas kernels for 35%

profile of v2, /device:TPU:0, one launch (start us, length us, event | category | flops | bytes accessed | tf_op | source)
XLA Modules:
  0.0 28.2 jit_solution(14460662619705525874)
XLA Ops:
  0.0 0.5 %collective-permute-start.5 = (f32[1,4,7,2,128,128]{5,4,3,2,1,0:T(8,128)}, f32[1,4,7,2,128,128]{5,4,3,2,1,0:T(8,128)S(1)}, u32[]{:S(2)}, u32[]{:S(2)}) collective-permute-start(f32[1,4,7,2,128,128]{5,4,3,2,1,0:T(8,128)} %own.3), channel_id=1, source_target_pairs={{0,8},{8,0},{1,9},{9,1},{2,10},{10,2},{3,11},{11,3},{4,12},{12,4},... | collective-permute-start | bytes 11010056 | tf_op jit(solution)/shard_map/ppermute | solution.py:328
  0.5 0.9 %enter.3 = (f32[96,256]{1,0:T(8,128)S(1)}, f32[2,256]{1,0:T(2,128)S(1)}) custom-call(f32[3,2,16,512]{3,2,1,0:T(8,128)} %sources.3, s32[1,512]{1,0:T(1,128)} %bitcast.1, f32[2,512]{1,0:T(2,128)} %refl_coef.3), custom_call_target="tpu_custom_call" | custom-call | tf_op jit(solution)/shard_map/enter/pallas_call | solution.py:334
  1.4 2.5 %collective-permute-start.1 = (f32[96,256]{1,0:T(8,128)S(1)}, f32[96,256]{1,0:T(8,128)S(1)}, u32[]{:S(2)}, u32[]{:S(2)}) collective-permute-start(f32[96,256]{1,0:T(8,128)S(1)} %get-tuple-element.19.refs_0_), channel_id=1, source_target_pairs={{0,1},{2,3},{4,5},{6,7},{8,9},{10,11},{12,13},{14,15},{1,0},{3,2},... | collective-permute-start | bytes 294920 | tf_op jit(solution)/shard_map/ppermute | solution.py:321
  4.0 0.9 %enter.2 = (f32[96,256]{1,0:T(8,128)S(1)}, f32[2,256]{1,0:T(2,128)S(1)}) custom-call(f32[3,2,16,512]{3,2,1,0:T(8,128)} %sources.3, s32[1,512]{1,0:T(1,128)} %bitcast.2, f32[2,512]{1,0:T(2,128)} %refl_coef.3), custom_call_target="tpu_custom_call" | custom-call | tf_op jit(solution)/shard_map/enter/pallas_call | solution.py:334
  4.9 0.1 collective-permute-start
  5.0 0.3 %collective-permute-start.3 = (f32[96,256]{1,0:T(8,128)S(1)}, f32[96,256]{1,0:T(8,128)S(1)}, u32[]{:S(2)}, u32[]{:S(2)}) collective-permute-start(f32[96,256]{1,0:T(8,128)S(1)} %get-tuple-element.18.refs_1_), channel_id=1, source_target_pairs={{1,2},{3,4},{5,6},{9,10},{11,12},{13,14},{0,8},{7,15},{2,1},{4,3},... | collective-permute-start | bytes 294920 | tf_op jit(solution)/shard_map/ppermute | solution.py:324
  5.3 2.1 %collective-permute-done.1.halo = f32[96,256]{1,0:T(8,128)S(1)} collective-permute-done((f32[96,256]{1,0:T(8,128)S(1)}, f32[96,256]{1,0:T(8,128)S(1)}, u32[]{:S(2)}, u32[]{:S(2)}) %collective-permute-start.1) | collective-permute-done | bytes 98336 | tf_op jit(solution)/shard_map/ppermute | solution.py:321
  7.5 1.8 %collective-permute-start.2 = (f32[96,256]{1,0:T(8,128)S(1)}, f32[96,256]{1,0:T(8,128)S(1)}, u32[]{:S(2)}, u32[]{:S(2)}) collective-permute-start(f32[96,256]{1,0:T(8,128)S(1)} %collective-permute-done.1.halo), channel_id=1, source_target_pairs={{0,2},{2,4},{4,6},{3,1},{5,3},{7,5},{6,7},{1,0},{8,10},{10,12},{12... | collective-permute-start | bytes 294920 | tf_op jit(solution)/shard_map/ppermute | solution.py:325
  9.3 0.0 collective-permute-start.4
  9.3 1.4 %collective-permute-done.4.other_cols = s32[1,4,7]{2,1,0:T(4,128)S(1)} collective-permute-done((s32[1,4,7]{2,1,0:T(4,128)}, s32[1,4,7]{2,1,0:T(4,128)S(1)}, u32[]{:S(2)}, u32[]{:S(2)}) %collective-permute-start.4) | collective-permute-done | bytes 144 | tf_op jit(solution)/shard_map/ppermute | solution.py:329
  10.7 0.0 collective-permute-done.5.received
  10.7 3.4 %prepare.2 = (bf16[4,9,128,256]{3,2,1,0:T(8,128)(2,1)S(1)}, bf16[4,9,128,256]{3,2,1,0:T(8,128)(2,1)S(1)}, f32[4,96,256]{2,1,0:T(8,128)S(1)}) custom-call(s32[1,4,7]{2,1,0:T(4,128)} %own_cols.3, s32[1,4,7]{2,1,0:T(4,128)S(1)} %collective-permute-done.4.other_cols, f32[1,4,7,2,128,128]{5,4,3,2,1,0:T(8,128)} %own.3, ...), custom_call_target="tpu_custom_call" | custom-call | flops 150994944 | bytes 7340032 | tf_op jit(solution)/shard_map/prepare/pallas_call | solution.py:366
  14.1 0.3 %early.2.sums = f32[4,96,256]{2,1,0:T(8,128)S(1)} custom-call(f32[96,256]{1,0:T(8,128)S(1)} %collective-permute-done.1.halo, bf16[4,9,128,256]{3,2,1,0:T(8,128)(2,1)S(1)} %get-tuple-element.20.high, bf16[4,9,128,256]{3,2,1,0:T(8,128)(2,1)S(1)} %get-tuple-element.21.low, f32[4,96,256]{2,1,0:T(8,128)S(1)} %get-tuple-element.22.sums), custom_call_target="tpu_custom_call" | custom-call | flops 37748736 | bytes 917504 | tf_op jit(solution)/shard_map/early/pallas_call | solution.py:383
  14.4 0.0 collective-permute-done.swapped
  14.4 0.0 collective-permute-done.3.diagonal
  14.5 0.0 collective-permute-done.2.relayed
  14.5 0.4 %first_rows.1 = (f32[96,256]{1,0:T(8,128)S(1)}, bf16[192,256]{1,0:T(8,128)(2,1)S(1)}, bf16[192,512]{1,0:T(8,128)(2,1)S(1)}) custom-call(f32[96,256]{1,0:T(8,128)S(1)} %collective-permute-done.swapped, f32[96,256]{1,0:T(8,128)S(1)} %collective-permute-done.2.relayed, f32[96,256]{1,0:T(8,128)S(1)} %collective-permute-done.3.diagonal, ...), custom_call_target="tpu_custom_call" | custom-call | flops 37748736 | bytes 917504 | tf_op jit(solution)/shard_map/first_rows/pallas_call | solution.py:397
  14.9 0.4 %collective-permute-start.7 = (f32[96,256]{1,0:T(8,128)S(1)}, f32[96,256]{1,0:T(8,128)S(1)}, u32[]{:S(2)}, u32[]{:S(2)}) collective-permute-start(f32[96,256]{1,0:T(8,128)S(1)} %get-tuple-element.27.refs_0_), channel_id=1, source_target_pairs={{0,1},{2,3},{4,5},{6,7},{8,9},{10,11},{12,13},{14,15},{1,0},{3,2},... | collective-permute-start | bytes 294920 | tf_op jit(solution)/shard_map/ppermute | solution.py:321
  15.2 0.3 %second_rows.1.refs_1_ = f32[96,256]{1,0:T(8,128)S(1)} custom-call(bf16[192,256]{1,0:T(8,128)(2,1)S(1)} %get-tuple-element.24.swapped, bf16[192,512]{1,0:T(8,128)(2,1)S(1)} %get-tuple-element.25.diagonal, bf16[4,9,128,256]{3,2,1,0:T(8,128)(2,1)S(1)} %get-tuple-element.20.high, bf16[4,9,128,256]{3,2,1,0:T(8,128)(2,1)S(1)} %get-tuple-element.21.low, ...), custom_call_target="tpu_custom_call" | custom-call | flops 37748736 | bytes 917504 | tf_op jit(solution)/shard_map/second_rows/pallas_call | solution.py:412
  15.5 1.9 %collective-permute-start.6 = (f32[96,256]{1,0:T(8,128)S(1)}, f32[96,256]{1,0:T(8,128)S(1)}, u32[]{:S(2)}, u32[]{:S(2)}) collective-permute-start(f32[96,256]{1,0:T(8,128)S(1)} %second_rows.1.refs_1_), channel_id=1, source_target_pairs={{0,1},{2,3},{4,5},{6,7},{8,9},{10,11},{12,13},{14,15},{1,0},{3,2},... | collective-permute-start | bytes 294920 | tf_op jit(solution)/shard_map/ppermute | solution.py:323
  17.4 0.0 collective-permute-start.9
  17.4 3.1 %collective-permute-done.7.halo = f32[96,256]{1,0:T(8,128)S(1)} collective-permute-done((f32[96,256]{1,0:T(8,128)S(1)}, f32[96,256]{1,0:T(8,128)S(1)}, u32[]{:S(2)}, u32[]{:S(2)}) %collective-permute-start.7) | collective-permute-done | bytes 98336 | tf_op jit(solution)/shard_map/ppermute | solution.py:321
  20.6 2.5 %collective-permute-start.8 = (f32[96,256]{1,0:T(8,128)S(1)}, f32[96,256]{1,0:T(8,128)S(1)}, u32[]{:S(2)}, u32[]{:S(2)}) collective-permute-start(f32[96,256]{1,0:T(8,128)S(1)} %collective-permute-done.7.halo), channel_id=1, source_target_pairs={{0,2},{2,4},{4,6},{3,1},{5,3},{7,5},{6,7},{1,0},{8,10},{10,12},{12... | collective-permute-start | bytes 294920 | tf_op jit(solution)/shard_map/ppermute | solution.py:325
  23.1 3.5 %prepare.3 = (bf16[4,9,128,256]{3,2,1,0:T(8,128)(2,1)S(1)}, bf16[4,9,128,256]{3,2,1,0:T(8,128)(2,1)S(1)}, f32[4,96,256]{2,1,0:T(8,128)S(1)}) custom-call(s32[1,4,7]{2,1,0:T(4,128)} %own_cols.3, s32[1,4,7]{2,1,0:T(4,128)S(1)} %collective-permute-done.4.other_cols, f32[1,4,7,2,128,128]{5,4,3,2,1,0:T(8,128)} %own.3, ...), custom_call_target="tpu_custom_call" | custom-call | flops 150994944 | bytes 7340032 | tf_op jit(solution)/shard_map/prepare/pallas_call | solution.py:366
  26.6 0.3 %early.3.sums = f32[4,96,256]{2,1,0:T(8,128)S(1)} custom-call(f32[96,256]{1,0:T(8,128)S(1)} %collective-permute-done.7.halo, bf16[4,9,128,256]{3,2,1,0:T(8,128)(2,1)S(1)} %get-tuple-element.28.high, bf16[4,9,128,256]{3,2,1,0:T(8,128)(2,1)S(1)} %get-tuple-element.29.low, f32[4,96,256]{2,1,0:T(8,128)S(1)} %get-tuple-element.30.sums), custom_call_target="tpu_custom_call" | custom-call | flops 37748736 | bytes 917504 | tf_op jit(solution)/shard_map/early/pallas_call | solution.py:383
  27.0 0.0 collective-permute-done.6.swapped
  27.0 0.0 collective-permute-done.9.diagonal
  27.0 0.0 collective-permute-done.8.relayed
  27.0 1.2 %bottom.1 = f32[3,2,16,512]{3,2,1,0:T(8,128)} custom-call(f32[96,256]{1,0:T(8,128)S(1)} %collective-permute-done.6.swapped, f32[96,256]{1,0:T(8,128)S(1)} %collective-permute-done.8.relayed, f32[96,256]{1,0:T(8,128)S(1)} %collective-permute-done.9.diagonal, bf16[4,9,128,256]{3,2,1,0:T(8,128)(2,1)S(1)} %get-tuple-element.28.high, ...), custom_call_target="tpu_custom_call" | custom-call | flops 37748736 | bytes 917504 | tf_op jit(solution)/shard_map/bottom/pallas_call | solution.py:424
Async XLA Ops:
  0.0 10.7 %collective-permute-start.5 = (f32[1,4,7,2,128,128]{5,4,3,2,1,0:T(8,128)}, f32[1,4,7,2,128,128]{5,4,3,2,1,0:T(8,128)S(1)}, u32[]{:S(2)}, u32[]{:S(2)}) collective-permute-start(f32[1,4,7,2,128,128]{5,4,3,2,1,0:T(8,128)} %own.3), channel_id=1, source_target_pairs={{0,8},{8,0},{1,9},{9,1},{2,10},{10,2},{3,11},{11,3},{4,12},{12,4},... | collective-permute-start | bytes 11010056 | tf_op jit(solution)/shard_map/ppermute | solution.py:328
  1.4 6.0 %collective-permute-start.1 = (f32[96,256]{1,0:T(8,128)S(1)}, f32[96,256]{1,0:T(8,128)S(1)}, u32[]{:S(2)}, u32[]{:S(2)}) collective-permute-start(f32[96,256]{1,0:T(8,128)S(1)} %get-tuple-element.19.refs_0_), channel_id=1, source_target_pairs={{0,1},{2,3},{4,5},{6,7},{8,9},{10,11},{12,13},{14,15},{1,0},{3,2},... | collective-permute-start | bytes 294920 | tf_op jit(solution)/shard_map/ppermute | solution.py:321
  4.9 9.5 %collective-permute-start = (f32[96,256]{1,0:T(8,128)S(1)}, f32[96,256]{1,0:T(8,128)S(1)}, u32[]{:S(2)}, u32[]{:S(2)}) collective-permute-start(f32[96,256]{1,0:T(8,128)S(1)} %get-tuple-element.18.refs_1_), channel_id=1, source_target_pairs={{0,1},{2,3},{4,5},{6,7},{8,9},{10,11},{12,13},{14,15},{1,0},{3,2},... | collective-permute-start | bytes 294920 | tf_op jit(solution)/shard_map/ppermute | solution.py:323
  5.0 9.4 %collective-permute-start.3 = (f32[96,256]{1,0:T(8,128)S(1)}, f32[96,256]{1,0:T(8,128)S(1)}, u32[]{:S(2)}, u32[]{:S(2)}) collective-permute-start(f32[96,256]{1,0:T(8,128)S(1)} %get-tuple-element.18.refs_1_), channel_id=1, source_target_pairs={{1,2},{3,4},{5,6},{9,10},{11,12},{13,14},{0,8},{7,15},{2,1},{4,3},... | collective-permute-start | bytes 294920 | tf_op jit(solution)/shard_map/ppermute | solution.py:324
  7.5 7.0 %collective-permute-start.2 = (f32[96,256]{1,0:T(8,128)S(1)}, f32[96,256]{1,0:T(8,128)S(1)}, u32[]{:S(2)}, u32[]{:S(2)}) collective-permute-start(f32[96,256]{1,0:T(8,128)S(1)} %collective-permute-done.1.halo), channel_id=1, source_target_pairs={{0,2},{2,4},{4,6},{3,1},{5,3},{7,5},{6,7},{1,0},{8,10},{10,12},{12... | collective-permute-start | bytes 294920 | tf_op jit(solution)/shard_map/ppermute | solution.py:325
  9.3 1.4 %collective-permute-start.4 = (s32[1,4,7]{2,1,0:T(4,128)}, s32[1,4,7]{2,1,0:T(4,128)S(1)}, u32[]{:S(2)}, u32[]{:S(2)}) collective-permute-start(s32[1,4,7]{2,1,0:T(4,128)} %own_cols.3), channel_id=1, source_target_pairs={{0,8},{8,0},{1,9},{9,1},{2,10},{10,2},{3,11},{11,3},{4,12},{12,4},... | collective-permute-start | bytes 344 | tf_op jit(solution)/shard_map/ppermute | solution.py:329
  14.9 5.7 %collective-permute-start.7 = (f32[96,256]{1,0:T(8,128)S(1)}, f32[96,256]{1,0:T(8,128)S(1)}, u32[]{:S(2)}, u32[]{:S(2)}) collective-permute-start(f32[96,256]{1,0:T(8,128)S(1)} %get-tuple-element.27.refs_0_), channel_id=1, source_target_pairs={{0,1},{2,3},{4,5},{6,7},{8,9},{10,11},{12,13},{14,15},{1,0},{3,2},... | collective-permute-start | bytes 294920 | tf_op jit(solution)/shard_map/ppermute | solution.py:321
  15.5 11.4 %collective-permute-start.6 = (f32[96,256]{1,0:T(8,128)S(1)}, f32[96,256]{1,0:T(8,128)S(1)}, u32[]{:S(2)}, u32[]{:S(2)}) collective-permute-start(f32[96,256]{1,0:T(8,128)S(1)} %second_rows.1.refs_1_), channel_id=1, source_target_pairs={{0,1},{2,3},{4,5},{6,7},{8,9},{10,11},{12,13},{14,15},{1,0},{3,2},... | collective-permute-start | bytes 294920 | tf_op jit(solution)/shard_map/ppermute | solution.py:323
  17.4 9.5 %collective-permute-start.9 = (f32[96,256]{1,0:T(8,128)S(1)}, f32[96,256]{1,0:T(8,128)S(1)}, u32[]{:S(2)}, u32[]{:S(2)}) collective-permute-start(f32[96,256]{1,0:T(8,128)S(1)} %second_rows.1.refs_1_), channel_id=1, source_target_pairs={{1,2},{3,4},{5,6},{9,10},{11,12},{13,14},{0,8},{7,15},{2,1},{4,3},... | collective-permute-start | bytes 294920 | tf_op jit(solution)/shard_map/ppermute | solution.py:324
  20.6 6.4 %collective-permute-start.8 = (f32[96,256]{1,0:T(8,128)S(1)}, f32[96,256]{1,0:T(8,128)S(1)}, u32[]{:S(2)}, u32[]{:S(2)}) collective-permute-start(f32[96,256]{1,0:T(8,128)S(1)} %collective-permute-done.7.halo), channel_id=1, source_target_pairs={{0,2},{2,4},{4,6},{3,1},{5,3},{7,5},{6,7},{1,0},{8,10},{10,12},{12... | collective-permute-start | bytes 294920 | tf_op jit(solution)/shard_map/ppermute | solution.py:325

commit v3 on v2

--- a/solution.py
+++ b/solution.py
@@ -70,30 +70,31 @@
     return both[:rows] + both[rows:] + cross
 
 
-def prepare_kernel(level, own_cols, other_cols, own, received, *refs):
+def prepare_kernel(level, rows, own_cols, other_cols, own, received, *refs):
     fields, (high, low, sums, held, left, sems) = refs[:-6], refs[-6:]
-    block_rows, per_row, _, size, _ = held.shape
+    per_row, size = held.shape[1], held.shape[3]
+    block_rows = own.shape[1]
     here = lax.axis_index("depth") == level
     first_row = lax.axis_index("lat") * block_rows
-    for b in range(block_rows):
+    for i, b in enumerate(rows):
 
         @pl.when(here)
         def _():
-            pltpu.make_async_copy(own.at[0, b], held.at[b], sems.at[b]).start()
+            pltpu.make_async_copy(own.at[0, b], held.at[i], sems.at[i]).start()
 
         @pl.when(jnp.logical_not(here))
         def _():
-            pltpu.make_async_copy(received.at[0, b], held.at[b], sems.at[b]).start()
+            pltpu.make_async_copy(received.at[0, b], held.at[i], sems.at[i]).start()
 
     span = 2 * block_rows + 1
     zeros = jnp.zeros((size, 2 * size), jnp.bfloat16)
 
-    def clear(b, o):
-        high[b, o] = zeros
-        low[b, o] = zeros
+    def clear(i, o):
+        high[i, o] = zeros
+        low[i, o] = zeros
 
     rows_at, rows_repeated = [], []
-    for b in range(block_rows):
+    for i, b in enumerate(rows):
         first = first_row + b - block_rows
         at = [
             jnp.where(here, own_cols[0, b, j], other_cols[0, b, j]) - first
@@ -106,8 +107,8 @@
         rows_repeated.append(repeated)
         absent = (1 << span) - 1 - present
         if span - per_row == 2:
-            clear(b, sum(jnp.where(absent % (2 << o) == 0, 1, 0) for o in range(span - 1)))
-            clear(b, sum(jnp.where(absent >= (2 << o), 1, 0) for o in range(span - 1)))
+            clear(i, sum(jnp.where(absent % (2 << o) == 0, 1, 0) for o in range(span - 1)))
+            clear(i, sum(jnp.where(absent >= (2 << o), 1, 0) for o in range(span - 1)))
         else:
             repeated = True
 
@@ -116,7 +117,7 @@
             def clear_one(o, carry):
                 @pl.when(jnp.bitwise_and(jnp.right_shift(absent, o), 1) == 1)
                 def _():
-                    clear(b, o)
+                    clear(i, o)
 
                 return carry
 
@@ -126,39 +127,51 @@
     for field in fields:
         left[:, at_lane : at_lane + field.shape[1]] = pieces(field[...])
         at_lane += field.shape[1]
-    for b in range(block_rows):
-        at = rows_at[b]
-        pltpu.make_async_copy(own.at[0, b], held.at[b], sems.at[b]).wait()
-
-        @pl.when(rows_repeated[b])
+    for i, b in enumerate(rows):
+        at = rows_at[i]
+        pltpu.make_async_copy(own.at[0, b], held.at[i], sems.at[i]).wait()
+
+        @pl.when(rows_repeated[i])
         def _():
             for j in reversed(range(1, per_row)):
                 target = jnp.int32(per_row)
-                for i in range(j):
-                    target = jnp.where(at[i] == at[j], i, target)
+                for k in range(j):
+                    target = jnp.where(at[k] == at[j], k, target)
 
                 @pl.when(target < per_row)
                 def _():
-                    held[b, target] = held[b, target] + held[b, j]
+                    held[i, target] = held[i, target] + held[i, j]
 
         def split(n, carry):
-            rows = pl.ds(pl.multiple_of(n * 16, 16), 16)
+            part = pl.ds(pl.multiple_of(n * 16, 16), 16)
             for j in reversed(range(per_row)):
                 head, tail = head_and_tail(
-                    jnp.concatenate([held[b, j, 0, rows], held[b, j, 1, rows]], axis=1)
+                    jnp.concatenate([held[i, j, 0, part], held[i, j, 1, part]], axis=1)
                 )
-                high[b, at[j], rows] = head
-                low[b, at[j], rows] = tail
+                high[i, at[j], part] = head
+                low[i, at[j], part] = tail
             return carry
 
         lax.fori_loop(0, size // 16, split, 0)
-    for b in range(block_rows):
+    for i, b in enumerate(rows):
         band = slice(block_rows - b, 2 * block_rows - b)
-        sums[b] = product(left[...], high[b, band], low[b, band])
-
-
-def side_product(b, first, piece, is_before, high, low):
-    block_rows, _, size, _ = high.shape
+        sums[i] = product(left[...], high[i, band], low[i, band])
+
+
+class Bands:
+    def __init__(self, refs):
+        count = len(refs) // 2
+        self.high, self.low = refs[:count], refs[count:]
+        self.rows = [(n, i) for n, ref in enumerate(self.high) for i in range(ref.shape[0])]
+        self.size = self.high[0].shape[2]
+
+    def product(self, b, left, band):
+        n, i = self.rows[b]
+        return product(left, self.high[n][i, band], self.low[n][i, band])
+
+
+def side_product(b, first, piece, is_before, bands):
+    block_rows, size = len(bands.rows), bands.size
     last = first + piece.shape[1] // size
     if is_before:
         low_col, high_col, shift = max(b, first), last, -b
@@ -168,7 +181,7 @@
         return 0.0
     lanes = slice((low_col - first) * size, (high_col - first) * size)
     band = slice(low_col + shift, high_col + shift)
-    return product(piece[:, lanes], high[b, band], low[b, band])
+    return bands.product(b, piece[:, lanes], band)
 
 
 def by_side(run):
@@ -177,18 +190,19 @@
     pl.when(jnp.logical_not(even))(functools.partial(run, True))
 
 
-def early_kernel(halo, high, low, sums, out, left):
+def early_kernel(halo, *refs):
+    bands, parts, (out, left) = Bands(refs[:4]), refs[4:-2], refs[-2:]
     left[...] = pieces(halo[...])
 
     def run(swapped_before):
-        for b in range(high.shape[0]):
-            out[b] = sums[b] + side_product(b, 0, left, swapped_before, high, low)
+        for b, (n, i) in enumerate(bands.rows):
+            out[b] = parts[n][i] + side_product(b, 0, left, swapped_before, bands)
 
     by_side(run)
 
 
-def late_products(rows, swapped, diagonal, high, low, sums, finish):
-    first = (diagonal.shape[1] - swapped.shape[1]) // high.shape[2]
+def late_products(rows, swapped, diagonal, bands, sums, finish):
+    first = (diagonal.shape[1] - swapped.shape[1]) // bands.size
 
     def run(swapped_before):
         for i, b in enumerate(rows):
@@ -196,8 +210,8 @@
                 i,
                 b,
                 sums[b]
-                + side_product(b, 0, diagonal, not swapped_before, high, low)
-                + side_product(b, first, swapped, swapped_before, high, low),
+                + side_product(b, 0, diagonal, not swapped_before, bands)
+                + side_product(b, first, swapped, swapped_before, bands),
             )
 
     by_side(run)
@@ -218,7 +232,9 @@
     )
 
 
-def level_rows(rows, swapped, diagonal, high, low, sums, next_coef, out):
+def level_rows(rows, swapped, diagonal, *refs):
+    bands, (sums, next_coef, out) = Bands(refs[:4]), refs[4:]
+
     def finish(i, b, value):
         re, im = leaving(value)
         channels, size = re.shape
@@ -227,31 +243,19 @@
         out[:channels, lanes] = re
         out[channels:, lanes] = im
 
-    late_products(rows, swapped, diagonal, high, low, sums, finish)
-
-
-def first_rows_kernel(
-    rows, swapped, relayed, diagonal, high, low, sums, next_coef, out, swapped_left, diagonal_left
-):
+    late_products(rows, swapped, diagonal, bands, sums, finish)
+
+
+def first_rows_kernel(rows, swapped, relayed, diagonal, *refs):
+    operands, (swapped_left, diagonal_left) = refs[:-2], refs[-2:]
     take_late(swapped, relayed, diagonal, swapped_left, diagonal_left)
-    level_rows(rows, swapped_left, diagonal_left, high, low, sums, next_coef, out)
-
-
-def bottom_kernel(
-    swapped,
-    relayed,
-    diagonal,
-    high,
-    low,
-    sums,
-    out,
-    held,
-    swapped_left,
-    diagonal_left,
-    sems,
-):
+    level_rows(rows, swapped_left, diagonal_left, *operands)
+
+
+def bottom_kernel(swapped, relayed, diagonal, *refs):
+    bands, (sums, out, held, swapped_left, diagonal_left, sems) = Bands(refs[:4]), refs[4:]
     panels, _, part, _ = out.shape
-    block_rows, _, size, _ = high.shape
+    block_rows, size = len(bands.rows), bands.size
     take_late(swapped, relayed, diagonal, swapped_left, diagonal_left)
 
     def copy_out(b):
@@ -266,7 +270,7 @@
         held[b, :, 1] = im.reshape(panels, part, size)
         copy_out(b).start()
 
-    late_products(range(block_rows), swapped_left, diagonal_left, high, low, sums, finish)
+    late_products(range(block_rows), swapped_left, diagonal_left, bands, sums, finish)
     for b in range(block_rows):
         copy_out(b).wait()
 
@@ -358,42 +362,45 @@
     coefs.append(coef)
     second_total, early, late = exchange(first_total, enter_second)
 
-    band_shape = jax.ShapeDtypeStruct((block_rows, 2 * block_rows + 1, size, 2 * size), bf16)
     sums_shape = jax.ShapeDtypeStruct((block_rows, 2 * channels, 2 * size), f32)
     macs = 6 * channels * points * 2 * size
 
-    def prepare(level, *fields):
+    def prepare(level, rows, *fields):
+        band = jax.ShapeDtypeStruct((len(rows), 2 * block_rows + 1, size, 2 * size), bf16)
+        sums = jax.ShapeDtypeStruct((len(rows), 2 * channels, 2 * size), f32)
         return pl.pallas_call(
-            functools.partial(prepare_kernel, level),
-            out_shape=[band_shape, band_shape, sums_shape],
+            functools.partial(prepare_kernel, level, rows),
+            out_shape=[band, band, sums],
             in_specs=[SMEM, SMEM, HBM, HBM] + [VMEM] * len(fields),
             out_specs=[VMEM] * 3,
             scratch_shapes=[
-                pltpu.VMEM(blocks.shape[1:], f32),
+                pltpu.VMEM((len(rows),) + blocks.shape[2:], f32),
                 pltpu.VMEM((4 * channels, points), bf16),
-                pltpu.SemaphoreType.DMA((block_rows,)),
+                pltpu.SemaphoreType.DMA((len(rows),)),
             ],
             compiler_params=params(16),
-            cost_estimate=cost(4 * macs, 8 * blocks.size),
+            cost_estimate=cost(2 * macs, 4 * blocks.size),
             name="prepare",
         )(in_hbm(block_cols), other_cols, in_hbm(blocks), other_blocks, *fields)
 
     def early_products(level, halo, *fields):
-        high, low, sums = prepare(level, *fields)
+        first = prepare(level, first_rows, *fields)
+        second = prepare(level, second_rows, *fields)
+        bands = (first[0], second[0], first[1], second[1])
         sums = pl.pallas_call(
             early_kernel,
             out_shape=sums_shape,
-            in_specs=[VMEM] * 4,
+            in_specs=[VMEM] * 7,
             out_specs=VMEM,
             scratch_shapes=[pltpu.VMEM(*piece_shape(first_rows))],
             compiler_params=params(12),
             cost_estimate=cost(macs, blocks.size),
             name="early",
-        )(halo, high, low, sums)
-        return high, low, sums
+        )(halo, *bands, first[2], second[2])
+        return *bands, sums
 
     every_row = range(block_rows)
-    high, low, sums = early_products(0, early, first_total, second_total)
+    bands = early_products(0, early, first_total, second_total)
     first_part, swapped_left, diagonal_left = pl.pallas_call(
         functools.partial(first_rows_kernel, first_rows),
         out_shape=[
@@ -401,30 +408,30 @@
             jax.ShapeDtypeStruct(*piece_shape(second_rows)),
             jax.ShapeDtypeStruct(*piece_shape(every_row)),
         ],
-        in_specs=[VMEM] * 7,
+        in_specs=[VMEM] * 9,
         out_specs=[VMEM] * 3,
         compiler_params=params(12),
         cost_estimate=cost(macs, blocks.size),
         name="first_rows",
-    )(*late, high, low, sums, coefs[0])
+    )(*late, *bands, coefs[0])
 
     def level_second():
         return pl.pallas_call(
             functools.partial(level_rows, second_rows),
             out_shape=part_shape(second_rows),
-            in_specs=[VMEM] * 6,
+            in_specs=[VMEM] * 8,
             out_specs=VMEM,
             compiler_params=params(12),
             cost_estimate=cost(macs, blocks.size),
             name="second_rows",
-        )(swapped_left, diagonal_left, high, low, sums, coefs[1])
+        )(swapped_left, diagonal_left, *bands, coefs[1])
 
     second_part, early, late = exchange(first_part, level_second)
-    last_high, last_low, last_sums = early_products(1, early, first_part, second_part)
+    last_bands = early_products(1, early, first_part, second_part)
     return pl.pallas_call(
         bottom_kernel,
         out_shape=jax.ShapeDtypeStruct(sources.shape, f32),
-        in_specs=[VMEM] * 6,
+        in_specs=[VMEM] * 8,
         out_specs=HBM,
         scratch_shapes=[
             pltpu.VMEM((block_rows, panels, 2, part, size), f32),
@@ -435,7 +442,7 @@
         compiler_params=params(12),
         cost_estimate=cost(macs, blocks.size),
         name="bottom",
-    )(*late, last_high, last_low, last_sums)
+    )(*late, *last_bands)
 
 
 def solution(mesh):

time: 28.4 us -> 30.4 us (1.070)
  Pallas kernels: 11.4 us -> 14.3 us
  waiting for transfers between devices: 6.68 us -> 6.11 us
  starting transfers between devices: 10 us -> 9.51 us
    pallas_call x4 -> x6, Pallas kernels: 7.59 us -> 10.5 us  [the longest x4 9.83 us: prepare(): pl.pallas_call(functools.partial(prepare_kernel, level, rows), out_shape=...]
    ppermute x2, waiting for transfers between devices: 5.29 us -> 4.72 us  [exchange(): first_swapped = lax.ppermute(first, axes, beside)]
    ppermute x2, starting transfers between devices: 4.35 us -> 3.85 us  [exchange(): relayed = lax.ppermute(first_swapped, axes, onward)]
  transfers between devices with their start and end apart: 10 -> 10, of which waited for: 3 -> 3; matrix products, arithmetic and copies ran while one was open for 0% -> 0% of each run, Pallas kernels for 35% -> 42%
where the time goes in v3:
time: 30.4 us; the launch traced here: 30.1 us
  Pallas kernels  14.3 us (47%)
  starting transfers between devices  9.51 us (31%)
  waiting for transfers between devices  6.11 us (20%)
    pallas_call x4, Pallas kernels, prepare(): pl.pallas_call(functools.partial(prepare_kernel, level, rows), out_shape=...  9.83 us
    ppermute x2, waiting for transfers between devices, exchange(): first_swapped = lax.ppermute(first, axes, beside)  4.72 us
    ppermute x2, starting transfers between devices, exchange(): relayed = lax.ppermute(first_swapped, axes, onward)  3.85 us
    ppermute x2, starting transfers between devices, exchange(): first_swapped = lax.ppermute(first, axes, beside)  2.77 us
    ppermute x2, starting transfers between devices, exchange(): second_swapped = lax.ppermute(second, axes, beside)  2.11 us
    pallas_call x2, Pallas kernels, enter(): pl.pallas_call(functools.partial(enter_kernel, rows[0] * size), out_shape...  1.89 us
    ppermute x1, waiting for transfers between devices, per_device(): other_cols = lax.ppermute(block_cols, 'depth', over_depth)  1.37 us
    pallas_call x1, Pallas kernels, per_device(): pl.pallas_call(bottom_kernel, out_shape=jax.ShapeDtypeStruct(sources.shap...  1.21 us
  transfers between devices with their start and end apart: 10, of which 3 were waited for; matrix products, arithmetic and copies ran while one was open for 0% of the time, Pallas kernels for 42%

profile of v3, /device:TPU:0, one launch (start us, length us, event | category | flops | bytes accessed | tf_op | source)
XLA Modules:
  0.0 30.1 jit_solution(10113226962302392010)
XLA Ops:
  0.0 0.5 %collective-permute-start.5 = (f32[1,4,7,2,128,128]{5,4,3,2,1,0:T(8,128)}, f32[1,4,7,2,128,128]{5,4,3,2,1,0:T(8,128)S(1)}, u32[]{:S(2)}, u32[]{:S(2)}) collective-permute-start(f32[1,4,7,2,128,128]{5,4,3,2,1,0:T(8,128)} %own.7), channel_id=1, source_target_pairs={{0,8},{8,0},{1,9},{9,1},{2,10},{10,2},{3,11},{11,3},{4,12},{12,4},... | collective-permute-start | bytes 11010056 | tf_op jit(solution)/shard_map/ppermute | solution.py:332
  0.5 0.9 %enter.3 = (f32[96,256]{1,0:T(8,128)S(1)}, f32[2,256]{1,0:T(2,128)S(1)}) custom-call(f32[3,2,16,512]{3,2,1,0:T(8,128)} %sources.3, s32[1,512]{1,0:T(1,128)} %bitcast.1, f32[2,512]{1,0:T(2,128)} %refl_coef.3), custom_call_target="tpu_custom_call" | custom-call | tf_op jit(solution)/shard_map/enter/pallas_call | solution.py:338
  1.4 2.5 %collective-permute-start.1 = (f32[96,256]{1,0:T(8,128)S(1)}, f32[96,256]{1,0:T(8,128)S(1)}, u32[]{:S(2)}, u32[]{:S(2)}) collective-permute-start(f32[96,256]{1,0:T(8,128)S(1)} %get-tuple-element.25.refs_0_), channel_id=1, source_target_pairs={{0,1},{2,3},{4,5},{6,7},{8,9},{10,11},{12,13},{14,15},{1,0},{3,2},... | collective-permute-start | bytes 294920 | tf_op jit(solution)/shard_map/ppermute | solution.py:325
  4.0 0.9 %enter.2 = (f32[96,256]{1,0:T(8,128)S(1)}, f32[2,256]{1,0:T(2,128)S(1)}) custom-call(f32[3,2,16,512]{3,2,1,0:T(8,128)} %sources.3, s32[1,512]{1,0:T(1,128)} %bitcast.2, f32[2,512]{1,0:T(2,128)} %refl_coef.3), custom_call_target="tpu_custom_call" | custom-call | tf_op jit(solution)/shard_map/enter/pallas_call | solution.py:338
  4.9 0.1 collective-permute-start
  5.0 0.3 collective-permute-start.3
  5.3 2.1 %collective-permute-done.1.halo = f32[96,256]{1,0:T(8,128)S(1)} collective-permute-done((f32[96,256]{1,0:T(8,128)S(1)}, f32[96,256]{1,0:T(8,128)S(1)}, u32[]{:S(2)}, u32[]{:S(2)}) %collective-permute-start.1) | collective-permute-done | bytes 98336 | tf_op jit(solution)/shard_map/ppermute | solution.py:325
  7.5 1.8 %collective-permute-start.2 = (f32[96,256]{1,0:T(8,128)S(1)}, f32[96,256]{1,0:T(8,128)S(1)}, u32[]{:S(2)}, u32[]{:S(2)}) collective-permute-start(f32[96,256]{1,0:T(8,128)S(1)} %collective-permute-done.1.halo), channel_id=1, source_target_pairs={{0,2},{2,4},{4,6},{3,1},{5,3},{7,5},{6,7},{1,0},{8,10},{10,12},{12... | collective-permute-start | bytes 294920 | tf_op jit(solution)/shard_map/ppermute | solution.py:329
  9.3 0.0 collective-permute-start.4
  9.3 1.4 %collective-permute-done.4.other_cols = s32[1,4,7]{2,1,0:T(4,128)S(1)} collective-permute-done((s32[1,4,7]{2,1,0:T(4,128)}, s32[1,4,7]{2,1,0:T(4,128)S(1)}, u32[]{:S(2)}, u32[]{:S(2)}) %collective-permute-start.4) | collective-permute-done | bytes 144 | tf_op jit(solution)/shard_map/ppermute | solution.py:333
  10.7 0.0 collective-permute-done.5.received
  10.7 2.8 %prepare.4 = (bf16[2,9,128,256]{3,2,1,0:T(8,128)(2,1)S(1)}, bf16[2,9,128,256]{3,2,1,0:T(8,128)(2,1)S(1)}, f32[2,96,256]{2,1,0:T(8,128)S(1)}) custom-call(s32[1,4,7]{2,1,0:T(4,128)} %own_cols.7, s32[1,4,7]{2,1,0:T(4,128)S(1)} %collective-permute-done.4.other_cols, f32[1,4,7,2,128,128]{5,4,3,2,1,0:T(8,128)} %own.7, ...), custom_call_target="tpu_custom_call" | custom-call | flops 75497472 | bytes 3670016 | tf_op jit(solution)/shard_map/prepare/pallas_call | solution.py:371
  13.5 2.7 %prepare.5 = (bf16[2,9,128,256]{3,2,1,0:T(8,128)(2,1)S(1)}, bf16[2,9,128,256]{3,2,1,0:T(8,128)(2,1)S(1)}, f32[2,96,256]{2,1,0:T(8,128)S(1)}) custom-call(s32[1,4,7]{2,1,0:T(4,128)} %own_cols.7, s32[1,4,7]{2,1,0:T(4,128)S(1)} %collective-permute-done.4.other_cols, f32[1,4,7,2,128,128]{5,4,3,2,1,0:T(8,128)} %own.7, ...), custom_call_target="tpu_custom_call" | custom-call | flops 75497472 | bytes 3670016 | tf_op jit(solution)/shard_map/prepare/pallas_call | solution.py:371
  16.1 0.3 %early.2.refs_4_ = f32[4,96,256]{2,1,0:T(8,128)S(1)} custom-call(f32[96,256]{1,0:T(8,128)S(1)} %collective-permute-done.1.halo, bf16[2,9,128,256]{3,2,1,0:T(8,128)(2,1)S(1)} %get-tuple-element.26.refs_0_, bf16[2,9,128,256]{3,2,1,0:T(8,128)(2,1)S(1)} %get-tuple-element.27.refs_1_, bf16[2,9,128,256]{3,2,1,0:T(8,128)(2,1)S(1)} %get-tuple-element.28.refs_2_, ...), custom_call_target="tpu_custom_call" | custom-call | flops 37748736 | bytes 917504 | tf_op jit(solution)/shard_map/early/pallas_call | solution.py:390
  16.5 0.0 collective-permute-done.swapped
  16.5 0.0 collective-permute-done.3.diagonal
  16.5 0.0 collective-permute-done.2.relayed
  16.5 0.4 %first_rows.1 = (f32[96,256]{1,0:T(8,128)S(1)}, bf16[192,256]{1,0:T(8,128)(2,1)S(1)}, bf16[192,512]{1,0:T(8,128)(2,1)S(1)}) custom-call(f32[96,256]{1,0:T(8,128)S(1)} %collective-permute-done.swapped, f32[96,256]{1,0:T(8,128)S(1)} %collective-permute-done.2.relayed, f32[96,256]{1,0:T(8,128)S(1)} %collective-permute-done.3.diagonal, ...), custom_call_target="tpu_custom_call" | custom-call | flops 37748736 | bytes 917504 | tf_op jit(solution)/shard_map/first_rows/pallas_call | solution.py:404
  16.9 0.2 collective-permute-start.7
  17.1 0.3 %second_rows.1.refs_1_ = f32[96,256]{1,0:T(8,128)S(1)} custom-call(bf16[192,256]{1,0:T(8,128)(2,1)S(1)} %get-tuple-element.33.swapped, bf16[192,512]{1,0:T(8,128)(2,1)S(1)} %get-tuple-element.34.diagonal, bf16[2,9,128,256]{3,2,1,0:T(8,128)(2,1)S(1)} %get-tuple-element.26.refs_0_, bf16[2,9,128,256]{3,2,1,0:T(8,128)(2,1)S(1)} %get-tuple-element.27.refs_1_, ...), custom_call_target="tpu_custom_call" | custom-call | flops 37748736 | bytes 917504 | tf_op jit(solution)/shard_map/second_rows/pallas_call | solution.py:419
  17.5 2.0 %collective-permute-start.6 = (f32[96,256]{1,0:T(8,128)S(1)}, f32[96,256]{1,0:T(8,128)S(1)}, u32[]{:S(2)}, u32[]{:S(2)}) collective-permute-start(f32[96,256]{1,0:T(8,128)S(1)} %second_rows.1.refs_1_), channel_id=1, source_target_pairs={{0,1},{2,3},{4,5},{6,7},{8,9},{10,11},{12,13},{14,15},{1,0},{3,2},... | collective-permute-start | bytes 294920 | tf_op jit(solution)/shard_map/ppermute | solution.py:327
  19.5 0.0 collective-permute-start.9
  19.5 2.6 %collective-permute-done.7.halo = f32[96,256]{1,0:T(8,128)S(1)} collective-permute-done((f32[96,256]{1,0:T(8,128)S(1)}, f32[96,256]{1,0:T(8,128)S(1)}, u32[]{:S(2)}, u32[]{:S(2)}) %collective-permute-start.7) | collective-permute-done | bytes 98336 | tf_op jit(solution)/shard_map/ppermute | solution.py:325
  22.1 2.0 %collective-permute-start.8 = (f32[96,256]{1,0:T(8,128)S(1)}, f32[96,256]{1,0:T(8,128)S(1)}, u32[]{:S(2)}, u32[]{:S(2)}) collective-permute-start(f32[96,256]{1,0:T(8,128)S(1)} %collective-permute-done.7.halo), channel_id=1, source_target_pairs={{0,2},{2,4},{4,6},{3,1},{5,3},{7,5},{6,7},{1,0},{8,10},{10,12},{12... | collective-permute-start | bytes 294920 | tf_op jit(solution)/shard_map/ppermute | solution.py:329
  24.1 2.0 %prepare.7 = (bf16[2,9,128,256]{3,2,1,0:T(8,128)(2,1)S(1)}, bf16[2,9,128,256]{3,2,1,0:T(8,128)(2,1)S(1)}, f32[2,96,256]{2,1,0:T(8,128)S(1)}) custom-call(s32[1,4,7]{2,1,0:T(4,128)} %own_cols.7, s32[1,4,7]{2,1,0:T(4,128)S(1)} %collective-permute-done.4.other_cols, f32[1,4,7,2,128,128]{5,4,3,2,1,0:T(8,128)} %own.7, ...), custom_call_target="tpu_custom_call" | custom-call | flops 75497472 | bytes 3670016 | tf_op jit(solution)/shard_map/prepare/pallas_call | solution.py:371
  26.1 2.4 %prepare.6 = (bf16[2,9,128,256]{3,2,1,0:T(8,128)(2,1)S(1)}, bf16[2,9,128,256]{3,2,1,0:T(8,128)(2,1)S(1)}, f32[2,96,256]{2,1,0:T(8,128)S(1)}) custom-call(s32[1,4,7]{2,1,0:T(4,128)} %own_cols.7, s32[1,4,7]{2,1,0:T(4,128)S(1)} %collective-permute-done.4.other_cols, f32[1,4,7,2,128,128]{5,4,3,2,1,0:T(8,128)} %own.7, ...), custom_call_target="tpu_custom_call" | custom-call | flops 75497472 | bytes 3670016 | tf_op jit(solution)/shard_map/prepare/pallas_call | solution.py:371
  28.5 0.3 %early.3.refs_4_ = f32[4,96,256]{2,1,0:T(8,128)S(1)} custom-call(f32[96,256]{1,0:T(8,128)S(1)} %collective-permute-done.7.halo, bf16[2,9,128,256]{3,2,1,0:T(8,128)(2,1)S(1)} %get-tuple-element.37.refs_0_, bf16[2,9,128,256]{3,2,1,0:T(8,128)(2,1)S(1)} %get-tuple-element.38.refs_1_, bf16[2,9,128,256]{3,2,1,0:T(8,128)(2,1)S(1)} %get-tuple-element.39.refs_2_, ...), custom_call_target="tpu_custom_call" | custom-call | flops 37748736 | bytes 917504 | tf_op jit(solution)/shard_map/early/pallas_call | solution.py:390
  28.8 0.0 collective-permute-done.6.swapped
  28.8 0.0 collective-permute-done.9.diagonal
  28.8 0.0 collective-permute-done.8.relayed
  28.9 1.2 %bottom.1 = f32[3,2,16,512]{3,2,1,0:T(8,128)} custom-call(f32[96,256]{1,0:T(8,128)S(1)} %collective-permute-done.6.swapped, f32[96,256]{1,0:T(8,128)S(1)} %collective-permute-done.8.relayed, f32[96,256]{1,0:T(8,128)S(1)} %collective-permute-done.9.diagonal, bf16[2,9,128,256]{3,2,1,0:T(8,128)(2,1)S(1)} %get-tuple-element.37.refs_0_, ...), custom_call_target="tpu_custom_call" | custom-call | flops 37748736 | bytes 917504 | tf_op jit(solution)/shard_map/bottom/pallas_call | solution.py:431
Async XLA Ops:
  0.0 10.7 %collective-permute-start.5 = (f32[1,4,7,2,128,128]{5,4,3,2,1,0:T(8,128)}, f32[1,4,7,2,128,128]{5,4,3,2,1,0:T(8,128)S(1)}, u32[]{:S(2)}, u32[]{:S(2)}) collective-permute-start(f32[1,4,7,2,128,128]{5,4,3,2,1,0:T(8,128)} %own.7), channel_id=1, source_target_pairs={{0,8},{8,0},{1,9},{9,1},{2,10},{10,2},{3,11},{11,3},{4,12},{12,4},... | collective-permute-start | bytes 11010056 | tf_op jit(solution)/shard_map/ppermute | solution.py:332
  1.4 6.0 %collective-permute-start.1 = (f32[96,256]{1,0:T(8,128)S(1)}, f32[96,256]{1,0:T(8,128)S(1)}, u32[]{:S(2)}, u32[]{:S(2)}) collective-permute-start(f32[96,256]{1,0:T(8,128)S(1)} %get-tuple-element.25.refs_0_), channel_id=1, source_target_pairs={{0,1},{2,3},{4,5},{6,7},{8,9},{10,11},{12,13},{14,15},{1,0},{3,2},... | collective-permute-start | bytes 294920 | tf_op jit(solution)/shard_map/ppermute | solution.py:325
  4.9 11.5 %collective-permute-start = (f32[96,256]{1,0:T(8,128)S(1)}, f32[96,256]{1,0:T(8,128)S(1)}, u32[]{:S(2)}, u32[]{:S(2)}) collective-permute-start(f32[96,256]{1,0:T(8,128)S(1)} %get-tuple-element.24.refs_1_), channel_id=1, source_target_pairs={{0,1},{2,3},{4,5},{6,7},{8,9},{10,11},{12,13},{14,15},{1,0},{3,2},... | collective-permute-start | bytes 294920 | tf_op jit(solution)/shard_map/ppermute | solution.py:327
  5.0 11.5 %collective-permute-start.3 = (f32[96,256]{1,0:T(8,128)S(1)}, f32[96,256]{1,0:T(8,128)S(1)}, u32[]{:S(2)}, u32[]{:S(2)}) collective-permute-start(f32[96,256]{1,0:T(8,128)S(1)} %get-tuple-element.24.refs_1_), channel_id=1, source_target_pairs={{1,2},{3,4},{5,6},{9,10},{11,12},{13,14},{0,8},{7,15},{2,1},{4,3},... | collective-permute-start | bytes 294920 | tf_op jit(solution)/shard_map/ppermute | solution.py:328
  7.5 9.0 %collective-permute-start.2 = (f32[96,256]{1,0:T(8,128)S(1)}, f32[96,256]{1,0:T(8,128)S(1)}, u32[]{:S(2)}, u32[]{:S(2)}) collective-permute-start(f32[96,256]{1,0:T(8,128)S(1)} %collective-permute-done.1.halo), channel_id=1, source_target_pairs={{0,2},{2,4},{4,6},{3,1},{5,3},{7,5},{6,7},{1,0},{8,10},{10,12},{12... | collective-permute-start | bytes 294920 | tf_op jit(solution)/shard_map/ppermute | solution.py:329
  9.3 1.4 %collective-permute-start.4 = (s32[1,4,7]{2,1,0:T(4,128)}, s32[1,4,7]{2,1,0:T(4,128)S(1)}, u32[]{:S(2)}, u32[]{:S(2)}) collective-permute-start(s32[1,4,7]{2,1,0:T(4,128)} %own_cols.7), channel_id=1, source_target_pairs={{0,8},{8,0},{1,9},{9,1},{2,10},{10,2},{3,11},{11,3},{4,12},{12,4},... | collective-permute-start | bytes 344 | tf_op jit(solution)/shard_map/ppermute | solution.py:333
  16.9 5.2 %collective-permute-start.7 = (f32[96,256]{1,0:T(8,128)S(1)}, f32[96,256]{1,0:T(8,128)S(1)}, u32[]{:S(2)}, u32[]{:S(2)}) collective-permute-start(f32[96,256]{1,0:T(8,128)S(1)} %get-tuple-element.36.refs_0_), channel_id=1, source_target_pairs={{0,1},{2,3},{4,5},{6,7},{8,9},{10,11},{12,13},{14,15},{1,0},{3,2},... | collective-permute-start | bytes 294920 | tf_op jit(solution)/shard_map/ppermute | solution.py:325
  17.5 11.4 %collective-permute-start.6 = (f32[96,256]{1,0:T(8,128)S(1)}, f32[96,256]{1,0:T(8,128)S(1)}, u32[]{:S(2)}, u32[]{:S(2)}) collective-permute-start(f32[96,256]{1,0:T(8,128)S(1)} %second_rows.1.refs_1_), channel_id=1, source_target_pairs={{0,1},{2,3},{4,5},{6,7},{8,9},{10,11},{12,13},{14,15},{1,0},{3,2},... | collective-permute-start | bytes 294920 | tf_op jit(solution)/shard_map/ppermute | solution.py:327
  19.5 9.4 %collective-permute-start.9 = (f32[96,256]{1,0:T(8,128)S(1)}, f32[96,256]{1,0:T(8,128)S(1)}, u32[]{:S(2)}, u32[]{:S(2)}) collective-permute-start(f32[96,256]{1,0:T(8,128)S(1)} %second_rows.1.refs_1_), channel_id=1, source_target_pairs={{1,2},{3,4},{5,6},{9,10},{11,12},{13,14},{0,8},{7,15},{2,1},{4,3},... | collective-permute-start | bytes 294920 | tf_op jit(solution)/shard_map/ppermute | solution.py:328
  22.1 6.8 %collective-permute-start.8 = (f32[96,256]{1,0:T(8,128)S(1)}, f32[96,256]{1,0:T(8,128)S(1)}, u32[]{:S(2)}, u32[]{:S(2)}) collective-permute-start(f32[96,256]{1,0:T(8,128)S(1)} %collective-permute-done.7.halo), channel_id=1, source_target_pairs={{0,2},{2,4},{4,6},{3,1},{5,3},{7,5},{6,7},{1,0},{8,10},{10,12},{12... | collective-permute-start | bytes 294920 | tf_op jit(solution)/shard_map/ppermute | solution.py:329

commit v4 on v3

--- a/solution.py
+++ b/solution.py
@@ -159,9 +159,8 @@
 
 
 class Bands:
-    def __init__(self, refs):
-        count = len(refs) // 2
-        self.high, self.low = refs[:count], refs[count:]
+    def __init__(self, groups, refs):
+        self.high, self.low = refs[:groups], refs[groups : 2 * groups]
         self.rows = [(n, i) for n, ref in enumerate(self.high) for i in range(ref.shape[0])]
         self.size = self.high[0].shape[2]
 
@@ -190,8 +189,8 @@
     pl.when(jnp.logical_not(even))(functools.partial(run, True))
 
 
-def early_kernel(halo, *refs):
-    bands, parts, (out, left) = Bands(refs[:4]), refs[4:-2], refs[-2:]
+def early_kernel(groups, halo, *refs):
+    bands, parts, (out, left) = Bands(groups, refs), refs[2 * groups : -2], refs[-2:]
     left[...] = pieces(halo[...])
 
     def run(swapped_before):
@@ -232,8 +231,8 @@
     )
 
 
-def level_rows(rows, swapped, diagonal, *refs):
-    bands, (sums, next_coef, out) = Bands(refs[:4]), refs[4:]
+def level_rows(groups, rows, swapped, diagonal, *refs):
+    bands, (sums, next_coef, out) = Bands(groups, refs), refs[2 * groups :]
 
     def finish(i, b, value):
         re, im = leaving(value)
@@ -246,14 +245,15 @@
     late_products(rows, swapped, diagonal, bands, sums, finish)
 
 
-def first_rows_kernel(rows, swapped, relayed, diagonal, *refs):
+def first_rows_kernel(groups, rows, swapped, relayed, diagonal, *refs):
     operands, (swapped_left, diagonal_left) = refs[:-2], refs[-2:]
     take_late(swapped, relayed, diagonal, swapped_left, diagonal_left)
-    level_rows(rows, swapped_left, diagonal_left, *operands)
-
-
-def bottom_kernel(swapped, relayed, diagonal, *refs):
-    bands, (sums, out, held, swapped_left, diagonal_left, sems) = Bands(refs[:4]), refs[4:]
+    level_rows(groups, rows, swapped_left, diagonal_left, *operands)
+
+
+def bottom_kernel(groups, swapped, relayed, diagonal, *refs):
+    bands = Bands(groups, refs)
+    sums, out, held, swapped_left, diagonal_left, sems = refs[2 * groups :]
     panels, _, part, _ = out.shape
     block_rows, size = len(bands.rows), bands.size
     take_late(swapped, relayed, diagonal, swapped_left, diagonal_left)
@@ -383,32 +383,35 @@
             name="prepare",
         )(in_hbm(block_cols), other_cols, in_hbm(blocks), other_blocks, *fields)
 
+    every_row = range(block_rows)
+    row_groups = ((every_row,), (every_row[:1], every_row[1:]))
+
     def early_products(level, halo, *fields):
-        first = prepare(level, first_rows, *fields)
-        second = prepare(level, second_rows, *fields)
-        bands = (first[0], second[0], first[1], second[1])
+        ready = []
+        for rows in row_groups[level]:
+            ready.append(prepare(level, rows, *fields))
+        high, low, parts = zip(*ready)
         sums = pl.pallas_call(
-            early_kernel,
+            functools.partial(early_kernel, len(ready)),
             out_shape=sums_shape,
-            in_specs=[VMEM] * 7,
+            in_specs=[VMEM] * (1 + 3 * len(ready)),
             out_specs=VMEM,
             scratch_shapes=[pltpu.VMEM(*piece_shape(first_rows))],
             compiler_params=params(12),
             cost_estimate=cost(macs, blocks.size),
             name="early",
-        )(halo, *bands, first[2], second[2])
-        return *bands, sums
-
-    every_row = range(block_rows)
+        )(halo, *high, *low, *parts)
+        return *high, *low, sums
+
     bands = early_products(0, early, first_total, second_total)
     first_part, swapped_left, diagonal_left = pl.pallas_call(
-        functools.partial(first_rows_kernel, first_rows),
+        functools.partial(first_rows_kernel, len(row_groups[0]), first_rows),
         out_shape=[
             part_shape(first_rows),
             jax.ShapeDtypeStruct(*piece_shape(second_rows)),
             jax.ShapeDtypeStruct(*piece_shape(every_row)),
         ],
-        in_specs=[VMEM] * 9,
+        in_specs=[VMEM] * (4 + len(bands)),
         out_specs=[VMEM] * 3,
         compiler_params=params(12),
         cost_estimate=cost(macs, blocks.size),
@@ -417,9 +420,9 @@
 
     def level_second():
         return pl.pallas_call(
-            functools.partial(level_rows, second_rows),
+            functools.partial(level_rows, len(row_groups[0]), second_rows),
             out_shape=part_shape(second_rows),
-            in_specs=[VMEM] * 8,
+            in_specs=[VMEM] * (3 + len(bands)),
             out_specs=VMEM,
             compiler_params=params(12),
             cost_estimate=cost(macs, blocks.size),
@@ -429,9 +432,9 @@
     second_part, early, late = exchange(first_part, level_second)
     last_bands = early_products(1, early, first_part, second_part)
     return pl.pallas_call(
-        bottom_kernel,
+        functools.partial(bottom_kernel, len(row_groups[1])),
         out_shape=jax.ShapeDtypeStruct(sources.shape, f32),
-        in_specs=[VMEM] * 8,
+        in_specs=[VMEM] * (3 + len(last_bands)),
         out_specs=HBM,
         scratch_shapes=[
             pltpu.VMEM((block_rows, panels, 2, part, size), f32),

time: 30.4 us -> 29.4 us (0.967)
  Pallas kernels: 14.3 us -> 12.3 us
  waiting for transfers between devices: 6.11 us -> 6.68 us
  starting transfers between devices: 9.51 us -> 10 us
    pallas_call x4 -> x3, Pallas kernels: 9.83 us -> 7.79 us  [prepare(): pl.pallas_call(functools.partial(prepare_kernel, level, rows), out_shape=...]
    ppermute x2, waiting for transfers between devices: 4.72 us -> 5.29 us  [exchange(): first_swapped = lax.ppermute(first, axes, beside)]
    ppermute x2, starting transfers between devices: 3.85 us -> 4.35 us  [exchange(): relayed = lax.ppermute(first_swapped, axes, onward)]
  transfers between devices with their start and end apart: 10 -> 10, of which waited for: 3 -> 3; matrix products, arithmetic and copies ran while one was open for 0% -> 0% of each run, Pallas kernels for 42% -> 37%
where the time goes in v4:
time: 29.4 us; the launch traced here: 29.1 us
  Pallas kernels  12.3 us (42%)
  starting transfers between devices  10 us (34%)
  waiting for transfers between devices  6.68 us (23%)
    pallas_call x3, Pallas kernels, prepare(): pl.pallas_call(functools.partial(prepare_kernel, level, rows), out_shape=...  7.79 us
    ppermute x2, waiting for transfers between devices, exchange(): first_swapped = lax.ppermute(first, axes, beside)  5.29 us
    ppermute x2, starting transfers between devices, exchange(): relayed = lax.ppermute(first_swapped, axes, onward)  4.35 us
    ppermute x2, starting transfers between devices, exchange(): first_swapped = lax.ppermute(first, axes, beside)  2.9 us
    ppermute x2, starting transfers between devices, exchange(): second_swapped = lax.ppermute(second, axes, beside)  1.98 us
    pallas_call x2, Pallas kernels, enter(): pl.pallas_call(functools.partial(enter_kernel, rows[0] * size), out_shape...  1.89 us
    ppermute x1, waiting for transfers between devices, per_device(): other_cols = lax.ppermute(block_cols, 'depth', over_depth)  1.37 us
    pallas_call x1, Pallas kernels, per_device(): pl.pallas_call(functools.partial(bottom_kernel, len(row_groups[1])), out_...  1.21 us
  transfers between devices with their start and end apart: 10, of which 3 were waited for; matrix products, arithmetic and copies ran while one was open for 0% of the time, Pallas kernels for 37%

profile of v4, /device:TPU:0, one launch (start us, length us, event | category | flops | bytes accessed | tf_op | source)
XLA Modules:
  0.0 29.1 jit_solution(6679659709456286214)
XLA Ops:
  0.0 0.5 %collective-permute-start.5 = (f32[1,4,7,2,128,128]{5,4,3,2,1,0:T(8,128)}, f32[1,4,7,2,128,128]{5,4,3,2,1,0:T(8,128)S(1)}, u32[]{:S(2)}, u32[]{:S(2)}) collective-permute-start(f32[1,4,7,2,128,128]{5,4,3,2,1,0:T(8,128)} %own.5), channel_id=1, source_target_pairs={{0,8},{8,0},{1,9},{9,1},{2,10},{10,2},{3,11},{11,3},{4,12},{12,4},... | collective-permute-start | bytes 11010056 | tf_op jit(solution)/shard_map/ppermute | solution.py:332
  0.5 0.9 %enter.3 = (f32[96,256]{1,0:T(8,128)S(1)}, f32[2,256]{1,0:T(2,128)S(1)}) custom-call(f32[3,2,16,512]{3,2,1,0:T(8,128)} %sources.3, s32[1,512]{1,0:T(1,128)} %bitcast.1, f32[2,512]{1,0:T(2,128)} %refl_coef.3), custom_call_target="tpu_custom_call" | custom-call | tf_op jit(solution)/shard_map/enter/pallas_call | solution.py:338
  1.4 2.5 %collective-permute-start.1 = (f32[96,256]{1,0:T(8,128)S(1)}, f32[96,256]{1,0:T(8,128)S(1)}, u32[]{:S(2)}, u32[]{:S(2)}) collective-permute-start(f32[96,256]{1,0:T(8,128)S(1)} %get-tuple-element.22.refs_0_), channel_id=1, source_target_pairs={{0,1},{2,3},{4,5},{6,7},{8,9},{10,11},{12,13},{14,15},{1,0},{3,2},... | collective-permute-start | bytes 294920 | tf_op jit(solution)/shard_map/ppermute | solution.py:325
  4.0 0.9 %enter.2 = (f32[96,256]{1,0:T(8,128)S(1)}, f32[2,256]{1,0:T(2,128)S(1)}) custom-call(f32[3,2,16,512]{3,2,1,0:T(8,128)} %sources.3, s32[1,512]{1,0:T(1,128)} %bitcast.2, f32[2,512]{1,0:T(2,128)} %refl_coef.3), custom_call_target="tpu_custom_call" | custom-call | tf_op jit(solution)/shard_map/enter/pallas_call | solution.py:338
  4.9 0.1 collective-permute-start
  5.0 0.3 collective-permute-start.3
  5.3 2.1 %collective-permute-done.1.halo = f32[96,256]{1,0:T(8,128)S(1)} collective-permute-done((f32[96,256]{1,0:T(8,128)S(1)}, f32[96,256]{1,0:T(8,128)S(1)}, u32[]{:S(2)}, u32[]{:S(2)}) %collective-permute-start.1) | collective-permute-done | bytes 98336 | tf_op jit(solution)/shard_map/ppermute | solution.py:325
  7.5 1.8 %collective-permute-start.2 = (f32[96,256]{1,0:T(8,128)S(1)}, f32[96,256]{1,0:T(8,128)S(1)}, u32[]{:S(2)}, u32[]{:S(2)}) collective-permute-start(f32[96,256]{1,0:T(8,128)S(1)} %collective-permute-done.1.halo), channel_id=1, source_target_pairs={{0,2},{2,4},{4,6},{3,1},{5,3},{7,5},{6,7},{1,0},{8,10},{10,12},{12... | collective-permute-start | bytes 294920 | tf_op jit(solution)/shard_map/ppermute | solution.py:329
  9.3 0.0 collective-permute-start.4
  9.3 1.4 %collective-permute-done.4.other_cols = s32[1,4,7]{2,1,0:T(4,128)S(1)} collective-permute-done((s32[1,4,7]{2,1,0:T(4,128)}, s32[1,4,7]{2,1,0:T(4,128)S(1)}, u32[]{:S(2)}, u32[]{:S(2)}) %collective-permute-start.4) | collective-permute-done | bytes 144 | tf_op jit(solution)/shard_map/ppermute | solution.py:333
  10.7 0.0 collective-permute-done.5.received
  10.7 3.4 %prepare.3 = (bf16[4,9,128,256]{3,2,1,0:T(8,128)(2,1)S(1)}, bf16[4,9,128,256]{3,2,1,0:T(8,128)(2,1)S(1)}, f32[4,96,256]{2,1,0:T(8,128)S(1)}) custom-call(s32[1,4,7]{2,1,0:T(4,128)} %own_cols.5, s32[1,4,7]{2,1,0:T(4,128)S(1)} %collective-permute-done.4.other_cols, f32[1,4,7,2,128,128]{5,4,3,2,1,0:T(8,128)} %own.5, ...), custom_call_target="tpu_custom_call" | custom-call | flops 75497472 | bytes 3670016 | tf_op jit(solution)/shard_map/prepare/pallas_call | solution.py:371
  14.1 0.3 %early.2.refs_2_ = f32[4,96,256]{2,1,0:T(8,128)S(1)} custom-call(f32[96,256]{1,0:T(8,128)S(1)} %collective-permute-done.1.halo, bf16[4,9,128,256]{3,2,1,0:T(8,128)(2,1)S(1)} %get-tuple-element.23.refs_0_, bf16[4,9,128,256]{3,2,1,0:T(8,128)(2,1)S(1)} %get-tuple-element.24.refs_1_, f32[4,96,256]{2,1,0:T(8,128)S(1)} %get-tuple-element.25.refs_2_), custom_call_target="tpu_custom_call" | custom-call | flops 37748736 | bytes 917504 | tf_op jit(solution)/shard_map/early/pallas_call | solution.py:394
  14.4 0.0 collective-permute-done.swapped
  14.4 0.0 collective-permute-done.3.diagonal
  14.5 0.0 collective-permute-done.2.relayed
  14.5 0.4 %first_rows.1 = (f32[96,256]{1,0:T(8,128)S(1)}, bf16[192,256]{1,0:T(8,128)(2,1)S(1)}, bf16[192,512]{1,0:T(8,128)(2,1)S(1)}) custom-call(f32[96,256]{1,0:T(8,128)S(1)} %collective-permute-done.swapped, f32[96,256]{1,0:T(8,128)S(1)} %collective-permute-done.2.relayed, f32[96,256]{1,0:T(8,128)S(1)} %collective-permute-done.3.diagonal, ...), custom_call_target="tpu_custom_call" | custom-call | flops 37748736 | bytes 917504 | tf_op jit(solution)/shard_map/first_rows/pallas_call | solution.py:407
  14.9 0.4 %collective-permute-start.7 = (f32[96,256]{1,0:T(8,128)S(1)}, f32[96,256]{1,0:T(8,128)S(1)}, u32[]{:S(2)}, u32[]{:S(2)}) collective-permute-start(f32[96,256]{1,0:T(8,128)S(1)} %get-tuple-element.30.refs_0_), channel_id=1, source_target_pairs={{0,1},{2,3},{4,5},{6,7},{8,9},{10,11},{12,13},{14,15},{1,0},{3,2},... | collective-permute-start | bytes 294920 | tf_op jit(solution)/shard_map/ppermute | solution.py:325
  15.2 0.3 %second_rows.1.refs_1_ = f32[96,256]{1,0:T(8,128)S(1)} custom-call(bf16[192,256]{1,0:T(8,128)(2,1)S(1)} %get-tuple-element.27.swapped, bf16[192,512]{1,0:T(8,128)(2,1)S(1)} %get-tuple-element.28.diagonal, bf16[4,9,128,256]{3,2,1,0:T(8,128)(2,1)S(1)} %get-tuple-element.23.refs_0_, bf16[4,9,128,256]{3,2,1,0:T(8,128)(2,1)S(1)} %get-tuple-element.24.refs_1_, ...), custom_call_target="tpu_custom_call" | custom-call | flops 37748736 | bytes 917504 | tf_op jit(solution)/shard_map/second_rows/pallas_call | solution.py:422
  15.5 1.9 %collective-permute-start.6 = (f32[96,256]{1,0:T(8,128)S(1)}, f32[96,256]{1,0:T(8,128)S(1)}, u32[]{:S(2)}, u32[]{:S(2)}) collective-permute-start(f32[96,256]{1,0:T(8,128)S(1)} %second_rows.1.refs_1_), channel_id=1, source_target_pairs={{0,1},{2,3},{4,5},{6,7},{8,9},{10,11},{12,13},{14,15},{1,0},{3,2},... | collective-permute-start | bytes 294920 | tf_op jit(solution)/shard_map/ppermute | solution.py:327
  17.4 0.0 collective-permute-start.9
  17.4 3.1 %collective-permute-done.7.halo = f32[96,256]{1,0:T(8,128)S(1)} collective-permute-done((f32[96,256]{1,0:T(8,128)S(1)}, f32[96,256]{1,0:T(8,128)S(1)}, u32[]{:S(2)}, u32[]{:S(2)}) %collective-permute-start.7) | collective-permute-done | bytes 98336 | tf_op jit(solution)/shard_map/ppermute | solution.py:325
  20.6 2.5 %collective-permute-start.8 = (f32[96,256]{1,0:T(8,128)S(1)}, f32[96,256]{1,0:T(8,128)S(1)}, u32[]{:S(2)}, u32[]{:S(2)}) collective-permute-start(f32[96,256]{1,0:T(8,128)S(1)} %collective-permute-done.7.halo), channel_id=1, source_target_pairs={{0,2},{2,4},{4,6},{3,1},{5,3},{7,5},{6,7},{1,0},{8,10},{10,12},{12... | collective-permute-start | bytes 294920 | tf_op jit(solution)/shard_map/ppermute | solution.py:329
  23.1 2.7 %prepare.5 = (bf16[3,9,128,256]{3,2,1,0:T(8,128)(2,1)S(1)}, bf16[3,9,128,256]{3,2,1,0:T(8,128)(2,1)S(1)}, f32[3,96,256]{2,1,0:T(8,128)S(1)}) custom-call(s32[1,4,7]{2,1,0:T(4,128)} %own_cols.5, s32[1,4,7]{2,1,0:T(4,128)S(1)} %collective-permute-done.4.other_cols, f32[1,4,7,2,128,128]{5,4,3,2,1,0:T(8,128)} %own.5, ...), custom_call_target="tpu_custom_call" | custom-call | flops 75497472 | bytes 3670016 | tf_op jit(solution)/shard_map/prepare/pallas_call | solution.py:371
  25.8 1.6 %prepare.4 = (bf16[1,9,128,256]{3,2,1,0:T(8,128)(2,1)S(1)}, bf16[1,9,128,256]{3,2,1,0:T(8,128)(2,1)S(1)}, f32[1,96,256]{2,1,0:T(8,128)S(1)}) custom-call(s32[1,4,7]{2,1,0:T(4,128)} %own_cols.5, s32[1,4,7]{2,1,0:T(4,128)S(1)} %collective-permute-done.4.other_cols, f32[1,4,7,2,128,128]{5,4,3,2,1,0:T(8,128)} %own.5, ...), custom_call_target="tpu_custom_call" | custom-call | flops 75497472 | bytes 3670016 | tf_op jit(solution)/shard_map/prepare/pallas_call | solution.py:371
  27.5 0.3 %early.3.refs_4_ = f32[4,96,256]{2,1,0:T(8,128)S(1)} custom-call(f32[96,256]{1,0:T(8,128)S(1)} %collective-permute-done.7.halo, bf16[1,9,128,256]{3,2,1,0:T(8,128)(2,1)S(1)} %get-tuple-element.31.refs_0_, bf16[3,9,128,256]{3,2,1,0:T(8,128)(2,1)S(1)} %get-tuple-element.32.refs_1_, bf16[1,9,128,256]{3,2,1,0:T(8,128)(2,1)S(1)} %get-tuple-element.33.refs_2_, ...), custom_call_target="tpu_custom_call" | custom-call | flops 37748736 | bytes 917504 | tf_op jit(solution)/shard_map/early/pallas_call | solution.py:394
  27.8 0.0 collective-permute-done.6.swapped
  27.9 0.0 collective-permute-done.9.diagonal
  27.9 0.0 collective-permute-done.8.relayed
  27.9 1.2 %bottom.1 = f32[3,2,16,512]{3,2,1,0:T(8,128)} custom-call(f32[96,256]{1,0:T(8,128)S(1)} %collective-permute-done.6.swapped, f32[96,256]{1,0:T(8,128)S(1)} %collective-permute-done.8.relayed, f32[96,256]{1,0:T(8,128)S(1)} %collective-permute-done.9.diagonal, bf16[1,9,128,256]{3,2,1,0:T(8,128)(2,1)S(1)} %get-tuple-element.31.refs_0_, ...), custom_call_target="tpu_custom_call" | custom-call | flops 37748736 | bytes 917504 | tf_op jit(solution)/shard_map/bottom/pallas_call | solution.py:434
Async XLA Ops:
  0.0 10.7 %collective-permute-start.5 = (f32[1,4,7,2,128,128]{5,4,3,2,1,0:T(8,128)}, f32[1,4,7,2,128,128]{5,4,3,2,1,0:T(8,128)S(1)}, u32[]{:S(2)}, u32[]{:S(2)}) collective-permute-start(f32[1,4,7,2,128,128]{5,4,3,2,1,0:T(8,128)} %own.5), channel_id=1, source_target_pairs={{0,8},{8,0},{1,9},{9,1},{2,10},{10,2},{3,11},{11,3},{4,12},{12,4},... | collective-permute-start | bytes 11010056 | tf_op jit(solution)/shard_map/ppermute | solution.py:332
  1.4 6.0 %collective-permute-start.1 = (f32[96,256]{1,0:T(8,128)S(1)}, f32[96,256]{1,0:T(8,128)S(1)}, u32[]{:S(2)}, u32[]{:S(2)}) collective-permute-start(f32[96,256]{1,0:T(8,128)S(1)} %get-tuple-element.22.refs_0_), channel_id=1, source_target_pairs={{0,1},{2,3},{4,5},{6,7},{8,9},{10,11},{12,13},{14,15},{1,0},{3,2},... | collective-permute-start | bytes 294920 | tf_op jit(solution)/shard_map/ppermute | solution.py:325
  4.9 9.5 %collective-permute-start = (f32[96,256]{1,0:T(8,128)S(1)}, f32[96,256]{1,0:T(8,128)S(1)}, u32[]{:S(2)}, u32[]{:S(2)}) collective-permute-start(f32[96,256]{1,0:T(8,128)S(1)} %get-tuple-element.21.refs_1_), channel_id=1, source_target_pairs={{0,1},{2,3},{4,5},{6,7},{8,9},{10,11},{12,13},{14,15},{1,0},{3,2},... | collective-permute-start | bytes 294920 | tf_op jit(solution)/shard_map/ppermute | solution.py:327
  5.0 9.4 %collective-permute-start.3 = (f32[96,256]{1,0:T(8,128)S(1)}, f32[96,256]{1,0:T(8,128)S(1)}, u32[]{:S(2)}, u32[]{:S(2)}) collective-permute-start(f32[96,256]{1,0:T(8,128)S(1)} %get-tuple-element.21.refs_1_), channel_id=1, source_target_pairs={{1,2},{3,4},{5,6},{9,10},{11,12},{13,14},{0,8},{7,15},{2,1},{4,3},... | collective-permute-start | bytes 294920 | tf_op jit(solution)/shard_map/ppermute | solution.py:328
  7.5 7.0 %collective-permute-start.2 = (f32[96,256]{1,0:T(8,128)S(1)}, f32[96,256]{1,0:T(8,128)S(1)}, u32[]{:S(2)}, u32[]{:S(2)}) collective-permute-start(f32[96,256]{1,0:T(8,128)S(1)} %collective-permute-done.1.halo), channel_id=1, source_target_pairs={{0,2},{2,4},{4,6},{3,1},{5,3},{7,5},{6,7},{1,0},{8,10},{10,12},{12... | collective-permute-start | bytes 294920 | tf_op jit(solution)/shard_map/ppermute | solution.py:329
  9.3 1.4 %collective-permute-start.4 = (s32[1,4,7]{2,1,0:T(4,128)}, s32[1,4,7]{2,1,0:T(4,128)S(1)}, u32[]{:S(2)}, u32[]{:S(2)}) collective-permute-start(s32[1,4,7]{2,1,0:T(4,128)} %own_cols.5), channel_id=1, source_target_pairs={{0,8},{8,0},{1,9},{9,1},{2,10},{10,2},{3,11},{11,3},{4,12},{12,4},... | collective-permute-start | bytes 344 | tf_op jit(solution)/shard_map/ppermute | solution.py:333
  14.9 5.7 %collective-permute-start.7 = (f32[96,256]{1,0:T(8,128)S(1)}, f32[96,256]{1,0:T(8,128)S(1)}, u32[]{:S(2)}, u32[]{:S(2)}) collective-permute-start(f32[96,256]{1,0:T(8,128)S(1)} %get-tuple-element.30.refs_0_), channel_id=1, source_target_pairs={{0,1},{2,3},{4,5},{6,7},{8,9},{10,11},{12,13},{14,15},{1,0},{3,2},... | collective-permute-start | bytes 294920 | tf_op jit(solution)/shard_map/ppermute | solution.py:325
  15.5 12.3 %collective-permute-start.6 = (f32[96,256]{1,0:T(8,128)S(1)}, f32[96,256]{1,0:T(8,128)S(1)}, u32[]{:S(2)}, u32[]{:S(2)}) collective-permute-start(f32[96,256]{1,0:T(8,128)S(1)} %second_rows.1.refs_1_), channel_id=1, source_target_pairs={{0,1},{2,3},{4,5},{6,7},{8,9},{10,11},{12,13},{14,15},{1,0},{3,2},... | collective-permute-start | bytes 294920 | tf_op jit(solution)/shard_map/ppermute | solution.py:327
  17.4 10.4 %collective-permute-start.9 = (f32[96,256]{1,0:T(8,128)S(1)}, f32[96,256]{1,0:T(8,128)S(1)}, u32[]{:S(2)}, u32[]{:S(2)}) collective-permute-start(f32[96,256]{1,0:T(8,128)S(1)} %second_rows.1.refs_1_), channel_id=1, source_target_pairs={{1,2},{3,4},{5,6},{9,10},{11,12},{13,14},{0,8},{7,15},{2,1},{4,3},... | collective-permute-start | bytes 294920 | tf_op jit(solution)/shard_map/ppermute | solution.py:328
  20.6 7.3 %collective-permute-start.8 = (f32[96,256]{1,0:T(8,128)S(1)}, f32[96,256]{1,0:T(8,128)S(1)}, u32[]{:S(2)}, u32[]{:S(2)}) collective-permute-start(f32[96,256]{1,0:T(8,128)S(1)} %collective-permute-done.7.halo), channel_id=1, source_target_pairs={{0,2},{2,4},{4,6},{3,1},{5,3},{7,5},{6,7},{1,0},{8,10},{10,12},{12... | collective-permute-start | bytes 294920 | tf_op jit(solution)/shard_map/ppermute | solution.py:329

commit v5 on v4

--- a/solution.py
+++ b/solution.py
@@ -29,9 +29,9 @@
     return jnp.concatenate([re for re, _ in panels] + [im for _, im in panels], axis=0)
 
 
-def enter_kernel(
-    first, sources, refl_level, refl_coef, total, next_coef, held, level_held, coef_held, coef, sems
-):
+def enter_kernel(first, tables, sources, refl_level, refl_coef, *refs):
+    tables_in, (total, next_coef), refs = refs[:tables], refs[tables : tables + 2], refs[tables + 2 :]
+    tables_out, (held, level_held, coef_held, coef, sems) = refs[:tables], refs[tables:]
     lanes = pl.ds(first, total.shape[1])
     copies = [
         pltpu.make_async_copy(a, b, sems.at[i])
@@ -40,6 +40,7 @@
                 (sources.at[:, :, :, lanes], held),
                 (refl_level.at[:, lanes], level_held),
                 (refl_coef.at[:, lanes], coef_held),
+                *zip(tables_in, tables_out),
             )
         )
     ]
@@ -333,23 +334,27 @@
     other_cols = lax.ppermute(block_cols, "depth", over_depth)
     refl_level = refl_level.reshape(1, points)
 
-    def enter(rows):
+    def enter(rows, *tables):
         width = len(rows) * size
         return pl.pallas_call(
-            functools.partial(enter_kernel, rows[0] * size),
-            out_shape=[part_shape(rows), jax.ShapeDtypeStruct((2, width), f32)],
-            in_specs=[HBM] * 3,
-            out_specs=[VMEM] * 2,
+            functools.partial(enter_kernel, rows[0] * size, len(tables)),
+            out_shape=[
+                part_shape(rows),
+                jax.ShapeDtypeStruct((2, width), f32),
+                *(jax.ShapeDtypeStruct(table.shape, table.dtype) for table in tables),
+            ],
+            in_specs=[HBM] * (3 + len(tables)),
+            out_specs=[VMEM] * (2 + len(tables)),
             scratch_shapes=[
                 pltpu.VMEM((panels, 2, part, width), f32),
                 pltpu.VMEM((1, width), jnp.int32),
                 pltpu.VMEM((2, width), f32),
                 pltpu.VMEM((2, width), f32),
-                pltpu.SemaphoreType.DMA((3,)),
+                pltpu.SemaphoreType.DMA((3 + len(tables),)),
             ],
             compiler_params=params(4),
             name="enter",
-        )(in_hbm(sources), in_hbm(refl_level), in_hbm(refl_coef))
+        )(*map(in_hbm, (sources, refl_level, refl_coef, *tables)))
 
     coefs = []
 
@@ -358,7 +363,7 @@
         coefs.append(coef)
         return part_total
 
-    first_total, coef = enter(first_rows)
+    first_total, coef, own_cols = enter(first_rows, block_cols)
     coefs.append(coef)
     second_total, early, late = exchange(first_total, enter_second)
 
@@ -381,7 +386,7 @@
             compiler_params=params(16),
             cost_estimate=cost(2 * macs, 4 * blocks.size),
             name="prepare",
-        )(in_hbm(block_cols), other_cols, in_hbm(blocks), other_blocks, *fields)
+        )(own_cols, other_cols, in_hbm(blocks), other_blocks, *fields)
 
     every_row = range(block_rows)
     row_groups = ((every_row,), (every_row[:1], every_row[1:]))

time: 29.4 us -> 29 us (0.986)
  Pallas kernels: 12.3 us -> 12 us
    pallas_call x3, Pallas kernels: 7.79 us -> 7.5 us  [prepare(): pl.pallas_call(functools.partial(prepare_kernel, level, rows), out_shape=...]
  transfers between devices with their start and end apart: 10 -> 10, of which waited for: 3 -> 3; matrix products, arithmetic and copies ran while one was open for 0% -> 0% of each run, Pallas kernels for 37% -> 36%
where the time goes in v5:
time: 29 us; the launch traced here: 28.8 us
  Pallas kernels  12 us (41%)
  starting transfers between devices  10 us (34%)
  waiting for transfers between devices  6.67 us (23%)
    pallas_call x3, Pallas kernels, prepare(): pl.pallas_call(functools.partial(prepare_kernel, level, rows), out_shape=...  7.5 us
    ppermute x2, waiting for transfers between devices, exchange(): first_swapped = lax.ppermute(first, axes, beside)  5.29 us
    ppermute x2, starting transfers between devices, exchange(): relayed = lax.ppermute(first_swapped, axes, onward)  4.36 us
    ppermute x2, starting transfers between devices, exchange(): first_swapped = lax.ppermute(first, axes, beside)  2.89 us
    ppermute x2, starting transfers between devices, exchange(): second_swapped = lax.ppermute(second, axes, beside)  1.99 us
    pallas_call x2, Pallas kernels, enter(): pl.pallas_call(functools.partial(enter_kernel, rows[0] * size, len(tables...  1.9 us
    ppermute x1, waiting for transfers between devices, per_device(): other_cols = lax.ppermute(block_cols, 'depth', over_depth)  1.37 us
    pallas_call x1, Pallas kernels, per_device(): pl.pallas_call(functools.partial(bottom_kernel, len(row_groups[1])), out_...  1.21 us
  transfers between devices with their start and end apart: 10, of which 3 were waited for; matrix products, arithmetic and copies ran while one was open for 0% of the time, Pallas kernels for 36%

profile of v5, /device:TPU:0, one launch (start us, length us, event | category | flops | bytes accessed | tf_op | source)
XLA Modules:
  0.0 28.8 jit_solution(3399986809878619749)
XLA Ops:
  0.0 0.5 %collective-permute-start.5 = (f32[1,4,7,2,128,128]{5,4,3,2,1,0:T(8,128)}, f32[1,4,7,2,128,128]{5,4,3,2,1,0:T(8,128)S(1)}, u32[]{:S(2)}, u32[]{:S(2)}) collective-permute-start(f32[1,4,7,2,128,128]{5,4,3,2,1,0:T(8,128)} %own.5), channel_id=1, source_target_pairs={{0,8},{8,0},{1,9},{9,1},{2,10},{10,2},{3,11},{11,3},{4,12},{12,4},... | collective-permute-start | bytes 11010056 | tf_op jit(solution)/shard_map/ppermute | solution.py:333
  0.5 1.0 %enter.3 = (f32[96,256]{1,0:T(8,128)S(1)}, f32[2,256]{1,0:T(2,128)S(1)}, s32[1,4,7]{2,1,0:T(4,128)S(1)}) custom-call(f32[3,2,16,512]{3,2,1,0:T(8,128)} %sources.3, s32[1,512]{1,0:T(1,128)} %bitcast.1, f32[2,512]{1,0:T(2,128)} %refl_coef.3, s32[1,4,7]{2,1,0:T(4,128)} %refs_0_.1), custom_call_target="tpu_custom_call" | custom-call | tf_op jit(solution)/shard_map/enter/pallas_call | solution.py:339
  1.5 2.5 %collective-permute-start.1 = (f32[96,256]{1,0:T(8,128)S(1)}, f32[96,256]{1,0:T(8,128)S(1)}, u32[]{:S(2)}, u32[]{:S(2)}) collective-permute-start(f32[96,256]{1,0:T(8,128)S(1)} %get-tuple-element.23.refs_0_), channel_id=1, source_target_pairs={{0,1},{2,3},{4,5},{6,7},{8,9},{10,11},{12,13},{14,15},{1,0},{3,2},... | collective-permute-start | bytes 294920 | tf_op jit(solution)/shard_map/ppermute | solution.py:326
  4.0 0.9 %enter.2 = (f32[96,256]{1,0:T(8,128)S(1)}, f32[2,256]{1,0:T(2,128)S(1)}) custom-call(f32[3,2,16,512]{3,2,1,0:T(8,128)} %sources.3, s32[1,512]{1,0:T(1,128)} %bitcast.2, f32[2,512]{1,0:T(2,128)} %refl_coef.3), custom_call_target="tpu_custom_call" | custom-call | tf_op jit(solution)/shard_map/enter/pallas_call | solution.py:339
  5.0 0.1 collective-permute-start
  5.0 0.3 collective-permute-start.3
  5.3 2.1 %collective-permute-done.1.halo = f32[96,256]{1,0:T(8,128)S(1)} collective-permute-done((f32[96,256]{1,0:T(8,128)S(1)}, f32[96,256]{1,0:T(8,128)S(1)}, u32[]{:S(2)}, u32[]{:S(2)}) %collective-permute-start.1) | collective-permute-done | bytes 98336 | tf_op jit(solution)/shard_map/ppermute | solution.py:326
  7.5 1.8 %collective-permute-start.2 = (f32[96,256]{1,0:T(8,128)S(1)}, f32[96,256]{1,0:T(8,128)S(1)}, u32[]{:S(2)}, u32[]{:S(2)}) collective-permute-start(f32[96,256]{1,0:T(8,128)S(1)} %collective-permute-done.1.halo), channel_id=1, source_target_pairs={{0,2},{2,4},{4,6},{3,1},{5,3},{7,5},{6,7},{1,0},{8,10},{10,12},{12... | collective-permute-start | bytes 294920 | tf_op jit(solution)/shard_map/ppermute | solution.py:330
  9.3 0.0 collective-permute-start.4
  9.3 1.4 %collective-permute-done.4.other_cols = s32[1,4,7]{2,1,0:T(4,128)S(1)} collective-permute-done((s32[1,4,7]{2,1,0:T(4,128)}, s32[1,4,7]{2,1,0:T(4,128)S(1)}, u32[]{:S(2)}, u32[]{:S(2)}) %collective-permute-start.4) | collective-permute-done | bytes 144 | tf_op jit(solution)/shard_map/ppermute | solution.py:334
  10.7 0.0 collective-permute-done.5.received
  10.7 3.3 %prepare.3 = (bf16[4,9,128,256]{3,2,1,0:T(8,128)(2,1)S(1)}, bf16[4,9,128,256]{3,2,1,0:T(8,128)(2,1)S(1)}, f32[4,96,256]{2,1,0:T(8,128)S(1)}) custom-call(s32[1,4,7]{2,1,0:T(4,128)S(1)} %get-tuple-element.24.own_cols, s32[1,4,7]{2,1,0:T(4,128)S(1)} %collective-permute-done.4.other_cols, f32[1,4,7,2,128,128]{5,4,3,2,1,0:T(8,128)} %own.5, ...), custom_call_target="tpu_custom_call" | custom-call | flops 75497472 | bytes 3670016 | tf_op jit(solution)/shard_map/prepare/pallas_call | solution.py:376
  14.0 0.3 %early.2.refs_2_ = f32[4,96,256]{2,1,0:T(8,128)S(1)} custom-call(f32[96,256]{1,0:T(8,128)S(1)} %collective-permute-done.1.halo, bf16[4,9,128,256]{3,2,1,0:T(8,128)(2,1)S(1)} %get-tuple-element.25.refs_0_, bf16[4,9,128,256]{3,2,1,0:T(8,128)(2,1)S(1)} %get-tuple-element.26.refs_1_, f32[4,96,256]{2,1,0:T(8,128)S(1)} %get-tuple-element.27.refs_2_), custom_call_target="tpu_custom_call" | custom-call | flops 37748736 | bytes 917504 | tf_op jit(solution)/shard_map/early/pallas_call | solution.py:399
  14.3 0.0 collective-permute-done.swapped
  14.4 0.0 collective-permute-done.3.diagonal
  14.4 0.0 collective-permute-done.2.relayed
  14.4 0.4 %first_rows.1 = (f32[96,256]{1,0:T(8,128)S(1)}, bf16[192,256]{1,0:T(8,128)(2,1)S(1)}, bf16[192,512]{1,0:T(8,128)(2,1)S(1)}) custom-call(f32[96,256]{1,0:T(8,128)S(1)} %collective-permute-done.swapped, f32[96,256]{1,0:T(8,128)S(1)} %collective-permute-done.2.relayed, f32[96,256]{1,0:T(8,128)S(1)} %collective-permute-done.3.diagonal, ...), custom_call_target="tpu_custom_call" | custom-call | flops 37748736 | bytes 917504 | tf_op jit(solution)/shard_map/first_rows/pallas_call | solution.py:412
  14.8 0.3 %collective-permute-start.7 = (f32[96,256]{1,0:T(8,128)S(1)}, f32[96,256]{1,0:T(8,128)S(1)}, u32[]{:S(2)}, u32[]{:S(2)}) collective-permute-start(f32[96,256]{1,0:T(8,128)S(1)} %get-tuple-element.32.refs_0_), channel_id=1, source_target_pairs={{0,1},{2,3},{4,5},{6,7},{8,9},{10,11},{12,13},{14,15},{1,0},{3,2},... | collective-permute-start | bytes 294920 | tf_op jit(solution)/shard_map/ppermute | solution.py:326
  15.1 0.3 %second_rows.1.refs_1_ = f32[96,256]{1,0:T(8,128)S(1)} custom-call(bf16[192,256]{1,0:T(8,128)(2,1)S(1)} %get-tuple-element.29.swapped, bf16[192,512]{1,0:T(8,128)(2,1)S(1)} %get-tuple-element.30.diagonal, bf16[4,9,128,256]{3,2,1,0:T(8,128)(2,1)S(1)} %get-tuple-element.25.refs_0_, bf16[4,9,128,256]{3,2,1,0:T(8,128)(2,1)S(1)} %get-tuple-element.26.refs_1_, ...), custom_call_target="tpu_custom_call" | custom-call | flops 37748736 | bytes 917504 | tf_op jit(solution)/shard_map/second_rows/pallas_call | solution.py:427
  15.4 1.9 %collective-permute-start.6 = (f32[96,256]{1,0:T(8,128)S(1)}, f32[96,256]{1,0:T(8,128)S(1)}, u32[]{:S(2)}, u32[]{:S(2)}) collective-permute-start(f32[96,256]{1,0:T(8,128)S(1)} %second_rows.1.refs_1_), channel_id=1, source_target_pairs={{0,1},{2,3},{4,5},{6,7},{8,9},{10,11},{12,13},{14,15},{1,0},{3,2},... | collective-permute-start | bytes 294920 | tf_op jit(solution)/shard_map/ppermute | solution.py:328
  17.4 0.0 collective-permute-start.9
  17.4 3.1 %collective-permute-done.7.halo = f32[96,256]{1,0:T(8,128)S(1)} collective-permute-done((f32[96,256]{1,0:T(8,128)S(1)}, f32[96,256]{1,0:T(8,128)S(1)}, u32[]{:S(2)}, u32[]{:S(2)}) %collective-permute-start.7) | collective-permute-done | bytes 98336 | tf_op jit(solution)/shard_map/ppermute | solution.py:326
  20.5 2.5 %collective-permute-start.8 = (f32[96,256]{1,0:T(8,128)S(1)}, f32[96,256]{1,0:T(8,128)S(1)}, u32[]{:S(2)}, u32[]{:S(2)}) collective-permute-start(f32[96,256]{1,0:T(8,128)S(1)} %collective-permute-done.7.halo), channel_id=1, source_target_pairs={{0,2},{2,4},{4,6},{3,1},{5,3},{7,5},{6,7},{1,0},{8,10},{10,12},{12... | collective-permute-start | bytes 294920 | tf_op jit(solution)/shard_map/ppermute | solution.py:330
  23.0 2.6 %prepare.5 = (bf16[3,9,128,256]{3,2,1,0:T(8,128)(2,1)S(1)}, bf16[3,9,128,256]{3,2,1,0:T(8,128)(2,1)S(1)}, f32[3,96,256]{2,1,0:T(8,128)S(1)}) custom-call(s32[1,4,7]{2,1,0:T(4,128)S(1)} %get-tuple-element.24.own_cols, s32[1,4,7]{2,1,0:T(4,128)S(1)} %collective-permute-done.4.other_cols, f32[1,4,7,2,128,128]{5,4,3,2,1,0:T(8,128)} %own.5, ...), custom_call_target="tpu_custom_call" | custom-call | flops 75497472 | bytes 3670016 | tf_op jit(solution)/shard_map/prepare/pallas_call | solution.py:376
  25.7 1.6 %prepare.4 = (bf16[1,9,128,256]{3,2,1,0:T(8,128)(2,1)S(1)}, bf16[1,9,128,256]{3,2,1,0:T(8,128)(2,1)S(1)}, f32[1,96,256]{2,1,0:T(8,128)S(1)}) custom-call(s32[1,4,7]{2,1,0:T(4,128)S(1)} %get-tuple-element.24.own_cols, s32[1,4,7]{2,1,0:T(4,128)S(1)} %collective-permute-done.4.other_cols, f32[1,4,7,2,128,128]{5,4,3,2,1,0:T(8,128)} %own.5, ...), custom_call_target="tpu_custom_call" | custom-call | flops 75497472 | bytes 3670016 | tf_op jit(solution)/shard_map/prepare/pallas_call | solution.py:376
  27.2 0.3 %early.3.refs_4_ = f32[4,96,256]{2,1,0:T(8,128)S(1)} custom-call(f32[96,256]{1,0:T(8,128)S(1)} %collective-permute-done.7.halo, bf16[1,9,128,256]{3,2,1,0:T(8,128)(2,1)S(1)} %get-tuple-element.33.refs_0_, bf16[3,9,128,256]{3,2,1,0:T(8,128)(2,1)S(1)} %get-tuple-element.34.refs_1_, bf16[1,9,128,256]{3,2,1,0:T(8,128)(2,1)S(1)} %get-tuple-element.35.refs_2_, ...), custom_call_target="tpu_custom_call" | custom-call | flops 37748736 | bytes 917504 | tf_op jit(solution)/shard_map/early/pallas_call | solution.py:399
  27.6 0.0 collective-permute-done.6.swapped
  27.6 0.0 collective-permute-done.9.diagonal
  27.6 0.0 collective-permute-done.8.relayed
  27.6 1.2 %bottom.1 = f32[3,2,16,512]{3,2,1,0:T(8,128)} custom-call(f32[96,256]{1,0:T(8,128)S(1)} %collective-permute-done.6.swapped, f32[96,256]{1,0:T(8,128)S(1)} %collective-permute-done.8.relayed, f32[96,256]{1,0:T(8,128)S(1)} %collective-permute-done.9.diagonal, bf16[1,9,128,256]{3,2,1,0:T(8,128)(2,1)S(1)} %get-tuple-element.33.refs_0_, ...), custom_call_target="tpu_custom_call" | custom-call | flops 37748736 | bytes 917504 | tf_op jit(solution)/shard_map/bottom/pallas_call | solution.py:439
Async XLA Ops:
  0.0 10.7 %collective-permute-start.5 = (f32[1,4,7,2,128,128]{5,4,3,2,1,0:T(8,128)}, f32[1,4,7,2,128,128]{5,4,3,2,1,0:T(8,128)S(1)}, u32[]{:S(2)}, u32[]{:S(2)}) collective-permute-start(f32[1,4,7,2,128,128]{5,4,3,2,1,0:T(8,128)} %own.5), channel_id=1, source_target_pairs={{0,8},{8,0},{1,9},{9,1},{2,10},{10,2},{3,11},{11,3},{4,12},{12,4},... | collective-permute-start | bytes 11010056 | tf_op jit(solution)/shard_map/ppermute | solution.py:333
  1.5 6.0 %collective-permute-start.1 = (f32[96,256]{1,0:T(8,128)S(1)}, f32[96,256]{1,0:T(8,128)S(1)}, u32[]{:S(2)}, u32[]{:S(2)}) collective-permute-start(f32[96,256]{1,0:T(8,128)S(1)} %get-tuple-element.23.refs_0_), channel_id=1, source_target_pairs={{0,1},{2,3},{4,5},{6,7},{8,9},{10,11},{12,13},{14,15},{1,0},{3,2},... | collective-permute-start | bytes 294920 | tf_op jit(solution)/shard_map/ppermute | solution.py:326
  5.0 9.4 %collective-permute-start = (f32[96,256]{1,0:T(8,128)S(1)}, f32[96,256]{1,0:T(8,128)S(1)}, u32[]{:S(2)}, u32[]{:S(2)}) collective-permute-start(f32[96,256]{1,0:T(8,128)S(1)} %get-tuple-element.22.refs_1_), channel_id=1, source_target_pairs={{0,1},{2,3},{4,5},{6,7},{8,9},{10,11},{12,13},{14,15},{1,0},{3,2},... | collective-permute-start | bytes 294920 | tf_op jit(solution)/shard_map/ppermute | solution.py:328
  5.0 9.3 %collective-permute-start.3 = (f32[96,256]{1,0:T(8,128)S(1)}, f32[96,256]{1,0:T(8,128)S(1)}, u32[]{:S(2)}, u32[]{:S(2)}) collective-permute-start(f32[96,256]{1,0:T(8,128)S(1)} %get-tuple-element.22.refs_1_), channel_id=1, source_target_pairs={{1,2},{3,4},{5,6},{9,10},{11,12},{13,14},{0,8},{7,15},{2,1},{4,3},... | collective-permute-start | bytes 294920 | tf_op jit(solution)/shard_map/ppermute | solution.py:329
  7.5 6.9 %collective-permute-start.2 = (f32[96,256]{1,0:T(8,128)S(1)}, f32[96,256]{1,0:T(8,128)S(1)}, u32[]{:S(2)}, u32[]{:S(2)}) collective-permute-start(f32[96,256]{1,0:T(8,128)S(1)} %collective-permute-done.1.halo), channel_id=1, source_target_pairs={{0,2},{2,4},{4,6},{3,1},{5,3},{7,5},{6,7},{1,0},{8,10},{10,12},{12... | collective-permute-start | bytes 294920 | tf_op jit(solution)/shard_map/ppermute | solution.py:330
  9.3 1.4 %collective-permute-start.4 = (s32[1,4,7]{2,1,0:T(4,128)}, s32[1,4,7]{2,1,0:T(4,128)S(1)}, u32[]{:S(2)}, u32[]{:S(2)}) collective-permute-start(s32[1,4,7]{2,1,0:T(4,128)} %refs_0_.1), channel_id=1, source_target_pairs={{0,8},{8,0},{1,9},{9,1},{2,10},{10,2},{3,11},{11,3},{4,12},{12,4},... | collective-permute-start | bytes 344 | tf_op jit(solution)/shard_map/ppermute | solution.py:334
  14.8 5.7 %collective-permute-start.7 = (f32[96,256]{1,0:T(8,128)S(1)}, f32[96,256]{1,0:T(8,128)S(1)}, u32[]{:S(2)}, u32[]{:S(2)}) collective-permute-start(f32[96,256]{1,0:T(8,128)S(1)} %get-tuple-element.32.refs_0_), channel_id=1, source_target_pairs={{0,1},{2,3},{4,5},{6,7},{8,9},{10,11},{12,13},{14,15},{1,0},{3,2},... | collective-permute-start | bytes 294920 | tf_op jit(solution)/shard_map/ppermute | solution.py:326
  15.4 12.1 %collective-permute-start.6 = (f32[96,256]{1,0:T(8,128)S(1)}, f32[96,256]{1,0:T(8,128)S(1)}, u32[]{:S(2)}, u32[]{:S(2)}) collective-permute-start(f32[96,256]{1,0:T(8,128)S(1)} %second_rows.1.refs_1_), channel_id=1, source_target_pairs={{0,1},{2,3},{4,5},{6,7},{8,9},{10,11},{12,13},{14,15},{1,0},{3,2},... | collective-permute-start | bytes 294920 | tf_op jit(solution)/shard_map/ppermute | solution.py:328
  17.4 10.2 %collective-permute-start.9 = (f32[96,256]{1,0:T(8,128)S(1)}, f32[96,256]{1,0:T(8,128)S(1)}, u32[]{:S(2)}, u32[]{:S(2)}) collective-permute-start(f32[96,256]{1,0:T(8,128)S(1)} %second_rows.1.refs_1_), channel_id=1, source_target_pairs={{1,2},{3,4},{5,6},{9,10},{11,12},{13,14},{0,8},{7,15},{2,1},{4,3},... | collective-permute-start | bytes 294920 | tf_op jit(solution)/shard_map/ppermute | solution.py:329
  20.5 7.1 %collective-permute-start.8 = (f32[96,256]{1,0:T(8,128)S(1)}, f32[96,256]{1,0:T(8,128)S(1)}, u32[]{:S(2)}, u32[]{:S(2)}) collective-permute-start(f32[96,256]{1,0:T(8,128)S(1)} %collective-permute-done.7.halo), channel_id=1, source_target_pairs={{0,2},{2,4},{4,6},{3,1},{5,3},{7,5},{6,7},{1,0},{8,10},{10,12},{12... | collective-permute-start | bytes 294920 | tf_op jit(solution)/shard_map/ppermute | solution.py:330

commit v6 on v5

--- a/solution.py
+++ b/solution.py
@@ -71,8 +71,13 @@
     return both[:rows] + both[rows:] + cross
 
 
-def prepare_kernel(level, rows, own_cols, other_cols, own, received, *refs):
-    fields, (high, low, sums, held, left, sems) = refs[:-6], refs[-6:]
+def prepare_kernel(level, rows, halos, done, own_cols, other_cols, own, received, *refs):
+    outs = len(refs) - 6 - halos
+    high, low, sums, held, left, *early, sems = refs[outs:]
+    fields, refs = refs[: outs - halos - 3 * done], refs[outs - halos - 3 * done : outs]
+    halo, refs = refs[:halos], refs[halos:]
+    parts = refs[2 * done :]
+    bands = Bands(done + 1, (*refs[:done], high, *refs[done : 2 * done], low))
     per_row, size = held.shape[1], held.shape[3]
     block_rows = own.shape[1]
     here = lax.axis_index("depth") == level
@@ -107,13 +112,13 @@
         rows_at.append(at)
         rows_repeated.append(repeated)
         absent = (1 << span) - 1 - present
-        if span - per_row == 2:
-            clear(i, sum(jnp.where(absent % (2 << o) == 0, 1, 0) for o in range(span - 1)))
-            clear(i, sum(jnp.where(absent >= (2 << o), 1, 0) for o in range(span - 1)))
-        else:
-            repeated = True
-
-        @pl.when(repeated)
+        lowest = sum(jnp.where(absent % (2 << o) == 0, 1, 0) for o in range(span - 1))
+        highest = sum(jnp.where(absent >= (2 << o), 1, 0) for o in range(span - 1))
+        clear(i, lowest)
+        clear(i, highest)
+        between = repeated if span - per_row == 2 else True
+
+        @pl.when(between)
         def _():
             def clear_one(o, carry):
                 @pl.when(jnp.bitwise_and(jnp.right_shift(absent, o), 1) == 1)
@@ -122,7 +127,7 @@
 
                 return carry
 
-            lax.fori_loop(0, span, clear_one, 0)
+            lax.fori_loop(lowest + 1, highest, clear_one, 0)
 
     at_lane = 0
     for field in fields:
@@ -153,10 +158,20 @@
                 low[i, at[j], part] = tail
             return carry
 
-        lax.fori_loop(0, size // 16, split, 0)
+        lax.fori_loop(0, size // 16, split, 0, unroll=2)
+    finished = block_rows - len(rows) if halos else 0
     for i, b in enumerate(rows):
         band = slice(block_rows - b, 2 * block_rows - b)
-        sums[i] = product(left[...], high[i, band], low[i, band])
+        sums[finished + i] = product(left[...], high[i, band], low[i, band])
+    if halos:
+        early[0][...] = pieces(halo[0][...])
+
+        def run(swapped_before):
+            for b, (n, i) in enumerate(bands.rows):
+                before = parts[n][i] if n < done else sums[b]
+                sums[b] = before + side_product(b, 0, early[0], swapped_before, bands)
+
+        by_side(run)
 
 
 class Bands:
@@ -188,17 +203,6 @@
     even = lax.axis_index("lat") % 2 == 0
     pl.when(even)(functools.partial(run, False))
     pl.when(jnp.logical_not(even))(functools.partial(run, True))
-
-
-def early_kernel(groups, halo, *refs):
-    bands, parts, (out, left) = Bands(groups, refs), refs[2 * groups : -2], refs[-2:]
-    left[...] = pieces(halo[...])
-
-    def run(swapped_before):
-        for b, (n, i) in enumerate(bands.rows):
-            out[b] = parts[n][i] + side_product(b, 0, left, swapped_before, bands)
-
-    by_side(run)
 
 
 def late_products(rows, swapped, diagonal, bands, sums, finish):
@@ -367,46 +371,42 @@
     coefs.append(coef)
     second_total, early, late = exchange(first_total, enter_second)
 
-    sums_shape = jax.ShapeDtypeStruct((block_rows, 2 * channels, 2 * size), f32)
     macs = 6 * channels * points * 2 * size
 
-    def prepare(level, rows, *fields):
+    every_row = range(block_rows)
+    row_groups = ((every_row,), (every_row[:1], every_row[1:]))
+
+    def prepare(level, rows, fields, halo, ready):
         band = jax.ShapeDtypeStruct((len(rows), 2 * block_rows + 1, size, 2 * size), bf16)
-        sums = jax.ShapeDtypeStruct((len(rows), 2 * channels, 2 * size), f32)
+        sums_rows = block_rows if halo else len(rows)
+        sums = jax.ShapeDtypeStruct((sums_rows, 2 * channels, 2 * size), f32)
+        operands = (*fields, *halo, *(array for arrays in zip(*ready) for array in arrays))
         return pl.pallas_call(
-            functools.partial(prepare_kernel, level, rows),
+            functools.partial(prepare_kernel, level, rows, len(halo), len(ready)),
             out_shape=[band, band, sums],
-            in_specs=[SMEM, SMEM, HBM, HBM] + [VMEM] * len(fields),
+            in_specs=[SMEM, SMEM, HBM, HBM] + [VMEM] * len(operands),
             out_specs=[VMEM] * 3,
             scratch_shapes=[
                 pltpu.VMEM((len(rows),) + blocks.shape[2:], f32),
                 pltpu.VMEM((4 * channels, points), bf16),
+                *[pltpu.VMEM(*piece_shape(first_rows))] * len(halo),
                 pltpu.SemaphoreType.DMA((len(rows),)),
             ],
             compiler_params=params(16),
             cost_estimate=cost(2 * macs, 4 * blocks.size),
             name="prepare",
-        )(own_cols, other_cols, in_hbm(blocks), other_blocks, *fields)
-
-    every_row = range(block_rows)
-    row_groups = ((every_row,), (every_row[:1], every_row[1:]))
+        )(own_cols, other_cols, in_hbm(blocks), other_blocks, *operands)
 
     def early_products(level, halo, *fields):
         ready = []
-        for rows in row_groups[level]:
-            ready.append(prepare(level, rows, *fields))
+        for n, rows in enumerate(row_groups[level]):
+            is_last = n + 1 == len(row_groups[level])
+            prepared = prepare(
+                level, rows, fields, (halo,) if is_last else (), ready if is_last else []
+            )
+            ready.append(prepared)
         high, low, parts = zip(*ready)
-        sums = pl.pallas_call(
-            functools.partial(early_kernel, len(ready)),
-            out_shape=sums_shape,
-            in_specs=[VMEM] * (1 + 3 * len(ready)),
-            out_specs=VMEM,
-            scratch_shapes=[pltpu.VMEM(*piece_shape(first_rows))],
-            compiler_params=params(12),
-            cost_estimate=cost(macs, blocks.size),
-            name="early",
-        )(halo, *high, *low, *parts)
-        return *high, *low, sums
+        return *high, *low, parts[-1]
 
     bands = early_products(0, early, first_total, second_total)
     first_part, swapped_left, diagonal_left = pl.pallas_call(

time: 29 us -> 29.9 us (1.031)
  starting transfers between devices: 10 us -> 14.4 us
  waiting for transfers between devices: 6.67 us -> 3.59 us
  Pallas kernels: 12 us -> 11.6 us
    ppermute x2, starting transfers between devices: 1.99 us -> 5.48 us  [exchange(): second_swapped = lax.ppermute(second, axes, beside)]
    ppermute x2, waiting for transfers between devices: 5.29 us -> 2.2 us  [exchange(): first_swapped = lax.ppermute(first, axes, beside)]
    ppermute x2, starting transfers between devices: 4.36 us -> 5.07 us  [exchange(): relayed = lax.ppermute(first_swapped, axes, onward)]
    pallas_call x5 -> x3, Pallas kernels: 8.17 us -> 7.77 us  [prepare(): pl.pallas_call(functools.partial(prepare_kernel, level, rows, len(halo),...]
  transfers between devices with their start and end apart: 10 -> 10, of which waited for: 3 -> 2; matrix products, arithmetic and copies ran while one was open for 0% -> 0% of each run, Pallas kernels for 36% -> 34%
where the time goes in v6:
time: 29.9 us; the launch traced here: 29.7 us
  starting transfers between devices  14.4 us (48%)
  Pallas kernels  11.6 us (39%)
  waiting for transfers between devices  3.59 us (12%)
    pallas_call x3, Pallas kernels, prepare(): pl.pallas_call(functools.partial(prepare_kernel, level, rows, len(halo),...  7.77 us
    ppermute x2, starting transfers between devices, exchange(): second_swapped = lax.ppermute(second, axes, beside)  5.48 us
    ppermute x2, starting transfers between devices, exchange(): relayed = lax.ppermute(first_swapped, axes, onward)  5.07 us
    ppermute x2, starting transfers between devices, exchange(): first_swapped = lax.ppermute(first, axes, beside)  3 us
    ppermute x2, waiting for transfers between devices, exchange(): first_swapped = lax.ppermute(first, axes, beside)  2.2 us
    pallas_call x2, Pallas kernels, enter(): pl.pallas_call(functools.partial(enter_kernel, rows[0] * size, len(tables...  1.9 us
    ppermute x1, waiting for transfers between devices, per_device(): other_cols = lax.ppermute(block_cols, 'depth', over_depth)  1.37 us
    pallas_call x1, Pallas kernels, per_device(): pl.pallas_call(functools.partial(bottom_kernel, len(row_groups[1])), out_...  1.2 us
  transfers between devices with their start and end apart: 10, of which 2 were waited for; matrix products, arithmetic and copies ran while one was open for 0% of the time, Pallas kernels for 34%

profile of v6, /device:TPU:0, one launch (start us, length us, event | category | flops | bytes accessed | tf_op | source)
XLA Modules:
  0.0 29.7 jit_solution(1245740046632912072)
XLA Ops:
  0.0 0.5 %collective-permute-start.5 = (f32[1,4,7,2,128,128]{5,4,3,2,1,0:T(8,128)}, f32[1,4,7,2,128,128]{5,4,3,2,1,0:T(8,128)S(1)}, u32[]{:S(2)}, u32[]{:S(2)}) collective-permute-start(f32[1,4,7,2,128,128]{5,4,3,2,1,0:T(8,128)} %own.5), channel_id=1, source_target_pairs={{0,8},{8,0},{1,9},{9,1},{2,10},{10,2},{3,11},{11,3},{4,12},{12,4},... | collective-permute-start | bytes 11010056 | tf_op jit(solution)/shard_map/ppermute | solution.py:337
  0.5 1.0 %enter.3 = (f32[96,256]{1,0:T(8,128)S(1)}, f32[2,256]{1,0:T(2,128)S(1)}, s32[1,4,7]{2,1,0:T(4,128)S(1)}) custom-call(f32[3,2,16,512]{3,2,1,0:T(8,128)} %sources.3, s32[1,512]{1,0:T(1,128)} %bitcast.1, f32[2,512]{1,0:T(2,128)} %refl_coef.3, s32[1,4,7]{2,1,0:T(4,128)} %refs_0_.1), custom_call_target="tpu_custom_call" | custom-call | tf_op jit(solution)/shard_map/enter/pallas_call | solution.py:343
  1.5 2.5 %collective-permute-start.1 = (f32[96,256]{1,0:T(8,128)S(1)}, f32[96,256]{1,0:T(8,128)S(1)}, u32[]{:S(2)}, u32[]{:S(2)}) collective-permute-start(f32[96,256]{1,0:T(8,128)S(1)} %get-tuple-element.23.refs_0_), channel_id=1, source_target_pairs={{0,1},{2,3},{4,5},{6,7},{8,9},{10,11},{12,13},{14,15},{1,0},{3,2},... | collective-permute-start | bytes 294920 | tf_op jit(solution)/shard_map/ppermute | solution.py:330
  4.0 0.9 %enter.2 = (f32[96,256]{1,0:T(8,128)S(1)}, f32[2,256]{1,0:T(2,128)S(1)}) custom-call(f32[3,2,16,512]{3,2,1,0:T(8,128)} %sources.3, s32[1,512]{1,0:T(1,128)} %bitcast.2, f32[2,512]{1,0:T(2,128)} %refl_coef.3), custom_call_target="tpu_custom_call" | custom-call | tf_op jit(solution)/shard_map/enter/pallas_call | solution.py:343
  5.0 0.3 collective-permute-start.3
  5.2 2.8 %collective-permute-start = (f32[96,256]{1,0:T(8,128)S(1)}, f32[96,256]{1,0:T(8,128)S(1)}, u32[]{:S(2)}, u32[]{:S(2)}) collective-permute-start(f32[96,256]{1,0:T(8,128)S(1)} %get-tuple-element.22.refs_1_), channel_id=1, source_target_pairs={{0,1},{2,3},{4,5},{6,7},{8,9},{10,11},{12,13},{14,15},{1,0},{3,2},... | collective-permute-start | bytes 294920 | tf_op jit(solution)/shard_map/ppermute | solution.py:332
  8.1 0.0 collective-permute-done.1.refs_2_
  8.1 1.6 %collective-permute-start.2 = (f32[96,256]{1,0:T(8,128)S(1)}, f32[96,256]{1,0:T(8,128)S(1)}, u32[]{:S(2)}, u32[]{:S(2)}) collective-permute-start(f32[96,256]{1,0:T(8,128)S(1)} %collective-permute-done.1.refs_2_), channel_id=1, source_target_pairs={{0,2},{2,4},{4,6},{3,1},{5,3},{7,5},{6,7},{1,0},{8,10},{10,12},{12... | collective-permute-start | bytes 294920 | tf_op jit(solution)/shard_map/ppermute | solution.py:334
  9.6 0.0 collective-permute-start.4
  9.6 1.4 %collective-permute-done.4.other_cols = s32[1,4,7]{2,1,0:T(4,128)S(1)} collective-permute-done((s32[1,4,7]{2,1,0:T(4,128)}, s32[1,4,7]{2,1,0:T(4,128)S(1)}, u32[]{:S(2)}, u32[]{:S(2)}) %collective-permute-start.4) | collective-permute-done | bytes 144 | tf_op jit(solution)/shard_map/ppermute | solution.py:338
  11.0 0.0 collective-permute-done.5.received
  11.0 3.6 %prepare.3 = (bf16[4,9,128,256]{3,2,1,0:T(8,128)(2,1)S(1)}, bf16[4,9,128,256]{3,2,1,0:T(8,128)(2,1)S(1)}, f32[4,96,256]{2,1,0:T(8,128)S(1)}) custom-call(s32[1,4,7]{2,1,0:T(4,128)S(1)} %get-tuple-element.24.own_cols, s32[1,4,7]{2,1,0:T(4,128)S(1)} %collective-permute-done.4.other_cols, f32[1,4,7,2,128,128]{5,4,3,2,1,0:T(8,128)} %own.5, ...), custom_call_target="tpu_custom_call" | custom-call | flops 75497472 | bytes 3670016 | tf_op jit(solution)/shard_map/prepare/pallas_call | solution.py:384
  14.6 0.0 collective-permute-done.3.diagonal
  14.6 0.0 collective-permute-done.swapped
  14.6 0.0 collective-permute-done.2.relayed
  14.6 0.4 %first_rows.1 = (f32[96,256]{1,0:T(8,128)S(1)}, bf16[192,256]{1,0:T(8,128)(2,1)S(1)}, bf16[192,512]{1,0:T(8,128)(2,1)S(1)}) custom-call(f32[96,256]{1,0:T(8,128)S(1)} %collective-permute-done.swapped, f32[96,256]{1,0:T(8,128)S(1)} %collective-permute-done.2.relayed, f32[96,256]{1,0:T(8,128)S(1)} %collective-permute-done.3.diagonal, ...), custom_call_target="tpu_custom_call" | custom-call | flops 37748736 | bytes 917504 | tf_op jit(solution)/shard_map/first_rows/pallas_call | solution.py:412
  15.0 0.5 %collective-permute-start.7 = (f32[96,256]{1,0:T(8,128)S(1)}, f32[96,256]{1,0:T(8,128)S(1)}, u32[]{:S(2)}, u32[]{:S(2)}) collective-permute-start(f32[96,256]{1,0:T(8,128)S(1)} %get-tuple-element.32.refs_0_), channel_id=1, source_target_pairs={{0,1},{2,3},{4,5},{6,7},{8,9},{10,11},{12,13},{14,15},{1,0},{3,2},... | collective-permute-start | bytes 294920 | tf_op jit(solution)/shard_map/ppermute | solution.py:330
  15.5 0.3 %second_rows.1.refs_1_ = f32[96,256]{1,0:T(8,128)S(1)} custom-call(bf16[192,256]{1,0:T(8,128)(2,1)S(1)} %get-tuple-element.29.swapped, bf16[192,512]{1,0:T(8,128)(2,1)S(1)} %get-tuple-element.30.diagonal, bf16[4,9,128,256]{3,2,1,0:T(8,128)(2,1)S(1)} %get-tuple-element.25.refs_0_, bf16[4,9,128,256]{3,2,1,0:T(8,128)(2,1)S(1)} %get-tuple-element.26.refs_1_, ...), custom_call_target="tpu_custom_call" | custom-call | flops 37748736 | bytes 917504 | tf_op jit(solution)/shard_map/second_rows/pallas_call | solution.py:427
  15.8 0.1 collective-permute-start.9
  15.9 2.7 %collective-permute-start.6 = (f32[96,256]{1,0:T(8,128)S(1)}, f32[96,256]{1,0:T(8,128)S(1)}, u32[]{:S(2)}, u32[]{:S(2)}) collective-permute-start(f32[96,256]{1,0:T(8,128)S(1)} %second_rows.1.refs_1_), channel_id=1, source_target_pairs={{0,1},{2,3},{4,5},{6,7},{8,9},{10,11},{12,13},{14,15},{1,0},{3,2},... | collective-permute-start | bytes 294920 | tf_op jit(solution)/shard_map/ppermute | solution.py:332
  18.6 2.2 %collective-permute-done.7.refs_2_ = f32[96,256]{1,0:T(8,128)S(1)} collective-permute-done((f32[96,256]{1,0:T(8,128)S(1)}, f32[96,256]{1,0:T(8,128)S(1)}, u32[]{:S(2)}, u32[]{:S(2)}) %collective-permute-start.7) | collective-permute-done | bytes 98336 | tf_op jit(solution)/shard_map/ppermute | solution.py:330
  20.8 3.5 %collective-permute-start.8 = (f32[96,256]{1,0:T(8,128)S(1)}, f32[96,256]{1,0:T(8,128)S(1)}, u32[]{:S(2)}, u32[]{:S(2)}) collective-permute-start(f32[96,256]{1,0:T(8,128)S(1)} %collective-permute-done.7.refs_2_), channel_id=1, source_target_pairs={{0,2},{2,4},{4,6},{3,1},{5,3},{7,5},{6,7},{1,0},{8,10},{10,12},{12... | collective-permute-start | bytes 294920 | tf_op jit(solution)/shard_map/ppermute | solution.py:334
  24.3 1.4 %prepare.4 = (bf16[1,9,128,256]{3,2,1,0:T(8,128)(2,1)S(1)}, bf16[1,9,128,256]{3,2,1,0:T(8,128)(2,1)S(1)}, f32[1,96,256]{2,1,0:T(8,128)S(1)}) custom-call(s32[1,4,7]{2,1,0:T(4,128)S(1)} %get-tuple-element.24.own_cols, s32[1,4,7]{2,1,0:T(4,128)S(1)} %collective-permute-done.4.other_cols, f32[1,4,7,2,128,128]{5,4,3,2,1,0:T(8,128)} %own.5, ...), custom_call_target="tpu_custom_call" | custom-call | flops 75497472 | bytes 3670016 | tf_op jit(solution)/shard_map/prepare/pallas_call | solution.py:384
  25.7 2.7 %prepare.5 = (bf16[3,9,128,256]{3,2,1,0:T(8,128)(2,1)S(1)}, bf16[3,9,128,256]{3,2,1,0:T(8,128)(2,1)S(1)}, f32[4,96,256]{2,1,0:T(8,128)S(1)}) custom-call(s32[1,4,7]{2,1,0:T(4,128)S(1)} %get-tuple-element.24.own_cols, s32[1,4,7]{2,1,0:T(4,128)S(1)} %collective-permute-done.4.other_cols, f32[1,4,7,2,128,128]{5,4,3,2,1,0:T(8,128)} %own.5, ...), custom_call_target="tpu_custom_call" | custom-call | flops 75497472 | bytes 3670016 | tf_op jit(solution)/shard_map/prepare/pallas_call | solution.py:384
  28.5 0.0 collective-permute-done.9.diagonal
  28.5 0.0 collective-permute-done.6.swapped
  28.5 0.0 collective-permute-done.8.relayed
  28.5 1.2 %bottom.1 = f32[3,2,16,512]{3,2,1,0:T(8,128)} custom-call(f32[96,256]{1,0:T(8,128)S(1)} %collective-permute-done.6.swapped, f32[96,256]{1,0:T(8,128)S(1)} %collective-permute-done.8.relayed, f32[96,256]{1,0:T(8,128)S(1)} %collective-permute-done.9.diagonal, bf16[1,9,128,256]{3,2,1,0:T(8,128)(2,1)S(1)} %get-tuple-element.33.refs_3_.refs_0_, ...), custom_call_target="tpu_custom_call" | custom-call | flops 37748736 | bytes 917504 | tf_op jit(solution)/shard_map/bottom/pallas_call | solution.py:439
Async XLA Ops:
  0.0 11.0 %collective-permute-start.5 = (f32[1,4,7,2,128,128]{5,4,3,2,1,0:T(8,128)}, f32[1,4,7,2,128,128]{5,4,3,2,1,0:T(8,128)S(1)}, u32[]{:S(2)}, u32[]{:S(2)}) collective-permute-start(f32[1,4,7,2,128,128]{5,4,3,2,1,0:T(8,128)} %own.5), channel_id=1, source_target_pairs={{0,8},{8,0},{1,9},{9,1},{2,10},{10,2},{3,11},{11,3},{4,12},{12,4},... | collective-permute-start | bytes 11010056 | tf_op jit(solution)/shard_map/ppermute | solution.py:337
  1.5 6.6 %collective-permute-start.1 = (f32[96,256]{1,0:T(8,128)S(1)}, f32[96,256]{1,0:T(8,128)S(1)}, u32[]{:S(2)}, u32[]{:S(2)}) collective-permute-start(f32[96,256]{1,0:T(8,128)S(1)} %get-tuple-element.23.refs_0_), channel_id=1, source_target_pairs={{0,1},{2,3},{4,5},{6,7},{8,9},{10,11},{12,13},{14,15},{1,0},{3,2},... | collective-permute-start | bytes 294920 | tf_op jit(solution)/shard_map/ppermute | solution.py:330
  5.0 9.7 %collective-permute-start.3 = (f32[96,256]{1,0:T(8,128)S(1)}, f32[96,256]{1,0:T(8,128)S(1)}, u32[]{:S(2)}, u32[]{:S(2)}) collective-permute-start(f32[96,256]{1,0:T(8,128)S(1)} %get-tuple-element.22.refs_1_), channel_id=1, source_target_pairs={{1,2},{3,4},{5,6},{9,10},{11,12},{13,14},{0,8},{7,15},{2,1},{4,3},... | collective-permute-start | bytes 294920 | tf_op jit(solution)/shard_map/ppermute | solution.py:333
  5.2 9.4 %collective-permute-start = (f32[96,256]{1,0:T(8,128)S(1)}, f32[96,256]{1,0:T(8,128)S(1)}, u32[]{:S(2)}, u32[]{:S(2)}) collective-permute-start(f32[96,256]{1,0:T(8,128)S(1)} %get-tuple-element.22.refs_1_), channel_id=1, source_target_pairs={{0,1},{2,3},{4,5},{6,7},{8,9},{10,11},{12,13},{14,15},{1,0},{3,2},... | collective-permute-start | bytes 294920 | tf_op jit(solution)/shard_map/ppermute | solution.py:332
  8.1 6.6 %collective-permute-start.2 = (f32[96,256]{1,0:T(8,128)S(1)}, f32[96,256]{1,0:T(8,128)S(1)}, u32[]{:S(2)}, u32[]{:S(2)}) collective-permute-start(f32[96,256]{1,0:T(8,128)S(1)} %collective-permute-done.1.refs_2_), channel_id=1, source_target_pairs={{0,2},{2,4},{4,6},{3,1},{5,3},{7,5},{6,7},{1,0},{8,10},{10,12},{12... | collective-permute-start | bytes 294920 | tf_op jit(solution)/shard_map/ppermute | solution.py:334
  9.6 1.4 %collective-permute-start.4 = (s32[1,4,7]{2,1,0:T(4,128)}, s32[1,4,7]{2,1,0:T(4,128)S(1)}, u32[]{:S(2)}, u32[]{:S(2)}) collective-permute-start(s32[1,4,7]{2,1,0:T(4,128)} %refs_0_.1), channel_id=1, source_target_pairs={{0,8},{8,0},{1,9},{9,1},{2,10},{10,2},{3,11},{11,3},{4,12},{12,4},... | collective-permute-start | bytes 344 | tf_op jit(solution)/shard_map/ppermute | solution.py:338
  15.0 5.7 %collective-permute-start.7 = (f32[96,256]{1,0:T(8,128)S(1)}, f32[96,256]{1,0:T(8,128)S(1)}, u32[]{:S(2)}, u32[]{:S(2)}) collective-permute-start(f32[96,256]{1,0:T(8,128)S(1)} %get-tuple-element.32.refs_0_), channel_id=1, source_target_pairs={{0,1},{2,3},{4,5},{6,7},{8,9},{10,11},{12,13},{14,15},{1,0},{3,2},... | collective-permute-start | bytes 294920 | tf_op jit(solution)/shard_map/ppermute | solution.py:330
  15.8 12.6 %collective-permute-start.9 = (f32[96,256]{1,0:T(8,128)S(1)}, f32[96,256]{1,0:T(8,128)S(1)}, u32[]{:S(2)}, u32[]{:S(2)}) collective-permute-start(f32[96,256]{1,0:T(8,128)S(1)} %second_rows.1.refs_1_), channel_id=1, source_target_pairs={{1,2},{3,4},{5,6},{9,10},{11,12},{13,14},{0,8},{7,15},{2,1},{4,3},... | collective-permute-start | bytes 294920 | tf_op jit(solution)/shard_map/ppermute | solution.py:333
  15.9 12.6 %collective-permute-start.6 = (f32[96,256]{1,0:T(8,128)S(1)}, f32[96,256]{1,0:T(8,128)S(1)}, u32[]{:S(2)}, u32[]{:S(2)}) collective-permute-start(f32[96,256]{1,0:T(8,128)S(1)} %second_rows.1.refs_1_), channel_id=1, source_target_pairs={{0,1},{2,3},{4,5},{6,7},{8,9},{10,11},{12,13},{14,15},{1,0},{3,2},... | collective-permute-start | bytes 294920 | tf_op jit(solution)/shard_map/ppermute | solution.py:332
  20.8 7.7 %collective-permute-start.8 = (f32[96,256]{1,0:T(8,128)S(1)}, f32[96,256]{1,0:T(8,128)S(1)}, u32[]{:S(2)}, u32[]{:S(2)}) collective-permute-start(f32[96,256]{1,0:T(8,128)S(1)} %collective-permute-done.7.refs_2_), channel_id=1, source_target_pairs={{0,2},{2,4},{4,6},{3,1},{5,3},{7,5},{6,7},{1,0},{8,10},{10,12},{12... | collective-permute-start | bytes 294920 | tf_op jit(solution)/shard_map/ppermute | solution.py:334

commit v7 on v6

--- a/solution.py
+++ b/solution.py
@@ -88,10 +88,6 @@
         def _():
             pltpu.make_async_copy(own.at[0, b], held.at[i], sems.at[i]).start()
 
-        @pl.when(jnp.logical_not(here))
-        def _():
-            pltpu.make_async_copy(received.at[0, b], held.at[i], sems.at[i]).start()
-
     span = 2 * block_rows + 1
     zeros = jnp.zeros((size, 2 * size), jnp.bfloat16)
 
@@ -135,10 +131,20 @@
         at_lane += field.shape[1]
     for i, b in enumerate(rows):
         at = rows_at[i]
-        pltpu.make_async_copy(own.at[0, b], held.at[i], sems.at[i]).wait()
+        other = jnp.logical_not(here)
+
+        @pl.when(here)
+        def _():
+            pltpu.make_async_copy(own.at[0, b], held.at[i], sems.at[i]).wait()
 
         @pl.when(rows_repeated[i])
         def _():
+            @pl.when(other)
+            def _():
+                copy = pltpu.make_async_copy(received.at[0, b], held.at[i], sems.at[i])
+                copy.start()
+                copy.wait()
+
             for j in reversed(range(1, per_row)):
                 target = jnp.int32(per_row)
                 for k in range(j):
@@ -148,17 +154,29 @@
                 def _():
                     held[i, target] = held[i, target] + held[i, j]
 
-        def split(n, carry):
-            part = pl.ds(pl.multiple_of(n * 16, 16), 16)
-            for j in reversed(range(per_row)):
-                head, tail = head_and_tail(
-                    jnp.concatenate([held[i, j, 0, part], held[i, j, 1, part]], axis=1)
-                )
-                high[i, at[j], part] = head
-                low[i, at[j], part] = tail
-            return carry
-
-        lax.fori_loop(0, size // 16, split, 0, unroll=2)
+        def split_from(blocks):
+            def split(n, carry):
+                part = pl.ds(pl.multiple_of(n * 16, 16), 16)
+                for j in reversed(range(per_row)):
+                    head, tail = head_and_tail(
+                        jnp.concatenate([blocks[j, 0, part], blocks[j, 1, part]], axis=1)
+                    )
+                    high[i, at[j], part] = head
+                    low[i, at[j], part] = tail
+                return carry
+
+            lax.fori_loop(0, size // 16, split, 0, unroll=2)
+
+        copied = jnp.logical_or(here, rows_repeated[i])
+
+        @pl.when(copied)
+        def _():
+            split_from(held.at[i])
+
+        @pl.when(jnp.logical_not(copied))
+        def _():
+            split_from(received.at[0, b])
+
     finished = block_rows - len(rows) if halos else 0
     for i, b in enumerate(rows):
         band = slice(block_rows - b, 2 * block_rows - b)
@@ -384,7 +402,7 @@
         return pl.pallas_call(
             functools.partial(prepare_kernel, level, rows, len(halo), len(ready)),
             out_shape=[band, band, sums],
-            in_specs=[SMEM, SMEM, HBM, HBM] + [VMEM] * len(operands),
+            in_specs=[SMEM, SMEM, HBM, VMEM] + [VMEM] * len(operands),
             out_specs=[VMEM] * 3,
             scratch_shapes=[
                 pltpu.VMEM((len(rows),) + blocks.shape[2:], f32),

time: 29.9 us -> 28.9 us (0.967)
  starting transfers between devices: 14.4 us -> 13.7 us
  Pallas kernels: 11.6 us -> 11.2 us
    ppermute x2, starting transfers between devices: 5.07 us -> 4.38 us  [exchange(): relayed = lax.ppermute(first_swapped, axes, onward)]
    pallas_call x3, Pallas kernels: 7.77 us -> 7.44 us  [prepare(): pl.pallas_call(functools.partial(prepare_kernel, level, rows, len(halo),...]
where the time goes in v7:
time: 28.9 us; the launch traced here: 28.7 us
  starting transfers between devices  13.7 us (47%)
  Pallas kernels  11.2 us (39%)
  waiting for transfers between devices  3.59 us (12%)
    pallas_call x3, Pallas kernels, prepare(): pl.pallas_call(functools.partial(prepare_kernel, level, rows, len(halo),...  7.44 us
    ppermute x2, starting transfers between devices, exchange(): second_swapped = lax.ppermute(second, axes, beside)  5.48 us
    ppermute x2, starting transfers between devices, exchange(): relayed = lax.ppermute(first_swapped, axes, onward)  4.38 us
    ppermute x2, starting transfers between devices, exchange(): first_swapped = lax.ppermute(first, axes, beside)  2.99 us
    ppermute x2, waiting for transfers between devices, exchange(): first_swapped = lax.ppermute(first, axes, beside)  2.2 us
    pallas_call x2, Pallas kernels, enter(): pl.pallas_call(functools.partial(enter_kernel, rows[0] * size, len(tables...  1.9 us
    ppermute x1, waiting for transfers between devices, per_device(): other_cols = lax.ppermute(block_cols, 'depth', over_depth)  1.37 us
    pallas_call x1, Pallas kernels, per_device(): pl.pallas_call(functools.partial(bottom_kernel, len(row_groups[1])), out_...  1.2 us
  transfers between devices with their start and end apart: 10, of which 2 were waited for; matrix products, arithmetic and copies ran while one was open for 0% of the time, Pallas kernels for 34%

profile of v7, /device:TPU:0, one launch (start us, length us, event | category | flops | bytes accessed | tf_op | source)
XLA Modules:
  0.0 28.7 jit_solution(9684532757235857895)
XLA Ops:
  0.0 0.5 %collective-permute-start.5 = (f32[1,4,7,2,128,128]{5,4,3,2,1,0:T(8,128)}, f32[1,4,7,2,128,128]{5,4,3,2,1,0:T(8,128)S(1)}, u32[]{:S(2)}, u32[]{:S(2)}) collective-permute-start(f32[1,4,7,2,128,128]{5,4,3,2,1,0:T(8,128)} %own.5), channel_id=1, source_target_pairs={{0,8},{8,0},{1,9},{9,1},{2,10},{10,2},{3,11},{11,3},{4,12},{12,4},... | collective-permute-start | bytes 11010056 | tf_op jit(solution)/shard_map/ppermute | solution.py:355
  0.5 1.0 %enter.3 = (f32[96,256]{1,0:T(8,128)S(1)}, f32[2,256]{1,0:T(2,128)S(1)}, s32[1,4,7]{2,1,0:T(4,128)S(1)}) custom-call(f32[3,2,16,512]{3,2,1,0:T(8,128)} %sources.3, s32[1,512]{1,0:T(1,128)} %bitcast.1, f32[2,512]{1,0:T(2,128)} %refl_coef.3, s32[1,4,7]{2,1,0:T(4,128)} %refs_0_.1), custom_call_target="tpu_custom_call" | custom-call | tf_op jit(solution)/shard_map/enter/pallas_call | solution.py:361
  1.5 2.5 %collective-permute-start.1 = (f32[96,256]{1,0:T(8,128)S(1)}, f32[96,256]{1,0:T(8,128)S(1)}, u32[]{:S(2)}, u32[]{:S(2)}) collective-permute-start(f32[96,256]{1,0:T(8,128)S(1)} %get-tuple-element.23.refs_0_), channel_id=1, source_target_pairs={{0,1},{2,3},{4,5},{6,7},{8,9},{10,11},{12,13},{14,15},{1,0},{3,2},... | collective-permute-start | bytes 294920 | tf_op jit(solution)/shard_map/ppermute | solution.py:348
  4.0 0.9 %enter.2 = (f32[96,256]{1,0:T(8,128)S(1)}, f32[2,256]{1,0:T(2,128)S(1)}) custom-call(f32[3,2,16,512]{3,2,1,0:T(8,128)} %sources.3, s32[1,512]{1,0:T(1,128)} %bitcast.2, f32[2,512]{1,0:T(2,128)} %refl_coef.3), custom_call_target="tpu_custom_call" | custom-call | tf_op jit(solution)/shard_map/enter/pallas_call | solution.py:361
  5.0 0.3 %collective-permute-start.3 = (f32[96,256]{1,0:T(8,128)S(1)}, f32[96,256]{1,0:T(8,128)S(1)}, u32[]{:S(2)}, u32[]{:S(2)}) collective-permute-start(f32[96,256]{1,0:T(8,128)S(1)} %get-tuple-element.22.refs_1_), channel_id=1, source_target_pairs={{1,2},{3,4},{5,6},{9,10},{11,12},{13,14},{0,8},{7,15},{2,1},{4,3},... | collective-permute-start | bytes 294920 | tf_op jit(solution)/shard_map/ppermute | solution.py:351
  5.2 2.8 %collective-permute-start = (f32[96,256]{1,0:T(8,128)S(1)}, f32[96,256]{1,0:T(8,128)S(1)}, u32[]{:S(2)}, u32[]{:S(2)}) collective-permute-start(f32[96,256]{1,0:T(8,128)S(1)} %get-tuple-element.22.refs_1_), channel_id=1, source_target_pairs={{0,1},{2,3},{4,5},{6,7},{8,9},{10,11},{12,13},{14,15},{1,0},{3,2},... | collective-permute-start | bytes 294920 | tf_op jit(solution)/shard_map/ppermute | solution.py:350
  8.1 0.0 collective-permute-done.1.refs_2_
  8.1 1.6 %collective-permute-start.2 = (f32[96,256]{1,0:T(8,128)S(1)}, f32[96,256]{1,0:T(8,128)S(1)}, u32[]{:S(2)}, u32[]{:S(2)}) collective-permute-start(f32[96,256]{1,0:T(8,128)S(1)} %collective-permute-done.1.refs_2_), channel_id=1, source_target_pairs={{0,2},{2,4},{4,6},{3,1},{5,3},{7,5},{6,7},{1,0},{8,10},{10,12},{12... | collective-permute-start | bytes 294920 | tf_op jit(solution)/shard_map/ppermute | solution.py:352
  9.6 0.0 collective-permute-start.4
  9.6 1.4 %collective-permute-done.4.other_cols = s32[1,4,7]{2,1,0:T(4,128)S(1)} collective-permute-done((s32[1,4,7]{2,1,0:T(4,128)}, s32[1,4,7]{2,1,0:T(4,128)S(1)}, u32[]{:S(2)}, u32[]{:S(2)}) %collective-permute-start.4) | collective-permute-done | bytes 144 | tf_op jit(solution)/shard_map/ppermute | solution.py:356
  11.0 0.0 collective-permute-done.5.received
  11.0 3.6 %prepare.3 = (bf16[4,9,128,256]{3,2,1,0:T(8,128)(2,1)S(1)}, bf16[4,9,128,256]{3,2,1,0:T(8,128)(2,1)S(1)}, f32[4,96,256]{2,1,0:T(8,128)S(1)}) custom-call(s32[1,4,7]{2,1,0:T(4,128)S(1)} %get-tuple-element.24.own_cols, s32[1,4,7]{2,1,0:T(4,128)S(1)} %collective-permute-done.4.other_cols, f32[1,4,7,2,128,128]{5,4,3,2,1,0:T(8,128)} %own.5, ...), custom_call_target="tpu_custom_call" | custom-call | flops 75497472 | bytes 3670016 | tf_op jit(solution)/shard_map/prepare/pallas_call | solution.py:402
  14.6 0.0 collective-permute-done.3.diagonal
  14.6 0.0 collective-permute-done.swapped
  14.6 0.0 collective-permute-done.2.relayed
  14.7 0.4 %first_rows.1 = (f32[96,256]{1,0:T(8,128)S(1)}, bf16[192,256]{1,0:T(8,128)(2,1)S(1)}, bf16[192,512]{1,0:T(8,128)(2,1)S(1)}) custom-call(f32[96,256]{1,0:T(8,128)S(1)} %collective-permute-done.swapped, f32[96,256]{1,0:T(8,128)S(1)} %collective-permute-done.2.relayed, f32[96,256]{1,0:T(8,128)S(1)} %collective-permute-done.3.diagonal, ...), custom_call_target="tpu_custom_call" | custom-call | flops 37748736 | bytes 917504 | tf_op jit(solution)/shard_map/first_rows/pallas_call | solution.py:430
  15.0 0.5 %collective-permute-start.7 = (f32[96,256]{1,0:T(8,128)S(1)}, f32[96,256]{1,0:T(8,128)S(1)}, u32[]{:S(2)}, u32[]{:S(2)}) collective-permute-start(f32[96,256]{1,0:T(8,128)S(1)} %get-tuple-element.32.refs_0_), channel_id=1, source_target_pairs={{0,1},{2,3},{4,5},{6,7},{8,9},{10,11},{12,13},{14,15},{1,0},{3,2},... | collective-permute-start | bytes 294920 | tf_op jit(solution)/shard_map/ppermute | solution.py:348
  15.5 0.3 %second_rows.1.refs_1_ = f32[96,256]{1,0:T(8,128)S(1)} custom-call(bf16[192,256]{1,0:T(8,128)(2,1)S(1)} %get-tuple-element.29.swapped, bf16[192,512]{1,0:T(8,128)(2,1)S(1)} %get-tuple-element.30.diagonal, bf16[4,9,128,256]{3,2,1,0:T(8,128)(2,1)S(1)} %get-tuple-element.25.refs_0_, bf16[4,9,128,256]{3,2,1,0:T(8,128)(2,1)S(1)} %get-tuple-element.26.refs_1_, ...), custom_call_target="tpu_custom_call" | custom-call | flops 37748736 | bytes 917504 | tf_op jit(solution)/shard_map/second_rows/pallas_call | solution.py:445
  15.8 0.1 collective-permute-start.9
  15.9 2.7 %collective-permute-start.6 = (f32[96,256]{1,0:T(8,128)S(1)}, f32[96,256]{1,0:T(8,128)S(1)}, u32[]{:S(2)}, u32[]{:S(2)}) collective-permute-start(f32[96,256]{1,0:T(8,128)S(1)} %second_rows.1.refs_1_), channel_id=1, source_target_pairs={{0,1},{2,3},{4,5},{6,7},{8,9},{10,11},{12,13},{14,15},{1,0},{3,2},... | collective-permute-start | bytes 294920 | tf_op jit(solution)/shard_map/ppermute | solution.py:350
  18.6 2.2 %collective-permute-done.7.refs_2_ = f32[96,256]{1,0:T(8,128)S(1)} collective-permute-done((f32[96,256]{1,0:T(8,128)S(1)}, f32[96,256]{1,0:T(8,128)S(1)}, u32[]{:S(2)}, u32[]{:S(2)}) %collective-permute-start.7) | collective-permute-done | bytes 98336 | tf_op jit(solution)/shard_map/ppermute | solution.py:348
  20.8 2.8 %collective-permute-start.8 = (f32[96,256]{1,0:T(8,128)S(1)}, f32[96,256]{1,0:T(8,128)S(1)}, u32[]{:S(2)}, u32[]{:S(2)}) collective-permute-start(f32[96,256]{1,0:T(8,128)S(1)} %collective-permute-done.7.refs_2_), channel_id=1, source_target_pairs={{0,2},{2,4},{4,6},{3,1},{5,3},{7,5},{6,7},{1,0},{8,10},{10,12},{12... | collective-permute-start | bytes 294920 | tf_op jit(solution)/shard_map/ppermute | solution.py:352
  23.6 1.5 %prepare.4 = (bf16[1,9,128,256]{3,2,1,0:T(8,128)(2,1)S(1)}, bf16[1,9,128,256]{3,2,1,0:T(8,128)(2,1)S(1)}, f32[1,96,256]{2,1,0:T(8,128)S(1)}) custom-call(s32[1,4,7]{2,1,0:T(4,128)S(1)} %get-tuple-element.24.own_cols, s32[1,4,7]{2,1,0:T(4,128)S(1)} %collective-permute-done.4.other_cols, f32[1,4,7,2,128,128]{5,4,3,2,1,0:T(8,128)} %own.5, ...), custom_call_target="tpu_custom_call" | custom-call | flops 75497472 | bytes 3670016 | tf_op jit(solution)/shard_map/prepare/pallas_call | solution.py:402
  25.1 2.4 %prepare.5 = (bf16[3,9,128,256]{3,2,1,0:T(8,128)(2,1)S(1)}, bf16[3,9,128,256]{3,2,1,0:T(8,128)(2,1)S(1)}, f32[4,96,256]{2,1,0:T(8,128)S(1)}) custom-call(s32[1,4,7]{2,1,0:T(4,128)S(1)} %get-tuple-element.24.own_cols, s32[1,4,7]{2,1,0:T(4,128)S(1)} %collective-permute-done.4.other_cols, f32[1,4,7,2,128,128]{5,4,3,2,1,0:T(8,128)} %own.5, ...), custom_call_target="tpu_custom_call" | custom-call | flops 75497472 | bytes 3670016 | tf_op jit(solution)/shard_map/prepare/pallas_call | solution.py:402
  27.4 0.0 collective-permute-done.9.diagonal
  27.4 0.0 collective-permute-done.6.swapped
  27.5 0.0 collective-permute-done.8.relayed
  27.5 1.2 %bottom.1 = f32[3,2,16,512]{3,2,1,0:T(8,128)} custom-call(f32[96,256]{1,0:T(8,128)S(1)} %collective-permute-done.6.swapped, f32[96,256]{1,0:T(8,128)S(1)} %collective-permute-done.8.relayed, f32[96,256]{1,0:T(8,128)S(1)} %collective-permute-done.9.diagonal, bf16[1,9,128,256]{3,2,1,0:T(8,128)(2,1)S(1)} %get-tuple-element.33.refs_3_.refs_0_, ...), custom_call_target="tpu_custom_call" | custom-call | flops 37748736 | bytes 917504 | tf_op jit(solution)/shard_map/bottom/pallas_call | solution.py:457
Async XLA Ops:
  0.0 11.0 %collective-permute-start.5 = (f32[1,4,7,2,128,128]{5,4,3,2,1,0:T(8,128)}, f32[1,4,7,2,128,128]{5,4,3,2,1,0:T(8,128)S(1)}, u32[]{:S(2)}, u32[]{:S(2)}) collective-permute-start(f32[1,4,7,2,128,128]{5,4,3,2,1,0:T(8,128)} %own.5), channel_id=1, source_target_pairs={{0,8},{8,0},{1,9},{9,1},{2,10},{10,2},{3,11},{11,3},{4,12},{12,4},... | collective-permute-start | bytes 11010056 | tf_op jit(solution)/shard_map/ppermute | solution.py:355
  1.5 6.6 %collective-permute-start.1 = (f32[96,256]{1,0:T(8,128)S(1)}, f32[96,256]{1,0:T(8,128)S(1)}, u32[]{:S(2)}, u32[]{:S(2)}) collective-permute-start(f32[96,256]{1,0:T(8,128)S(1)} %get-tuple-element.23.refs_0_), channel_id=1, source_target_pairs={{0,1},{2,3},{4,5},{6,7},{8,9},{10,11},{12,13},{14,15},{1,0},{3,2},... | collective-permute-start | bytes 294920 | tf_op jit(solution)/shard_map/ppermute | solution.py:348
  5.0 9.7 %collective-permute-start.3 = (f32[96,256]{1,0:T(8,128)S(1)}, f32[96,256]{1,0:T(8,128)S(1)}, u32[]{:S(2)}, u32[]{:S(2)}) collective-permute-start(f32[96,256]{1,0:T(8,128)S(1)} %get-tuple-element.22.refs_1_), channel_id=1, source_target_pairs={{1,2},{3,4},{5,6},{9,10},{11,12},{13,14},{0,8},{7,15},{2,1},{4,3},... | collective-permute-start | bytes 294920 | tf_op jit(solution)/shard_map/ppermute | solution.py:351
  5.2 9.4 %collective-permute-start = (f32[96,256]{1,0:T(8,128)S(1)}, f32[96,256]{1,0:T(8,128)S(1)}, u32[]{:S(2)}, u32[]{:S(2)}) collective-permute-start(f32[96,256]{1,0:T(8,128)S(1)} %get-tuple-element.22.refs_1_), channel_id=1, source_target_pairs={{0,1},{2,3},{4,5},{6,7},{8,9},{10,11},{12,13},{14,15},{1,0},{3,2},... | collective-permute-start | bytes 294920 | tf_op jit(solution)/shard_map/ppermute | solution.py:350
  8.1 6.6 %collective-permute-start.2 = (f32[96,256]{1,0:T(8,128)S(1)}, f32[96,256]{1,0:T(8,128)S(1)}, u32[]{:S(2)}, u32[]{:S(2)}) collective-permute-start(f32[96,256]{1,0:T(8,128)S(1)} %collective-permute-done.1.refs_2_), channel_id=1, source_target_pairs={{0,2},{2,4},{4,6},{3,1},{5,3},{7,5},{6,7},{1,0},{8,10},{10,12},{12... | collective-permute-start | bytes 294920 | tf_op jit(solution)/shard_map/ppermute | solution.py:352
  9.6 1.4 %collective-permute-start.4 = (s32[1,4,7]{2,1,0:T(4,128)}, s32[1,4,7]{2,1,0:T(4,128)S(1)}, u32[]{:S(2)}, u32[]{:S(2)}) collective-permute-start(s32[1,4,7]{2,1,0:T(4,128)} %refs_0_.1), channel_id=1, source_target_pairs={{0,8},{8,0},{1,9},{9,1},{2,10},{10,2},{3,11},{11,3},{4,12},{12,4},... | collective-permute-start | bytes 344 | tf_op jit(solution)/shard_map/ppermute | solution.py:356
  15.0 5.7 %collective-permute-start.7 = (f32[96,256]{1,0:T(8,128)S(1)}, f32[96,256]{1,0:T(8,128)S(1)}, u32[]{:S(2)}, u32[]{:S(2)}) collective-permute-start(f32[96,256]{1,0:T(8,128)S(1)} %get-tuple-element.32.refs_0_), channel_id=1, source_target_pairs={{0,1},{2,3},{4,5},{6,7},{8,9},{10,11},{12,13},{14,15},{1,0},{3,2},... | collective-permute-start | bytes 294920 | tf_op jit(solution)/shard_map/ppermute | solution.py:348
  15.8 11.6 %collective-permute-start.9 = (f32[96,256]{1,0:T(8,128)S(1)}, f32[96,256]{1,0:T(8,128)S(1)}, u32[]{:S(2)}, u32[]{:S(2)}) collective-permute-start(f32[96,256]{1,0:T(8,128)S(1)} %second_rows.1.refs_1_), channel_id=1, source_target_pairs={{1,2},{3,4},{5,6},{9,10},{11,12},{13,14},{0,8},{7,15},{2,1},{4,3},... | collective-permute-start | bytes 294920 | tf_op jit(solution)/shard_map/ppermute | solution.py:351
  15.9 11.5 %collective-permute-start.6 = (f32[96,256]{1,0:T(8,128)S(1)}, f32[96,256]{1,0:T(8,128)S(1)}, u32[]{:S(2)}, u32[]{:S(2)}) collective-permute-start(f32[96,256]{1,0:T(8,128)S(1)} %second_rows.1.refs_1_), channel_id=1, source_target_pairs={{0,1},{2,3},{4,5},{6,7},{8,9},{10,11},{12,13},{14,15},{1,0},{3,2},... | collective-permute-start | bytes 294920 | tf_op jit(solution)/shard_map/ppermute | solution.py:350
  20.8 6.7 %collective-permute-start.8 = (f32[96,256]{1,0:T(8,128)S(1)}, f32[96,256]{1,0:T(8,128)S(1)}, u32[]{:S(2)}, u32[]{:S(2)}) collective-permute-start(f32[96,256]{1,0:T(8,128)S(1)} %collective-permute-done.7.refs_2_), channel_id=1, source_target_pairs={{0,2},{2,4},{4,6},{3,1},{5,3},{7,5},{6,7},{1,0},{8,10},{10,12},{12... | collective-permute-start | bytes 294920 | tf_op jit(solution)/shard_map/ppermute | solution.py:352

commit v8 on v7

--- a/solution.py
+++ b/solution.py
@@ -40,7 +40,7 @@
                 (sources.at[:, :, :, lanes], held),
                 (refl_level.at[:, lanes], level_held),
                 (refl_coef.at[:, lanes], coef_held),
-                *zip(tables_in, tables_out),
+                *((a.at[:, : b.shape[1]], b) for a, b in zip(tables_in, tables_out)),
             )
         )
     ]
@@ -53,6 +53,14 @@
     total[...] = entered(held, coef)
 
 
+def fetch_kernel(table, out, sems):
+    count = out.shape[1]
+    for i in range(count):
+        pltpu.make_async_copy(table.at[0, i], out.at[0, i], sems.at[i]).start()
+    for i in range(count):
+        pltpu.make_async_copy(table.at[0, i], out.at[0, i], sems.at[i]).wait()
+
+
 def head_and_tail(value):
     head = value.astype(jnp.bfloat16)
     return head, (value - head.astype(jnp.float32)).astype(jnp.bfloat16)
@@ -71,7 +79,7 @@
     return both[:rows] + both[rows:] + cross
 
 
-def prepare_kernel(level, rows, halos, done, own_cols, other_cols, own, received, *refs):
+def prepare_kernel(level, rows, halos, done, own_cols, other_cols, own, near, received, *refs):
     outs = len(refs) - 6 - halos
     high, low, sums, held, left, *early, sems = refs[outs:]
     fields, refs = refs[: outs - halos - 3 * done], refs[outs - halos - 3 * done : outs]
@@ -82,11 +90,17 @@
     block_rows = own.shape[1]
     here = lax.axis_index("depth") == level
     first_row = lax.axis_index("lat") * block_rows
+    other = jnp.logical_not(here)
+    far = [b >= near.shape[1] for b in rows]
+
+    def start(condition, source, i, b):
+        @pl.when(condition)
+        def _():
+            pltpu.make_async_copy(source.at[0, b], held.at[i], sems.at[i]).start()
+
     for i, b in enumerate(rows):
-
-        @pl.when(here)
-        def _():
-            pltpu.make_async_copy(own.at[0, b], held.at[i], sems.at[i]).start()
+        if far[i]:
+            start(here, own, i, b)
 
     span = 2 * block_rows + 1
     zeros = jnp.zeros((size, 2 * size), jnp.bfloat16)
@@ -107,6 +121,9 @@
         repeated = sum(bits) != present
         rows_at.append(at)
         rows_repeated.append(repeated)
+        start(jnp.logical_and(other, repeated), received, i, b)
+        if not far[i]:
+            start(jnp.logical_and(here, repeated), near, i, b)
         absent = (1 << span) - 1 - present
         lowest = sum(jnp.where(absent % (2 << o) == 0, 1, 0) for o in range(span - 1))
         highest = sum(jnp.where(absent >= (2 << o), 1, 0) for o in range(span - 1))
@@ -131,20 +148,14 @@
         at_lane += field.shape[1]
     for i, b in enumerate(rows):
         at = rows_at[i]
-        other = jnp.logical_not(here)
-
-        @pl.when(here)
+        copied = jnp.logical_or(here, rows_repeated[i]) if far[i] else rows_repeated[i]
+
+        @pl.when(copied)
         def _():
-            pltpu.make_async_copy(own.at[0, b], held.at[i], sems.at[i]).wait()
+            pltpu.make_async_copy(received.at[0, b], held.at[i], sems.at[i]).wait()
 
         @pl.when(rows_repeated[i])
         def _():
-            @pl.when(other)
-            def _():
-                copy = pltpu.make_async_copy(received.at[0, b], held.at[i], sems.at[i])
-                copy.start()
-                copy.wait()
-
             for j in reversed(range(1, per_row)):
                 target = jnp.int32(per_row)
                 for k in range(j):
@@ -167,15 +178,21 @@
 
             lax.fori_loop(0, size // 16, split, 0, unroll=2)
 
-        copied = jnp.logical_or(here, rows_repeated[i])
+        direct = jnp.logical_not(copied)
 
         @pl.when(copied)
         def _():
             split_from(held.at[i])
 
-        @pl.when(jnp.logical_not(copied))
+        @pl.when(jnp.logical_and(direct, other))
         def _():
             split_from(received.at[0, b])
+
+        if not far[i]:
+
+            @pl.when(jnp.logical_and(direct, here))
+            def _():
+                split_from(near.at[0, b])
 
     finished = block_rows - len(rows) if halos else 0
     for i, b in enumerate(rows):
@@ -363,7 +380,10 @@
             out_shape=[
                 part_shape(rows),
                 jax.ShapeDtypeStruct((2, width), f32),
-                *(jax.ShapeDtypeStruct(table.shape, table.dtype) for table in tables),
+                *(
+                    jax.ShapeDtypeStruct((1, count) + table.shape[2:], table.dtype)
+                    for table, count in tables
+                ),
             ],
             in_specs=[HBM] * (3 + len(tables)),
             out_specs=[VMEM] * (2 + len(tables)),
@@ -374,9 +394,9 @@
                 pltpu.VMEM((2, width), f32),
                 pltpu.SemaphoreType.DMA((3 + len(tables),)),
             ],
-            compiler_params=params(4),
+            compiler_params=params(8),
             name="enter",
-        )(*map(in_hbm, (sources, refl_level, refl_coef, *tables)))
+        )(*map(in_hbm, (sources, refl_level, refl_coef, *(table for table, _ in tables))))
 
     coefs = []
 
@@ -385,14 +405,24 @@
         coefs.append(coef)
         return part_total
 
-    first_total, coef, own_cols = enter(first_rows, block_cols)
+    near = pl.pallas_call(
+        fetch_kernel,
+        out_shape=jax.ShapeDtypeStruct((1, half) + blocks.shape[2:], f32),
+        in_specs=[HBM],
+        out_specs=VMEM,
+        scratch_shapes=[pltpu.SemaphoreType.DMA((half,))],
+        compiler_params=params(8),
+        cost_estimate=cost(0, 2 * blocks.size),
+        name="fetch",
+    )(in_hbm(blocks))
+    first_total, coef, own_cols = enter(first_rows, (block_cols, block_rows))
     coefs.append(coef)
     second_total, early, late = exchange(first_total, enter_second)
 
     macs = 6 * channels * points * 2 * size
 
     every_row = range(block_rows)
-    row_groups = ((every_row,), (every_row[:1], every_row[1:]))
+    row_groups = ((every_row,), (every_row[:1], every_row[1:half], every_row[half:]))
 
     def prepare(level, rows, fields, halo, ready):
         band = jax.ShapeDtypeStruct((len(rows), 2 * block_rows + 1, size, 2 * size), bf16)
@@ -402,7 +432,7 @@
         return pl.pallas_call(
             functools.partial(prepare_kernel, level, rows, len(halo), len(ready)),
             out_shape=[band, band, sums],
-            in_specs=[SMEM, SMEM, HBM, VMEM] + [VMEM] * len(operands),
+            in_specs=[SMEM, SMEM, HBM, VMEM, VMEM] + [VMEM] * len(operands),
             out_specs=[VMEM] * 3,
             scratch_shapes=[
                 pltpu.VMEM((len(rows),) + blocks.shape[2:], f32),
@@ -413,7 +443,7 @@
             compiler_params=params(16),
             cost_estimate=cost(2 * macs, 4 * blocks.size),
             name="prepare",
-        )(own_cols, other_cols, in_hbm(blocks), other_blocks, *operands)
+        )(own_cols, other_cols, in_hbm(blocks), near, other_blocks, *operands)
 
     def early_products(level, halo, *fields):
         ready = []

time: 28.9 us -> 28.5 us (0.986)
  starting transfers between devices: 13.7 us -> 9.94 us
  Pallas kernels: 11.2 us -> 13.1 us
  waiting for transfers between devices: 3.59 us -> 5.15 us
    ppermute x2, starting transfers between devices: 5.48 us -> 2.08 us  [exchange(): second_swapped = lax.ppermute(second, axes, beside)]
    ppermute x2, waiting for transfers between devices: 2.2 us -> 5.13 us  [exchange(): first_swapped = lax.ppermute(first, axes, beside)]
    pallas_call x0 -> x1, Pallas kernels: none -> 1.47 us  [per_device(): pl.pallas_call(fetch_kernel, out_shape=jax.ShapeDtypeStruct((1, half) + b...]
    ppermute x1, waiting for transfers between devices: 1.37 us -> 0.01 us  [per_device(): other_cols = lax.ppermute(block_cols, 'depth', over_depth)]
    pallas_call x3 -> x4, Pallas kernels: 7.44 us -> 7.8 us  [prepare(): pl.pallas_call(functools.partial(prepare_kernel, level, rows, len(halo),...]
  transfers between devices with their start and end apart: 10 -> 10, of which waited for: 2 -> 2; matrix products, arithmetic and copies ran while one was open for 0% -> 0% of each run, Pallas kernels for 34% -> 41%
where the time goes in v8:
time: 28.5 us; the launch traced here: 28.3 us
  Pallas kernels  13.1 us (46%)
  starting transfers between devices  9.94 us (35%)
  waiting for transfers between devices  5.15 us (18%)
    pallas_call x4, Pallas kernels, prepare(): pl.pallas_call(functools.partial(prepare_kernel, level, rows, len(halo),...  7.8 us
    ppermute x2, waiting for transfers between devices, exchange(): first_swapped = lax.ppermute(first, axes, beside)  5.13 us
    ppermute x2, starting transfers between devices, exchange(): relayed = lax.ppermute(first_swapped, axes, onward)  4.12 us
    ppermute x2, starting transfers between devices, exchange(): first_swapped = lax.ppermute(first, axes, beside)  2.8 us
    ppermute x2, starting transfers between devices, exchange(): second_swapped = lax.ppermute(second, axes, beside)  2.08 us
    pallas_call x2, Pallas kernels, enter(): pl.pallas_call(functools.partial(enter_kernel, rows[0] * size, len(tables...  1.9 us
    pallas_call x1, Pallas kernels, per_device(): pl.pallas_call(fetch_kernel, out_shape=jax.ShapeDtypeStruct((1, half) + b...  1.47 us
    pallas_call x1, Pallas kernels, per_device(): pl.pallas_call(functools.partial(bottom_kernel, len(row_groups[1])), out_...  1.2 us
  transfers between devices with their start and end apart: 10, of which 2 were waited for; matrix products, arithmetic and copies ran while one was open for 0% of the time, Pallas kernels for 41%

profile of v8, /device:TPU:0, one launch (start us, length us, event | category | flops | bytes accessed | tf_op | source)
XLA Modules:
  0.0 28.3 jit_solution(7918612813541194502)
XLA Ops:
  0.0 0.5 %collective-permute-start.5 = (f32[1,4,7,2,128,128]{5,4,3,2,1,0:T(8,128)}, f32[1,4,7,2,128,128]{5,4,3,2,1,0:T(8,128)S(1)}, u32[]{:S(2)}, u32[]{:S(2)}) collective-permute-start(f32[1,4,7,2,128,128]{5,4,3,2,1,0:T(8,128)} %own.7), channel_id=1, source_target_pairs={{0,8},{8,0},{1,9},{9,1},{2,10},{10,2},{3,11},{11,3},{4,12},{12,4},... | collective-permute-start | bytes 11010056 | tf_op jit(solution)/shard_map/ppermute | solution.py:372
  0.5 1.0 %enter.3 = (f32[96,256]{1,0:T(8,128)S(1)}, f32[2,256]{1,0:T(2,128)S(1)}, s32[1,4,7]{2,1,0:T(4,128)S(1)}) custom-call(f32[3,2,16,512]{3,2,1,0:T(8,128)} %sources.3, s32[1,512]{1,0:T(1,128)} %bitcast.1, f32[2,512]{1,0:T(2,128)} %refl_coef.3, s32[1,4,7]{2,1,0:T(4,128)} %refs_0_.1), custom_call_target="tpu_custom_call" | custom-call | tf_op jit(solution)/shard_map/enter/pallas_call | solution.py:378
  1.5 2.5 %collective-permute-start.1 = (f32[96,256]{1,0:T(8,128)S(1)}, f32[96,256]{1,0:T(8,128)S(1)}, u32[]{:S(2)}, u32[]{:S(2)}) collective-permute-start(f32[96,256]{1,0:T(8,128)S(1)} %get-tuple-element.26.refs_0_), channel_id=1, source_target_pairs={{0,1},{2,3},{4,5},{6,7},{8,9},{10,11},{12,13},{14,15},{1,0},{3,2},... | collective-permute-start | bytes 294920 | tf_op jit(solution)/shard_map/ppermute | solution.py:365
  4.0 0.9 %enter.2 = (f32[96,256]{1,0:T(8,128)S(1)}, f32[2,256]{1,0:T(2,128)S(1)}) custom-call(f32[3,2,16,512]{3,2,1,0:T(8,128)} %sources.3, s32[1,512]{1,0:T(1,128)} %bitcast.2, f32[2,512]{1,0:T(2,128)} %refl_coef.3), custom_call_target="tpu_custom_call" | custom-call | tf_op jit(solution)/shard_map/enter/pallas_call | solution.py:378
  5.0 0.1 collective-permute-start
  5.0 0.3 %collective-permute-start.3 = (f32[96,256]{1,0:T(8,128)S(1)}, f32[96,256]{1,0:T(8,128)S(1)}, u32[]{:S(2)}, u32[]{:S(2)}) collective-permute-start(f32[96,256]{1,0:T(8,128)S(1)} %get-tuple-element.25.refs_1_), channel_id=1, source_target_pairs={{1,2},{3,4},{5,6},{9,10},{11,12},{13,14},{0,8},{7,15},{2,1},{4,3},... | collective-permute-start | bytes 294920 | tf_op jit(solution)/shard_map/ppermute | solution.py:368
  5.3 2.1 %collective-permute-done.1.refs_2_ = f32[96,256]{1,0:T(8,128)S(1)} collective-permute-done((f32[96,256]{1,0:T(8,128)S(1)}, f32[96,256]{1,0:T(8,128)S(1)}, u32[]{:S(2)}, u32[]{:S(2)}) %collective-permute-start.1) | collective-permute-done | bytes 98336 | tf_op jit(solution)/shard_map/ppermute | solution.py:365
  7.5 1.8 %collective-permute-start.2 = (f32[96,256]{1,0:T(8,128)S(1)}, f32[96,256]{1,0:T(8,128)S(1)}, u32[]{:S(2)}, u32[]{:S(2)}) collective-permute-start(f32[96,256]{1,0:T(8,128)S(1)} %collective-permute-done.1.refs_2_), channel_id=1, source_target_pairs={{0,2},{2,4},{4,6},{3,1},{5,3},{7,5},{6,7},{1,0},{8,10},{10,12},{12... | collective-permute-start | bytes 294920 | tf_op jit(solution)/shard_map/ppermute | solution.py:369
  9.3 0.0 collective-permute-start.4
  9.3 1.5 %fetch.1.near = f32[1,2,7,2,128,128]{5,4,3,2,1,0:T(8,128)S(1)} custom-call(f32[1,4,7,2,128,128]{5,4,3,2,1,0:T(8,128)} %own.7), custom_call_target="tpu_custom_call" | custom-call | bytes 1835008 | tf_op jit(solution)/shard_map/fetch/pallas_call | solution.py:408
  10.8 0.0 collective-permute-done.4.other_cols
  10.8 0.0 collective-permute-done.5.received
  10.8 3.2 %prepare.4 = (bf16[4,9,128,256]{3,2,1,0:T(8,128)(2,1)S(1)}, bf16[4,9,128,256]{3,2,1,0:T(8,128)(2,1)S(1)}, f32[4,96,256]{2,1,0:T(8,128)S(1)}) custom-call(s32[1,4,7]{2,1,0:T(4,128)S(1)} %get-tuple-element.27.own_cols, s32[1,4,7]{2,1,0:T(4,128)S(1)} %collective-permute-done.4.other_cols, f32[1,4,7,2,128,128]{5,4,3,2,1,0:T(8,128)} %own.7, ...), custom_call_target="tpu_custom_call" | custom-call | flops 75497472 | bytes 3670016 | tf_op jit(solution)/shard_map/prepare/pallas_call | solution.py:432
  14.1 0.0 collective-permute-done.swapped
  14.1 0.0 collective-permute-done.3.diagonal
  14.1 0.0 collective-permute-done.2.relayed
  14.1 0.4 %first_rows.1 = (f32[96,256]{1,0:T(8,128)S(1)}, bf16[192,256]{1,0:T(8,128)(2,1)S(1)}, bf16[192,512]{1,0:T(8,128)(2,1)S(1)}) custom-call(f32[96,256]{1,0:T(8,128)S(1)} %collective-permute-done.swapped, f32[96,256]{1,0:T(8,128)S(1)} %collective-permute-done.2.relayed, f32[96,256]{1,0:T(8,128)S(1)} %collective-permute-done.3.diagonal, ...), custom_call_target="tpu_custom_call" | custom-call | flops 37748736 | bytes 917504 | tf_op jit(solution)/shard_map/first_rows/pallas_call | solution.py:460
  14.5 0.3 collective-permute-start.7
  14.7 0.3 %second_rows.1.refs_1_ = f32[96,256]{1,0:T(8,128)S(1)} custom-call(bf16[192,256]{1,0:T(8,128)(2,1)S(1)} %get-tuple-element.32.swapped, bf16[192,512]{1,0:T(8,128)(2,1)S(1)} %get-tuple-element.33.diagonal, bf16[4,9,128,256]{3,2,1,0:T(8,128)(2,1)S(1)} %get-tuple-element.28.refs_0_, bf16[4,9,128,256]{3,2,1,0:T(8,128)(2,1)S(1)} %get-tuple-element.29.refs_1_, ...), custom_call_target="tpu_custom_call" | custom-call | flops 37748736 | bytes 917504 | tf_op jit(solution)/shard_map/second_rows/pallas_call | solution.py:475
  15.1 2.0 %collective-permute-start.6 = (f32[96,256]{1,0:T(8,128)S(1)}, f32[96,256]{1,0:T(8,128)S(1)}, u32[]{:S(2)}, u32[]{:S(2)}) collective-permute-start(f32[96,256]{1,0:T(8,128)S(1)} %second_rows.1.refs_1_), channel_id=1, source_target_pairs={{0,1},{2,3},{4,5},{6,7},{8,9},{10,11},{12,13},{14,15},{1,0},{3,2},... | collective-permute-start | bytes 294920 | tf_op jit(solution)/shard_map/ppermute | solution.py:367
  17.1 0.2 collective-permute-start.9
  17.2 3.0 %collective-permute-done.7.refs_2_ = f32[96,256]{1,0:T(8,128)S(1)} collective-permute-done((f32[96,256]{1,0:T(8,128)S(1)}, f32[96,256]{1,0:T(8,128)S(1)}, u32[]{:S(2)}, u32[]{:S(2)}) %collective-permute-start.7) | collective-permute-done | bytes 98336 | tf_op jit(solution)/shard_map/ppermute | solution.py:365
  20.2 2.3 %collective-permute-start.8 = (f32[96,256]{1,0:T(8,128)S(1)}, f32[96,256]{1,0:T(8,128)S(1)}, u32[]{:S(2)}, u32[]{:S(2)}) collective-permute-start(f32[96,256]{1,0:T(8,128)S(1)} %collective-permute-done.7.refs_2_), channel_id=1, source_target_pairs={{0,2},{2,4},{4,6},{3,1},{5,3},{7,5},{6,7},{1,0},{8,10},{10,12},{12... | collective-permute-start | bytes 294920 | tf_op jit(solution)/shard_map/ppermute | solution.py:369
  22.5 1.4 %prepare.6 = (bf16[1,9,128,256]{3,2,1,0:T(8,128)(2,1)S(1)}, bf16[1,9,128,256]{3,2,1,0:T(8,128)(2,1)S(1)}, f32[1,96,256]{2,1,0:T(8,128)S(1)}) custom-call(s32[1,4,7]{2,1,0:T(4,128)S(1)} %get-tuple-element.27.own_cols, s32[1,4,7]{2,1,0:T(4,128)S(1)} %collective-permute-done.4.other_cols, f32[1,4,7,2,128,128]{5,4,3,2,1,0:T(8,128)} %own.7, ...), custom_call_target="tpu_custom_call" | custom-call | flops 75497472 | bytes 3670016 | tf_op jit(solution)/shard_map/prepare/pallas_call | solution.py:432
  23.9 1.5 %prepare.5 = (bf16[1,9,128,256]{3,2,1,0:T(8,128)(2,1)S(1)}, bf16[1,9,128,256]{3,2,1,0:T(8,128)(2,1)S(1)}, f32[1,96,256]{2,1,0:T(8,128)S(1)}) custom-call(s32[1,4,7]{2,1,0:T(4,128)S(1)} %get-tuple-element.27.own_cols, s32[1,4,7]{2,1,0:T(4,128)S(1)} %collective-permute-done.4.other_cols, f32[1,4,7,2,128,128]{5,4,3,2,1,0:T(8,128)} %own.7, ...), custom_call_target="tpu_custom_call" | custom-call | flops 75497472 | bytes 3670016 | tf_op jit(solution)/shard_map/prepare/pallas_call | solution.py:432
  25.4 1.7 %prepare.7 = (bf16[2,9,128,256]{3,2,1,0:T(8,128)(2,1)S(1)}, bf16[2,9,128,256]{3,2,1,0:T(8,128)(2,1)S(1)}, f32[4,96,256]{2,1,0:T(8,128)S(1)}) custom-call(s32[1,4,7]{2,1,0:T(4,128)S(1)} %get-tuple-element.27.own_cols, s32[1,4,7]{2,1,0:T(4,128)S(1)} %collective-permute-done.4.other_cols, f32[1,4,7,2,128,128]{5,4,3,2,1,0:T(8,128)} %own.7, ...), custom_call_target="tpu_custom_call" | custom-call | flops 75497472 | bytes 3670016 | tf_op jit(solution)/shard_map/prepare/pallas_call | solution.py:432
  27.1 0.0 collective-permute-done.6.swapped
  27.1 0.0 collective-permute-done.9.diagonal
  27.1 0.0 collective-permute-done.8.relayed
  27.1 1.2 %bottom.1 = f32[3,2,16,512]{3,2,1,0:T(8,128)} custom-call(f32[96,256]{1,0:T(8,128)S(1)} %collective-permute-done.6.swapped, f32[96,256]{1,0:T(8,128)S(1)} %collective-permute-done.8.relayed, f32[96,256]{1,0:T(8,128)S(1)} %collective-permute-done.9.diagonal, bf16[1,9,128,256]{3,2,1,0:T(8,128)(2,1)S(1)} %get-tuple-element.36.refs_3_.refs_0_, ...), custom_call_target="tpu_custom_call" | custom-call | flops 37748736 | bytes 917504 | tf_op jit(solution)/shard_map/bottom/pallas_call | solution.py:487
Async XLA Ops:
  0.0 10.8 %collective-permute-start.5 = (f32[1,4,7,2,128,128]{5,4,3,2,1,0:T(8,128)}, f32[1,4,7,2,128,128]{5,4,3,2,1,0:T(8,128)S(1)}, u32[]{:S(2)}, u32[]{:S(2)}) collective-permute-start(f32[1,4,7,2,128,128]{5,4,3,2,1,0:T(8,128)} %own.7), channel_id=1, source_target_pairs={{0,8},{8,0},{1,9},{9,1},{2,10},{10,2},{3,11},{11,3},{4,12},{12,4},... | collective-permute-start | bytes 11010056 | tf_op jit(solution)/shard_map/ppermute | solution.py:372
  1.5 6.0 %collective-permute-start.1 = (f32[96,256]{1,0:T(8,128)S(1)}, f32[96,256]{1,0:T(8,128)S(1)}, u32[]{:S(2)}, u32[]{:S(2)}) collective-permute-start(f32[96,256]{1,0:T(8,128)S(1)} %get-tuple-element.26.refs_0_), channel_id=1, source_target_pairs={{0,1},{2,3},{4,5},{6,7},{8,9},{10,11},{12,13},{14,15},{1,0},{3,2},... | collective-permute-start | bytes 294920 | tf_op jit(solution)/shard_map/ppermute | solution.py:365
  5.0 9.1 %collective-permute-start = (f32[96,256]{1,0:T(8,128)S(1)}, f32[96,256]{1,0:T(8,128)S(1)}, u32[]{:S(2)}, u32[]{:S(2)}) collective-permute-start(f32[96,256]{1,0:T(8,128)S(1)} %get-tuple-element.25.refs_1_), channel_id=1, source_target_pairs={{0,1},{2,3},{4,5},{6,7},{8,9},{10,11},{12,13},{14,15},{1,0},{3,2},... | collective-permute-start | bytes 294920 | tf_op jit(solution)/shard_map/ppermute | solution.py:367
  5.0 9.0 %collective-permute-start.3 = (f32[96,256]{1,0:T(8,128)S(1)}, f32[96,256]{1,0:T(8,128)S(1)}, u32[]{:S(2)}, u32[]{:S(2)}) collective-permute-start(f32[96,256]{1,0:T(8,128)S(1)} %get-tuple-element.25.refs_1_), channel_id=1, source_target_pairs={{1,2},{3,4},{5,6},{9,10},{11,12},{13,14},{0,8},{7,15},{2,1},{4,3},... | collective-permute-start | bytes 294920 | tf_op jit(solution)/shard_map/ppermute | solution.py:368
  7.5 6.6 %collective-permute-start.2 = (f32[96,256]{1,0:T(8,128)S(1)}, f32[96,256]{1,0:T(8,128)S(1)}, u32[]{:S(2)}, u32[]{:S(2)}) collective-permute-start(f32[96,256]{1,0:T(8,128)S(1)} %collective-permute-done.1.refs_2_), channel_id=1, source_target_pairs={{0,2},{2,4},{4,6},{3,1},{5,3},{7,5},{6,7},{1,0},{8,10},{10,12},{12... | collective-permute-start | bytes 294920 | tf_op jit(solution)/shard_map/ppermute | solution.py:369
  9.3 1.5 %collective-permute-start.4 = (s32[1,4,7]{2,1,0:T(4,128)}, s32[1,4,7]{2,1,0:T(4,128)S(1)}, u32[]{:S(2)}, u32[]{:S(2)}) collective-permute-start(s32[1,4,7]{2,1,0:T(4,128)} %refs_0_.1), channel_id=1, source_target_pairs={{0,8},{8,0},{1,9},{9,1},{2,10},{10,2},{3,11},{11,3},{4,12},{12,4},... | collective-permute-start | bytes 344 | tf_op jit(solution)/shard_map/ppermute | solution.py:373
  14.5 5.7 %collective-permute-start.7 = (f32[96,256]{1,0:T(8,128)S(1)}, f32[96,256]{1,0:T(8,128)S(1)}, u32[]{:S(2)}, u32[]{:S(2)}) collective-permute-start(f32[96,256]{1,0:T(8,128)S(1)} %get-tuple-element.35.refs_0_), channel_id=1, source_target_pairs={{0,1},{2,3},{4,5},{6,7},{8,9},{10,11},{12,13},{14,15},{1,0},{3,2},... | collective-permute-start | bytes 294920 | tf_op jit(solution)/shard_map/ppermute | solution.py:365
  15.1 12.0 %collective-permute-start.6 = (f32[96,256]{1,0:T(8,128)S(1)}, f32[96,256]{1,0:T(8,128)S(1)}, u32[]{:S(2)}, u32[]{:S(2)}) collective-permute-start(f32[96,256]{1,0:T(8,128)S(1)} %second_rows.1.refs_1_), channel_id=1, source_target_pairs={{0,1},{2,3},{4,5},{6,7},{8,9},{10,11},{12,13},{14,15},{1,0},{3,2},... | collective-permute-start | bytes 294920 | tf_op jit(solution)/shard_map/ppermute | solution.py:367
  17.1 10.0 %collective-permute-start.9 = (f32[96,256]{1,0:T(8,128)S(1)}, f32[96,256]{1,0:T(8,128)S(1)}, u32[]{:S(2)}, u32[]{:S(2)}) collective-permute-start(f32[96,256]{1,0:T(8,128)S(1)} %second_rows.1.refs_1_), channel_id=1, source_target_pairs={{1,2},{3,4},{5,6},{9,10},{11,12},{13,14},{0,8},{7,15},{2,1},{4,3},... | collective-permute-start | bytes 294920 | tf_op jit(solution)/shard_map/ppermute | solution.py:368
  20.2 6.9 %collective-permute-start.8 = (f32[96,256]{1,0:T(8,128)S(1)}, f32[96,256]{1,0:T(8,128)S(1)}, u32[]{:S(2)}, u32[]{:S(2)}) collective-permute-start(f32[96,256]{1,0:T(8,128)S(1)} %collective-permute-done.7.refs_2_), channel_id=1, source_target_pairs={{0,2},{2,4},{4,6},{3,1},{5,3},{7,5},{6,7},{1,0},{8,10},{10,12},{12... | collective-permute-start | bytes 294920 | tf_op jit(solution)/shard_map/ppermute | solution.py:369

commit v9 on v8

--- a/solution.py
+++ b/solution.py
@@ -53,14 +53,6 @@
     total[...] = entered(held, coef)
 
 
-def fetch_kernel(table, out, sems):
-    count = out.shape[1]
-    for i in range(count):
-        pltpu.make_async_copy(table.at[0, i], out.at[0, i], sems.at[i]).start()
-    for i in range(count):
-        pltpu.make_async_copy(table.at[0, i], out.at[0, i], sems.at[i]).wait()
-
-
 def head_and_tail(value):
     head = value.astype(jnp.bfloat16)
     return head, (value - head.astype(jnp.float32)).astype(jnp.bfloat16)
@@ -146,6 +138,19 @@
     for field in fields:
         left[:, at_lane : at_lane + field.shape[1]] = pieces(field[...])
         at_lane += field.shape[1]
+    finished = block_rows - len(rows) if halos else 0
+
+    def add_early(b, before):
+        def run(swapped_before):
+            sums[b] = before + side_product(b, 0, early[0], swapped_before, bands)
+
+        by_side(run)
+
+    if halos:
+        early[0][...] = pieces(halo[0][...])
+        for b, (n, i) in enumerate(bands.rows):
+            if n < done:
+                add_early(b, parts[n][i])
     for i, b in enumerate(rows):
         at = rows_at[i]
         copied = jnp.logical_or(here, rows_repeated[i]) if far[i] else rows_repeated[i]
@@ -194,19 +199,12 @@
             def _():
                 split_from(near.at[0, b])
 
-    finished = block_rows - len(rows) if halos else 0
-    for i, b in enumerate(rows):
         band = slice(block_rows - b, 2 * block_rows - b)
-        sums[finished + i] = product(left[...], high[i, band], low[i, band])
-    if halos:
-        early[0][...] = pieces(halo[0][...])
-
-        def run(swapped_before):
-            for b, (n, i) in enumerate(bands.rows):
-                before = parts[n][i] if n < done else sums[b]
-                sums[b] = before + side_product(b, 0, early[0], swapped_before, bands)
-
-        by_side(run)
+        own_product = product(left[...], high[i, band], low[i, band])
+        if halos:
+            add_early(b, own_product)
+        else:
+            sums[finished + i] = own_product
 
 
 class Bands:
@@ -401,20 +399,10 @@
     coefs = []
 
     def enter_second():
-        part_total, coef = enter(second_rows)
-        coefs.append(coef)
+        part_total, coef, near = enter(second_rows, (blocks, 1))
+        coefs.extend((coef, near))
         return part_total
 
-    near = pl.pallas_call(
-        fetch_kernel,
-        out_shape=jax.ShapeDtypeStruct((1, half) + blocks.shape[2:], f32),
-        in_specs=[HBM],
-        out_specs=VMEM,
-        scratch_shapes=[pltpu.SemaphoreType.DMA((half,))],
-        compiler_params=params(8),
-        cost_estimate=cost(0, 2 * blocks.size),
-        name="fetch",
-    )(in_hbm(blocks))
     first_total, coef, own_cols = enter(first_rows, (block_cols, block_rows))
     coefs.append(coef)
     second_total, early, late = exchange(first_total, enter_second)
@@ -422,7 +410,7 @@
     macs = 6 * channels * points * 2 * size
 
     every_row = range(block_rows)
-    row_groups = ((every_row,), (every_row[:1], every_row[1:half], every_row[half:]))
+    row_groups = ((every_row,), (every_row[:1], every_row[1:]))
 
     def prepare(level, rows, fields, halo, ready):
         band = jax.ShapeDtypeStruct((len(rows), 2 * block_rows + 1, size, 2 * size), bf16)
@@ -443,7 +431,7 @@
             compiler_params=params(16),
             cost_estimate=cost(2 * macs, 4 * blocks.size),
             name="prepare",
-        )(own_cols, other_cols, in_hbm(blocks), near, other_blocks, *operands)
+        )(own_cols, other_cols, in_hbm(blocks), coefs[2], other_blocks, *operands)
 
     def early_products(level, halo, *fields):
         ready = []

time: 28.5 us -> 30.1 us (1.056)
  starting transfers between devices: 9.94 us -> 13.3 us
  waiting for transfers between devices: 5.15 us -> 3.78 us
    ppermute x2, starting transfers between devices: 2.08 us -> 4.86 us  [exchange(): second_swapped = lax.ppermute(second, axes, beside)]
    ppermute x2, waiting for transfers between devices: 5.13 us -> 2.6 us  [exchange(): first_swapped = lax.ppermute(first, axes, beside)]
    pallas_call x1 -> x0, Pallas kernels: 1.47 us -> none  [per_device(): pl.pallas_call(fetch_kernel, out_shape=jax.ShapeDtypeStruct((1, half) + b...]
    ppermute x1, waiting for transfers between devices: 0.01 us -> 1.16 us  [per_device(): other_cols = lax.ppermute(block_cols, 'depth', over_depth)]
    pallas_call x4 -> x3, Pallas kernels: 7.8 us -> 8.58 us  [prepare(): pl.pallas_call(functools.partial(prepare_kernel, level, rows, len(halo),...]
    ppermute x2, starting transfers between devices: 0.45 us -> 0.95 us  [exchange(): second_diagonal = lax.ppermute(second, axes, across)]
    pallas_call x2, Pallas kernels: 1.9 us -> 2.29 us  [enter(): pl.pallas_call(functools.partial(enter_kernel, rows[0] * size, len(tables...]
  transfers between devices with their start and end apart: 10 -> 10, of which waited for: 2 -> 2; matrix products, arithmetic and copies ran while one was open for 0% -> 0% of each run, Pallas kernels for 41% -> 37%
where the time goes in v9:
time: 30.1 us; the launch traced here: 30 us
  starting transfers between devices  13.3 us (44%)
  Pallas kernels  12.8 us (43%)
  waiting for transfers between devices  3.78 us (13%)
    pallas_call x3, Pallas kernels, prepare(): pl.pallas_call(functools.partial(prepare_kernel, level, rows, len(halo),...  8.58 us
    ppermute x2, starting transfers between devices, exchange(): second_swapped = lax.ppermute(second, axes, beside)  4.86 us
    ppermute x2, starting transfers between devices, exchange(): relayed = lax.ppermute(first_swapped, axes, onward)  4.34 us
    ppermute x2, starting transfers between devices, exchange(): first_swapped = lax.ppermute(first, axes, beside)  2.62 us
    ppermute x2, waiting for transfers between devices, exchange(): first_swapped = lax.ppermute(first, axes, beside)  2.6 us
    pallas_call x2, Pallas kernels, enter(): pl.pallas_call(functools.partial(enter_kernel, rows[0] * size, len(tables...  2.29 us
    pallas_call x1, Pallas kernels, per_device(): pl.pallas_call(functools.partial(bottom_kernel, len(row_groups[1])), out_...  1.2 us
    ppermute x1, waiting for transfers between devices, per_device(): other_cols = lax.ppermute(block_cols, 'depth', over_depth)  1.16 us
  transfers between devices with their start and end apart: 10, of which 2 were waited for; matrix products, arithmetic and copies ran while one was open for 0% of the time, Pallas kernels for 37%

profile of v9, /device:TPU:0, one launch (start us, length us, event | category | flops | bytes accessed | tf_op | source)
XLA Modules:
  0.0 30.0 jit_solution(15771143507842779812)
XLA Ops:
  0.0 0.0 copy-start
  0.0 0.5 %collective-permute-start.5 = (f32[1,4,7,2,128,128]{5,4,3,2,1,0:T(8,128)}, f32[1,4,7,2,128,128]{5,4,3,2,1,0:T(8,128)S(1)}, u32[]{:S(2)}, u32[]{:S(2)}) collective-permute-start(f32[1,4,7,2,128,128]{5,4,3,2,1,0:T(8,128)} %own.5), channel_id=1, source_target_pairs={{0,8},{8,0},{1,9},{9,1},{2,10},{10,2},{3,11},{11,3},{4,12},{12,4},... | collective-permute-start | bytes 11010056 | tf_op jit(solution)/shard_map/ppermute | solution.py:370
  0.5 1.0 %enter.3 = (f32[96,256]{1,0:T(8,128)S(1)}, f32[2,256]{1,0:T(2,128)S(1)}, s32[1,4,7]{2,1,0:T(4,128)S(1)}) custom-call(f32[3,2,16,512]{3,2,1,0:T(8,128)} %sources.3, s32[1,512]{1,0:T(1,128)} %bitcast.1, f32[2,512]{1,0:T(2,128)} %refl_coef.3, s32[1,4,7]{2,1,0:T(4,128)} %refs_0_.3), custom_call_target="tpu_custom_call" | custom-call | tf_op jit(solution)/shard_map/enter/pallas_call | solution.py:376
  1.5 2.6 %collective-permute-start.1 = (f32[96,256]{1,0:T(8,128)S(1)}, f32[96,256]{1,0:T(8,128)S(1)}, u32[]{:S(2)}, u32[]{:S(2)}) collective-permute-start(f32[96,256]{1,0:T(8,128)S(1)} %get-tuple-element.24.refs_0_), channel_id=1, source_target_pairs={{0,1},{2,3},{4,5},{6,7},{8,9},{10,11},{12,13},{14,15},{1,0},{3,2},... | collective-permute-start | bytes 294920 | tf_op jit(solution)/shard_map/ppermute | solution.py:363
  4.0 1.3 %enter.2 = (f32[96,256]{1,0:T(8,128)S(1)}, f32[2,256]{1,0:T(2,128)S(1)}, f32[1,1,7,2,128,128]{5,4,3,2,1,0:T(8,128)S(1)}) custom-call(f32[3,2,16,512]{3,2,1,0:T(8,128)} %sources.3, s32[1,512]{1,0:T(1,128)} %bitcast.2, f32[2,512]{1,0:T(2,128)} %refl_coef.3, f32[1,4,7,2,128,128]{5,4,3,2,1,0:T(8,128)} %own.5), custom_call_target="tpu_custom_call" | custom-call | tf_op jit(solution)/shard_map/enter/pallas_call | solution.py:376
  5.4 0.3 collective-permute-start.3
  5.6 2.8 %collective-permute-start = (f32[96,256]{1,0:T(8,128)S(1)}, f32[96,256]{1,0:T(8,128)S(1)}, u32[]{:S(2)}, u32[]{:S(2)}) collective-permute-start(f32[96,256]{1,0:T(8,128)S(1)} %get-tuple-element.23.refs_1_), channel_id=1, source_target_pairs={{0,1},{2,3},{4,5},{6,7},{8,9},{10,11},{12,13},{14,15},{1,0},{3,2},... | collective-permute-start | bytes 294920 | tf_op jit(solution)/shard_map/ppermute | solution.py:365
  8.5 0.0 collective-permute-done.1.refs_2_
  8.5 1.6 %collective-permute-start.2 = (f32[96,256]{1,0:T(8,128)S(1)}, f32[96,256]{1,0:T(8,128)S(1)}, u32[]{:S(2)}, u32[]{:S(2)}) collective-permute-start(f32[96,256]{1,0:T(8,128)S(1)} %collective-permute-done.1.refs_2_), channel_id=1, source_target_pairs={{0,2},{2,4},{4,6},{3,1},{5,3},{7,5},{6,7},{1,0},{8,10},{10,12},{12... | collective-permute-start | bytes 294920 | tf_op jit(solution)/shard_map/ppermute | solution.py:367
  10.0 0.0 copy-done
  10.0 0.0 collective-permute-start.4
  10.0 1.2 %collective-permute-done.4.other_cols = s32[1,4,7]{2,1,0:T(4,128)S(1)} collective-permute-done((s32[1,4,7]{2,1,0:T(4,128)S(1)}, s32[1,4,7]{2,1,0:T(4,128)S(1)}, u32[]{:S(2)}, u32[]{:S(2)}) %collective-permute-start.4) | collective-permute-done | bytes 144 | tf_op jit(solution)/shard_map/ppermute | solution.py:371
  11.2 0.0 collective-permute-done.5.received
  11.2 4.0 %prepare.3 = (bf16[4,9,128,256]{3,2,1,0:T(8,128)(2,1)S(1)}, bf16[4,9,128,256]{3,2,1,0:T(8,128)(2,1)S(1)}, f32[4,96,256]{2,1,0:T(8,128)S(1)}) custom-call(s32[1,4,7]{2,1,0:T(4,128)S(1)} %get-tuple-element.25.own_cols, s32[1,4,7]{2,1,0:T(4,128)S(1)} %collective-permute-done.4.other_cols, f32[1,4,7,2,128,128]{5,4,3,2,1,0:T(8,128)} %own.5, ...), custom_call_target="tpu_custom_call" | custom-call | flops 75497472 | bytes 3670016 | tf_op jit(solution)/shard_map/prepare/pallas_call | solution.py:420
  15.2 0.0 collective-permute-done.3.diagonal
  15.2 0.0 collective-permute-done.swapped
  15.2 0.0 collective-permute-done.2.relayed
  15.2 0.4 %first_rows.1 = (f32[96,256]{1,0:T(8,128)S(1)}, bf16[192,256]{1,0:T(8,128)(2,1)S(1)}, bf16[192,512]{1,0:T(8,128)(2,1)S(1)}) custom-call(f32[96,256]{1,0:T(8,128)S(1)} %collective-permute-done.swapped, f32[96,256]{1,0:T(8,128)S(1)} %collective-permute-done.2.relayed, f32[96,256]{1,0:T(8,128)S(1)} %collective-permute-done.3.diagonal, ...), custom_call_target="tpu_custom_call" | custom-call | flops 37748736 | bytes 917504 | tf_op jit(solution)/shard_map/first_rows/pallas_call | solution.py:448
  15.6 0.1 collective-permute-start.7
  15.7 0.3 %second_rows.1.refs_1_ = f32[96,256]{1,0:T(8,128)S(1)} custom-call(bf16[192,256]{1,0:T(8,128)(2,1)S(1)} %get-tuple-element.31.swapped, bf16[192,512]{1,0:T(8,128)(2,1)S(1)} %get-tuple-element.32.diagonal, bf16[4,9,128,256]{3,2,1,0:T(8,128)(2,1)S(1)} %get-tuple-element.27.refs_0_, bf16[4,9,128,256]{3,2,1,0:T(8,128)(2,1)S(1)} %get-tuple-element.28.refs_1_, ...), custom_call_target="tpu_custom_call" | custom-call | flops 37748736 | bytes 917504 | tf_op jit(solution)/shard_map/second_rows/pallas_call | solution.py:463
  16.0 0.7 %collective-permute-start.9 = (f32[96,256]{1,0:T(8,128)S(1)}, f32[96,256]{1,0:T(8,128)S(1)}, u32[]{:S(2)}, u32[]{:S(2)}) collective-permute-start(f32[96,256]{1,0:T(8,128)S(1)} %second_rows.1.refs_1_), channel_id=1, source_target_pairs={{1,2},{3,4},{5,6},{9,10},{11,12},{13,14},{0,8},{7,15},{2,1},{4,3},... | collective-permute-start | bytes 294920 | tf_op jit(solution)/shard_map/ppermute | solution.py:366
  16.7 2.0 %collective-permute-start.6 = (f32[96,256]{1,0:T(8,128)S(1)}, f32[96,256]{1,0:T(8,128)S(1)}, u32[]{:S(2)}, u32[]{:S(2)}) collective-permute-start(f32[96,256]{1,0:T(8,128)S(1)} %second_rows.1.refs_1_), channel_id=1, source_target_pairs={{0,1},{2,3},{4,5},{6,7},{8,9},{10,11},{12,13},{14,15},{1,0},{3,2},... | collective-permute-start | bytes 294920 | tf_op jit(solution)/shard_map/ppermute | solution.py:365
  18.7 2.6 %collective-permute-done.7.refs_2_ = f32[96,256]{1,0:T(8,128)S(1)} collective-permute-done((f32[96,256]{1,0:T(8,128)S(1)}, f32[96,256]{1,0:T(8,128)S(1)}, u32[]{:S(2)}, u32[]{:S(2)}) %collective-permute-start.7) | collective-permute-done | bytes 98336 | tf_op jit(solution)/shard_map/ppermute | solution.py:363
  21.3 2.8 %collective-permute-start.8 = (f32[96,256]{1,0:T(8,128)S(1)}, f32[96,256]{1,0:T(8,128)S(1)}, u32[]{:S(2)}, u32[]{:S(2)}) collective-permute-start(f32[96,256]{1,0:T(8,128)S(1)} %collective-permute-done.7.refs_2_), channel_id=1, source_target_pairs={{0,2},{2,4},{4,6},{3,1},{5,3},{7,5},{6,7},{1,0},{8,10},{10,12},{12... | collective-permute-start | bytes 294920 | tf_op jit(solution)/shard_map/ppermute | solution.py:367
  24.1 1.4 %prepare.4 = (bf16[1,9,128,256]{3,2,1,0:T(8,128)(2,1)S(1)}, bf16[1,9,128,256]{3,2,1,0:T(8,128)(2,1)S(1)}, f32[1,96,256]{2,1,0:T(8,128)S(1)}) custom-call(s32[1,4,7]{2,1,0:T(4,128)S(1)} %get-tuple-element.25.own_cols, s32[1,4,7]{2,1,0:T(4,128)S(1)} %collective-permute-done.4.other_cols, f32[1,4,7,2,128,128]{5,4,3,2,1,0:T(8,128)} %own.5, ...), custom_call_target="tpu_custom_call" | custom-call | flops 75497472 | bytes 3670016 | tf_op jit(solution)/shard_map/prepare/pallas_call | solution.py:420
  25.6 3.1 %prepare.5 = (bf16[3,9,128,256]{3,2,1,0:T(8,128)(2,1)S(1)}, bf16[3,9,128,256]{3,2,1,0:T(8,128)(2,1)S(1)}, f32[4,96,256]{2,1,0:T(8,128)S(1)}) custom-call(s32[1,4,7]{2,1,0:T(4,128)S(1)} %get-tuple-element.25.own_cols, s32[1,4,7]{2,1,0:T(4,128)S(1)} %collective-permute-done.4.other_cols, f32[1,4,7,2,128,128]{5,4,3,2,1,0:T(8,128)} %own.5, ...), custom_call_target="tpu_custom_call" | custom-call | flops 75497472 | bytes 3670016 | tf_op jit(solution)/shard_map/prepare/pallas_call | solution.py:420
  28.7 0.0 collective-permute-done.9.diagonal
  28.7 0.0 collective-permute-done.6.swapped
  28.7 0.0 collective-permute-done.8.relayed
  28.8 1.2 %bottom.1 = f32[3,2,16,512]{3,2,1,0:T(8,128)} custom-call(f32[96,256]{1,0:T(8,128)S(1)} %collective-permute-done.6.swapped, f32[96,256]{1,0:T(8,128)S(1)} %collective-permute-done.8.relayed, f32[96,256]{1,0:T(8,128)S(1)} %collective-permute-done.9.diagonal, bf16[1,9,128,256]{3,2,1,0:T(8,128)(2,1)S(1)} %get-tuple-element.35.refs_3_.refs_0_, ...), custom_call_target="tpu_custom_call" | custom-call | flops 37748736 | bytes 917504 | tf_op jit(solution)/shard_map/bottom/pallas_call | solution.py:475
Async XLA Ops:
  0.0 10.0 %copy-start = (s32[1,4,7]{2,1,0:T(4,128)S(1)}, s32[1,4,7]{2,1,0:T(4,128)}, u32[]{:S(2)}) copy-start(s32[1,4,7]{2,1,0:T(4,128)} %refs_0_.3) | copy-start | bytes 340
  0.0 11.2 %collective-permute-start.5 = (f32[1,4,7,2,128,128]{5,4,3,2,1,0:T(8,128)}, f32[1,4,7,2,128,128]{5,4,3,2,1,0:T(8,128)S(1)}, u32[]{:S(2)}, u32[]{:S(2)}) collective-permute-start(f32[1,4,7,2,128,128]{5,4,3,2,1,0:T(8,128)} %own.5), channel_id=1, source_target_pairs={{0,8},{8,0},{1,9},{9,1},{2,10},{10,2},{3,11},{11,3},{4,12},{12,4},... | collective-permute-start | bytes 11010056 | tf_op jit(solution)/shard_map/ppermute | solution.py:370
  1.5 7.0 %collective-permute-start.1 = (f32[96,256]{1,0:T(8,128)S(1)}, f32[96,256]{1,0:T(8,128)S(1)}, u32[]{:S(2)}, u32[]{:S(2)}) collective-permute-start(f32[96,256]{1,0:T(8,128)S(1)} %get-tuple-element.24.refs_0_), channel_id=1, source_target_pairs={{0,1},{2,3},{4,5},{6,7},{8,9},{10,11},{12,13},{14,15},{1,0},{3,2},... | collective-permute-start | bytes 294920 | tf_op jit(solution)/shard_map/ppermute | solution.py:363
  5.4 9.8 %collective-permute-start.3 = (f32[96,256]{1,0:T(8,128)S(1)}, f32[96,256]{1,0:T(8,128)S(1)}, u32[]{:S(2)}, u32[]{:S(2)}) collective-permute-start(f32[96,256]{1,0:T(8,128)S(1)} %get-tuple-element.23.refs_1_), channel_id=1, source_target_pairs={{1,2},{3,4},{5,6},{9,10},{11,12},{13,14},{0,8},{7,15},{2,1},{4,3},... | collective-permute-start | bytes 294920 | tf_op jit(solution)/shard_map/ppermute | solution.py:366
  5.6 9.6 %collective-permute-start = (f32[96,256]{1,0:T(8,128)S(1)}, f32[96,256]{1,0:T(8,128)S(1)}, u32[]{:S(2)}, u32[]{:S(2)}) collective-permute-start(f32[96,256]{1,0:T(8,128)S(1)} %get-tuple-element.23.refs_1_), channel_id=1, source_target_pairs={{0,1},{2,3},{4,5},{6,7},{8,9},{10,11},{12,13},{14,15},{1,0},{3,2},... | collective-permute-start | bytes 294920 | tf_op jit(solution)/shard_map/ppermute | solution.py:365
  8.5 6.8 %collective-permute-start.2 = (f32[96,256]{1,0:T(8,128)S(1)}, f32[96,256]{1,0:T(8,128)S(1)}, u32[]{:S(2)}, u32[]{:S(2)}) collective-permute-start(f32[96,256]{1,0:T(8,128)S(1)} %collective-permute-done.1.refs_2_), channel_id=1, source_target_pairs={{0,2},{2,4},{4,6},{3,1},{5,3},{7,5},{6,7},{1,0},{8,10},{10,12},{12... | collective-permute-start | bytes 294920 | tf_op jit(solution)/shard_map/ppermute | solution.py:367
  10.0 1.2 %collective-permute-start.4 = (s32[1,4,7]{2,1,0:T(4,128)S(1)}, s32[1,4,7]{2,1,0:T(4,128)S(1)}, u32[]{:S(2)}, u32[]{:S(2)}) collective-permute-start(s32[1,4,7]{2,1,0:T(4,128)S(1)} %copy-done), channel_id=1, source_target_pairs={{0,8},{8,0},{1,9},{9,1},{2,10},{10,2},{3,11},{11,3},{4,12},{12,4},... | collective-permute-start | bytes 344 | tf_op jit(solution)/shard_map/ppermute | solution.py:371
  15.6 5.7 %collective-permute-start.7 = (f32[96,256]{1,0:T(8,128)S(1)}, f32[96,256]{1,0:T(8,128)S(1)}, u32[]{:S(2)}, u32[]{:S(2)}) collective-permute-start(f32[96,256]{1,0:T(8,128)S(1)} %get-tuple-element.34.refs_0_), channel_id=1, source_target_pairs={{0,1},{2,3},{4,5},{6,7},{8,9},{10,11},{12,13},{14,15},{1,0},{3,2},... | collective-permute-start | bytes 294920 | tf_op jit(solution)/shard_map/ppermute | solution.py:363
  16.0 12.7 %collective-permute-start.9 = (f32[96,256]{1,0:T(8,128)S(1)}, f32[96,256]{1,0:T(8,128)S(1)}, u32[]{:S(2)}, u32[]{:S(2)}) collective-permute-start(f32[96,256]{1,0:T(8,128)S(1)} %second_rows.1.refs_1_), channel_id=1, source_target_pairs={{1,2},{3,4},{5,6},{9,10},{11,12},{13,14},{0,8},{7,15},{2,1},{4,3},... | collective-permute-start | bytes 294920 | tf_op jit(solution)/shard_map/ppermute | solution.py:366
  16.7 12.0 %collective-permute-start.6 = (f32[96,256]{1,0:T(8,128)S(1)}, f32[96,256]{1,0:T(8,128)S(1)}, u32[]{:S(2)}, u32[]{:S(2)}) collective-permute-start(f32[96,256]{1,0:T(8,128)S(1)} %second_rows.1.refs_1_), channel_id=1, source_target_pairs={{0,1},{2,3},{4,5},{6,7},{8,9},{10,11},{12,13},{14,15},{1,0},{3,2},... | collective-permute-start | bytes 294920 | tf_op jit(solution)/shard_map/ppermute | solution.py:365
  21.3 7.4 %collective-permute-start.8 = (f32[96,256]{1,0:T(8,128)S(1)}, f32[96,256]{1,0:T(8,128)S(1)}, u32[]{:S(2)}, u32[]{:S(2)}) collective-permute-start(f32[96,256]{1,0:T(8,128)S(1)} %collective-permute-done.7.refs_2_), channel_id=1, source_target_pairs={{0,2},{2,4},{4,6},{3,1},{5,3},{7,5},{6,7},{1,0},{8,10},{10,12},{12... | collective-permute-start | bytes 294920 | tf_op jit(solution)/shard_map/ppermute | solution.py:367

commit v10 on v8

--- a/solution.py
+++ b/solution.py
@@ -53,14 +53,6 @@
     total[...] = entered(held, coef)
 
 
-def fetch_kernel(table, out, sems):
-    count = out.shape[1]
-    for i in range(count):
-        pltpu.make_async_copy(table.at[0, i], out.at[0, i], sems.at[i]).start()
-    for i in range(count):
-        pltpu.make_async_copy(table.at[0, i], out.at[0, i], sems.at[i]).wait()
-
-
 def head_and_tail(value):
     head = value.astype(jnp.bfloat16)
     return head, (value - head.astype(jnp.float32)).astype(jnp.bfloat16)
@@ -121,9 +113,6 @@
         repeated = sum(bits) != present
         rows_at.append(at)
         rows_repeated.append(repeated)
-        start(jnp.logical_and(other, repeated), received, i, b)
-        if not far[i]:
-            start(jnp.logical_and(here, repeated), near, i, b)
         absent = (1 << span) - 1 - present
         lowest = sum(jnp.where(absent % (2 << o) == 0, 1, 0) for o in range(span - 1))
         highest = sum(jnp.where(absent >= (2 << o), 1, 0) for o in range(span - 1))
@@ -148,27 +137,31 @@
         at_lane += field.shape[1]
     for i, b in enumerate(rows):
         at = rows_at[i]
-        copied = jnp.logical_or(here, rows_repeated[i]) if far[i] else rows_repeated[i]
-
-        @pl.when(copied)
-        def _():
-            pltpu.make_async_copy(received.at[0, b], held.at[i], sems.at[i]).wait()
-
-        @pl.when(rows_repeated[i])
-        def _():
+        repeats = [
+            functools.reduce(jnp.logical_or, [a == at[j] for a in at[j + 1 :]])
+            for j in range(per_row - 1)
+        ]
+
+        def merge(blocks):
             for j in reversed(range(1, per_row)):
                 target = jnp.int32(per_row)
                 for k in range(j):
                     target = jnp.where(at[k] == at[j], k, target)
-
-                @pl.when(target < per_row)
+                found = target < per_row
+                again = repeats[j] if j < per_row - 1 else False
+
+                @pl.when(jnp.logical_and(found, again))
                 def _():
-                    held[i, target] = held[i, target] + held[i, j]
-
-        def split_from(blocks):
+                    held[i, target] = blocks[target] + held[i, j]
+
+                @pl.when(jnp.logical_and(found, jnp.logical_not(again)))
+                def _():
+                    held[i, target] = blocks[target] + blocks[j]
+
+        def split_from(blocks, entries):
             def split(n, carry):
                 part = pl.ds(pl.multiple_of(n * 16, 16), 16)
-                for j in reversed(range(per_row)):
+                for j in entries:
                     head, tail = head_and_tail(
                         jnp.concatenate([blocks[j, 0, part], blocks[j, 1, part]], axis=1)
                     )
@@ -178,21 +171,30 @@
 
             lax.fori_loop(0, size // 16, split, 0, unroll=2)
 
-        direct = jnp.logical_not(copied)
-
-        @pl.when(copied)
+        def take_row(blocks):
+            split_from(blocks, range(per_row)[::-1])
+
+            @pl.when(rows_repeated[i])
+            def _():
+                merge(blocks)
+                for j in reversed(range(per_row - 1)):
+
+                    @pl.when(repeats[j])
+                    def _():
+                        split_from(held.at[i], (j,))
+
+        @pl.when(here)
         def _():
-            split_from(held.at[i])
-
-        @pl.when(jnp.logical_and(direct, other))
+            if far[i]:
+                pltpu.make_async_copy(own.at[0, b], held.at[i], sems.at[i]).wait()
+                pl.when(rows_repeated[i])(functools.partial(merge, held.at[i]))
+                split_from(held.at[i], range(per_row)[::-1])
+            else:
+                take_row(near.at[0, b])
+
+        @pl.when(other)
         def _():
-            split_from(received.at[0, b])
-
-        if not far[i]:
-
-            @pl.when(jnp.logical_and(direct, here))
-            def _():
-                split_from(near.at[0, b])
+            take_row(received.at[0, b])
 
     finished = block_rows - len(rows) if halos else 0
     for i, b in enumerate(rows):
@@ -401,20 +403,10 @@
     coefs = []
 
     def enter_second():
-        part_total, coef = enter(second_rows)
-        coefs.append(coef)
+        part_total, coef, near = enter(second_rows, (blocks, 1))
+        coefs.extend((coef, near))
         return part_total
 
-    near = pl.pallas_call(
-        fetch_kernel,
-        out_shape=jax.ShapeDtypeStruct((1, half) + blocks.shape[2:], f32),
-        in_specs=[HBM],
-        out_specs=VMEM,
-        scratch_shapes=[pltpu.SemaphoreType.DMA((half,))],
-        compiler_params=params(8),
-        cost_estimate=cost(0, 2 * blocks.size),
-        name="fetch",
-    )(in_hbm(blocks))
     first_total, coef, own_cols = enter(first_rows, (block_cols, block_rows))
     coefs.append(coef)
     second_total, early, late = exchange(first_total, enter_second)
@@ -422,7 +414,7 @@
     macs = 6 * channels * points * 2 * size
 
     every_row = range(block_rows)
-    row_groups = ((every_row,), (every_row[:1], every_row[1:half], every_row[half:]))
+    row_groups = ((every_row,), (every_row[:1], every_row[1:]))
 
     def prepare(level, rows, fields, halo, ready):
         band = jax.ShapeDtypeStruct((len(rows), 2 * block_rows + 1, size, 2 * size), bf16)
@@ -443,7 +435,7 @@
             compiler_params=params(16),
             cost_estimate=cost(2 * macs, 4 * blocks.size),
             name="prepare",
-        )(own_cols, other_cols, in_hbm(blocks), near, other_blocks, *operands)
+        )(own_cols, other_cols, in_hbm(blocks), coefs[2], other_blocks, *operands)
 
     def early_products(level, halo, *fields):
         ready = []

time: 28.5 us -> 28.6 us (level)
  starting transfers between devices: 9.94 us -> 14 us
  Pallas kernels: 13.1 us -> 11.1 us
  waiting for transfers between devices: 5.15 us -> 3.22 us
    ppermute x2, starting transfers between devices: 2.08 us -> 5.49 us  [exchange(): second_swapped = lax.ppermute(second, axes, beside)]
    ppermute x2, waiting for transfers between devices: 5.13 us -> 2.04 us  [exchange(): first_swapped = lax.ppermute(first, axes, beside)]
    pallas_call x1 -> x0, Pallas kernels: 1.47 us -> none  [per_device(): pl.pallas_call(fetch_kernel, out_shape=jax.ShapeDtypeStruct((1, half) + b...]
    ppermute x1, waiting for transfers between devices: 0.01 us -> 1.16 us  [per_device(): other_cols = lax.ppermute(block_cols, 'depth', over_depth)]
    pallas_call x4 -> x3, Pallas kernels: 7.8 us -> 6.9 us  [prepare(): pl.pallas_call(functools.partial(prepare_kernel, level, rows, len(halo),...]
    ppermute x2, starting transfers between devices: 4.12 us -> 4.69 us  [exchange(): relayed = lax.ppermute(first_swapped, axes, onward)]
    pallas_call x2, Pallas kernels: 1.9 us -> 2.29 us  [enter(): pl.pallas_call(functools.partial(enter_kernel, rows[0] * size, len(tables...]
  transfers between devices with their start and end apart: 10 -> 10, of which waited for: 2 -> 2; matrix products, arithmetic and copies ran while one was open for 0% -> 0% of each run, Pallas kernels for 41% -> 33%
where the time goes in v10:
time: 28.6 us; the launch traced here: 28.4 us
  starting transfers between devices  14 us (49%)
  Pallas kernels  11.1 us (39%)
  waiting for transfers between devices  3.22 us (11%)
    pallas_call x3, Pallas kernels, prepare(): pl.pallas_call(functools.partial(prepare_kernel, level, rows, len(halo),...  6.9 us
    ppermute x2, starting transfers between devices, exchange(): second_swapped = lax.ppermute(second, axes, beside)  5.49 us
    ppermute x2, starting transfers between devices, exchange(): relayed = lax.ppermute(first_swapped, axes, onward)  4.69 us
    ppermute x2, starting transfers between devices, exchange(): first_swapped = lax.ppermute(first, axes, beside)  2.96 us
    pallas_call x2, Pallas kernels, enter(): pl.pallas_call(functools.partial(enter_kernel, rows[0] * size, len(tables...  2.29 us
    ppermute x2, waiting for transfers between devices, exchange(): first_swapped = lax.ppermute(first, axes, beside)  2.04 us
    pallas_call x1, Pallas kernels, per_device(): pl.pallas_call(functools.partial(bottom_kernel, len(row_groups[1])), out_...  1.2 us
    ppermute x1, waiting for transfers between devices, per_device(): other_cols = lax.ppermute(block_cols, 'depth', over_depth)  1.16 us
  transfers between devices with their start and end apart: 10, of which 2 were waited for; matrix products, arithmetic and copies ran while one was open for 0% of the time, Pallas kernels for 33%

profile of v10, /device:TPU:0, one launch (start us, length us, event | category | flops | bytes accessed | tf_op | source)
XLA Modules:
  0.0 28.4 jit_solution(12728688776455700643)
XLA Ops:
  0.0 0.0 copy-start
  0.0 0.5 %collective-permute-start.5 = (f32[1,4,7,2,128,128]{5,4,3,2,1,0:T(8,128)}, f32[1,4,7,2,128,128]{5,4,3,2,1,0:T(8,128)S(1)}, u32[]{:S(2)}, u32[]{:S(2)}) collective-permute-start(f32[1,4,7,2,128,128]{5,4,3,2,1,0:T(8,128)} %own.5), channel_id=1, source_target_pairs={{0,8},{8,0},{1,9},{9,1},{2,10},{10,2},{3,11},{11,3},{4,12},{12,4},... | collective-permute-start | bytes 11010056 | tf_op jit(solution)/shard_map/ppermute | solution.py:374
  0.5 1.0 %enter.3 = (f32[96,256]{1,0:T(8,128)S(1)}, f32[2,256]{1,0:T(2,128)S(1)}, s32[1,4,7]{2,1,0:T(4,128)S(1)}) custom-call(f32[3,2,16,512]{3,2,1,0:T(8,128)} %sources.3, s32[1,512]{1,0:T(1,128)} %bitcast.1, f32[2,512]{1,0:T(2,128)} %refl_coef.3, s32[1,4,7]{2,1,0:T(4,128)} %refs_0_.3), custom_call_target="tpu_custom_call" | custom-call | tf_op jit(solution)/shard_map/enter/pallas_call | solution.py:380
  1.5 2.6 %collective-permute-start.1 = (f32[96,256]{1,0:T(8,128)S(1)}, f32[96,256]{1,0:T(8,128)S(1)}, u32[]{:S(2)}, u32[]{:S(2)}) collective-permute-start(f32[96,256]{1,0:T(8,128)S(1)} %get-tuple-element.24.refs_0_), channel_id=1, source_target_pairs={{0,1},{2,3},{4,5},{6,7},{8,9},{10,11},{12,13},{14,15},{1,0},{3,2},... | collective-permute-start | bytes 294920 | tf_op jit(solution)/shard_map/ppermute | solution.py:367
  4.0 1.3 %enter.2 = (f32[96,256]{1,0:T(8,128)S(1)}, f32[2,256]{1,0:T(2,128)S(1)}, f32[1,1,7,2,128,128]{5,4,3,2,1,0:T(8,128)S(1)}) custom-call(f32[3,2,16,512]{3,2,1,0:T(8,128)} %sources.3, s32[1,512]{1,0:T(1,128)} %bitcast.2, f32[2,512]{1,0:T(2,128)} %refl_coef.3, f32[1,4,7,2,128,128]{5,4,3,2,1,0:T(8,128)} %own.5), custom_call_target="tpu_custom_call" | custom-call | tf_op jit(solution)/shard_map/enter/pallas_call | solution.py:380
  5.4 0.3 collective-permute-start.3
  5.6 2.8 %collective-permute-start = (f32[96,256]{1,0:T(8,128)S(1)}, f32[96,256]{1,0:T(8,128)S(1)}, u32[]{:S(2)}, u32[]{:S(2)}) collective-permute-start(f32[96,256]{1,0:T(8,128)S(1)} %get-tuple-element.23.refs_1_), channel_id=1, source_target_pairs={{0,1},{2,3},{4,5},{6,7},{8,9},{10,11},{12,13},{14,15},{1,0},{3,2},... | collective-permute-start | bytes 294920 | tf_op jit(solution)/shard_map/ppermute | solution.py:369
  8.5 0.0 collective-permute-done.1.refs_2_
  8.5 1.6 %collective-permute-start.2 = (f32[96,256]{1,0:T(8,128)S(1)}, f32[96,256]{1,0:T(8,128)S(1)}, u32[]{:S(2)}, u32[]{:S(2)}) collective-permute-start(f32[96,256]{1,0:T(8,128)S(1)} %collective-permute-done.1.refs_2_), channel_id=1, source_target_pairs={{0,2},{2,4},{4,6},{3,1},{5,3},{7,5},{6,7},{1,0},{8,10},{10,12},{12... | collective-permute-start | bytes 294920 | tf_op jit(solution)/shard_map/ppermute | solution.py:371
  10.0 0.0 copy-done
  10.0 0.0 collective-permute-start.4
  10.0 1.2 %collective-permute-done.4.other_cols = s32[1,4,7]{2,1,0:T(4,128)S(1)} collective-permute-done((s32[1,4,7]{2,1,0:T(4,128)S(1)}, s32[1,4,7]{2,1,0:T(4,128)S(1)}, u32[]{:S(2)}, u32[]{:S(2)}) %collective-permute-start.4) | collective-permute-done | bytes 144 | tf_op jit(solution)/shard_map/ppermute | solution.py:375
  11.2 0.0 collective-permute-done.5.received
  11.2 3.4 %prepare.3 = (bf16[4,9,128,256]{3,2,1,0:T(8,128)(2,1)S(1)}, bf16[4,9,128,256]{3,2,1,0:T(8,128)(2,1)S(1)}, f32[4,96,256]{2,1,0:T(8,128)S(1)}) custom-call(s32[1,4,7]{2,1,0:T(4,128)S(1)} %get-tuple-element.25.own_cols, s32[1,4,7]{2,1,0:T(4,128)S(1)} %collective-permute-done.4.other_cols, f32[1,4,7,2,128,128]{5,4,3,2,1,0:T(8,128)} %own.5, ...), custom_call_target="tpu_custom_call" | custom-call | flops 75497472 | bytes 3670016 | tf_op jit(solution)/shard_map/prepare/pallas_call | solution.py:424
  14.6 0.0 collective-permute-done.3.diagonal
  14.6 0.0 collective-permute-done.swapped
  14.6 0.0 collective-permute-done.2.relayed
  14.6 0.4 %first_rows.1 = (f32[96,256]{1,0:T(8,128)S(1)}, bf16[192,256]{1,0:T(8,128)(2,1)S(1)}, bf16[192,512]{1,0:T(8,128)(2,1)S(1)}) custom-call(f32[96,256]{1,0:T(8,128)S(1)} %collective-permute-done.swapped, f32[96,256]{1,0:T(8,128)S(1)} %collective-permute-done.2.relayed, f32[96,256]{1,0:T(8,128)S(1)} %collective-permute-done.3.diagonal, ...), custom_call_target="tpu_custom_call" | custom-call | flops 37748736 | bytes 917504 | tf_op jit(solution)/shard_map/first_rows/pallas_call | solution.py:452
  15.0 0.4 %collective-permute-start.7 = (f32[96,256]{1,0:T(8,128)S(1)}, f32[96,256]{1,0:T(8,128)S(1)}, u32[]{:S(2)}, u32[]{:S(2)}) collective-permute-start(f32[96,256]{1,0:T(8,128)S(1)} %get-tuple-element.34.refs_0_), channel_id=1, source_target_pairs={{0,1},{2,3},{4,5},{6,7},{8,9},{10,11},{12,13},{14,15},{1,0},{3,2},... | collective-permute-start | bytes 294920 | tf_op jit(solution)/shard_map/ppermute | solution.py:367
  15.4 0.3 %second_rows.1.refs_1_ = f32[96,256]{1,0:T(8,128)S(1)} custom-call(bf16[192,256]{1,0:T(8,128)(2,1)S(1)} %get-tuple-element.31.swapped, bf16[192,512]{1,0:T(8,128)(2,1)S(1)} %get-tuple-element.32.diagonal, bf16[4,9,128,256]{3,2,1,0:T(8,128)(2,1)S(1)} %get-tuple-element.27.refs_0_, bf16[4,9,128,256]{3,2,1,0:T(8,128)(2,1)S(1)} %get-tuple-element.28.refs_1_, ...), custom_call_target="tpu_custom_call" | custom-call | flops 37748736 | bytes 917504 | tf_op jit(solution)/shard_map/second_rows/pallas_call | solution.py:467
  15.7 0.1 collective-permute-start.9
  15.8 2.7 %collective-permute-start.6 = (f32[96,256]{1,0:T(8,128)S(1)}, f32[96,256]{1,0:T(8,128)S(1)}, u32[]{:S(2)}, u32[]{:S(2)}) collective-permute-start(f32[96,256]{1,0:T(8,128)S(1)} %second_rows.1.refs_1_), channel_id=1, source_target_pairs={{0,1},{2,3},{4,5},{6,7},{8,9},{10,11},{12,13},{14,15},{1,0},{3,2},... | collective-permute-start | bytes 294920 | tf_op jit(solution)/shard_map/ppermute | solution.py:369
  18.5 2.0 %collective-permute-done.7.refs_2_ = f32[96,256]{1,0:T(8,128)S(1)} collective-permute-done((f32[96,256]{1,0:T(8,128)S(1)}, f32[96,256]{1,0:T(8,128)S(1)}, u32[]{:S(2)}, u32[]{:S(2)}) %collective-permute-start.7) | collective-permute-done | bytes 98336 | tf_op jit(solution)/shard_map/ppermute | solution.py:367
  20.5 3.1 %collective-permute-start.8 = (f32[96,256]{1,0:T(8,128)S(1)}, f32[96,256]{1,0:T(8,128)S(1)}, u32[]{:S(2)}, u32[]{:S(2)}) collective-permute-start(f32[96,256]{1,0:T(8,128)S(1)} %collective-permute-done.7.refs_2_), channel_id=1, source_target_pairs={{0,2},{2,4},{4,6},{3,1},{5,3},{7,5},{6,7},{1,0},{8,10},{10,12},{12... | collective-permute-start | bytes 294920 | tf_op jit(solution)/shard_map/ppermute | solution.py:371
  23.6 1.3 %prepare.4 = (bf16[1,9,128,256]{3,2,1,0:T(8,128)(2,1)S(1)}, bf16[1,9,128,256]{3,2,1,0:T(8,128)(2,1)S(1)}, f32[1,96,256]{2,1,0:T(8,128)S(1)}) custom-call(s32[1,4,7]{2,1,0:T(4,128)S(1)} %get-tuple-element.25.own_cols, s32[1,4,7]{2,1,0:T(4,128)S(1)} %collective-permute-done.4.other_cols, f32[1,4,7,2,128,128]{5,4,3,2,1,0:T(8,128)} %own.5, ...), custom_call_target="tpu_custom_call" | custom-call | flops 75497472 | bytes 3670016 | tf_op jit(solution)/shard_map/prepare/pallas_call | solution.py:424
  25.0 2.2 %prepare.5 = (bf16[3,9,128,256]{3,2,1,0:T(8,128)(2,1)S(1)}, bf16[3,9,128,256]{3,2,1,0:T(8,128)(2,1)S(1)}, f32[4,96,256]{2,1,0:T(8,128)S(1)}) custom-call(s32[1,4,7]{2,1,0:T(4,128)S(1)} %get-tuple-element.25.own_cols, s32[1,4,7]{2,1,0:T(4,128)S(1)} %collective-permute-done.4.other_cols, f32[1,4,7,2,128,128]{5,4,3,2,1,0:T(8,128)} %own.5, ...), custom_call_target="tpu_custom_call" | custom-call | flops 75497472 | bytes 3670016 | tf_op jit(solution)/shard_map/prepare/pallas_call | solution.py:424
  27.2 0.0 collective-permute-done.9.diagonal
  27.2 0.0 collective-permute-done.6.swapped
  27.2 0.0 collective-permute-done.8.relayed
  27.2 1.2 %bottom.1 = f32[3,2,16,512]{3,2,1,0:T(8,128)} custom-call(f32[96,256]{1,0:T(8,128)S(1)} %collective-permute-done.6.swapped, f32[96,256]{1,0:T(8,128)S(1)} %collective-permute-done.8.relayed, f32[96,256]{1,0:T(8,128)S(1)} %collective-permute-done.9.diagonal, bf16[1,9,128,256]{3,2,1,0:T(8,128)(2,1)S(1)} %get-tuple-element.35.refs_3_.refs_0_, ...), custom_call_target="tpu_custom_call" | custom-call | flops 37748736 | bytes 917504 | tf_op jit(solution)/shard_map/bottom/pallas_call | solution.py:479
Async XLA Ops:
  0.0 10.0 %copy-start = (s32[1,4,7]{2,1,0:T(4,128)S(1)}, s32[1,4,7]{2,1,0:T(4,128)}, u32[]{:S(2)}) copy-start(s32[1,4,7]{2,1,0:T(4,128)} %refs_0_.3) | copy-start | bytes 340
  0.0 11.2 %collective-permute-start.5 = (f32[1,4,7,2,128,128]{5,4,3,2,1,0:T(8,128)}, f32[1,4,7,2,128,128]{5,4,3,2,1,0:T(8,128)S(1)}, u32[]{:S(2)}, u32[]{:S(2)}) collective-permute-start(f32[1,4,7,2,128,128]{5,4,3,2,1,0:T(8,128)} %own.5), channel_id=1, source_target_pairs={{0,8},{8,0},{1,9},{9,1},{2,10},{10,2},{3,11},{11,3},{4,12},{12,4},... | collective-permute-start | bytes 11010056 | tf_op jit(solution)/shard_map/ppermute | solution.py:374
  1.5 7.0 %collective-permute-start.1 = (f32[96,256]{1,0:T(8,128)S(1)}, f32[96,256]{1,0:T(8,128)S(1)}, u32[]{:S(2)}, u32[]{:S(2)}) collective-permute-start(f32[96,256]{1,0:T(8,128)S(1)} %get-tuple-element.24.refs_0_), channel_id=1, source_target_pairs={{0,1},{2,3},{4,5},{6,7},{8,9},{10,11},{12,13},{14,15},{1,0},{3,2},... | collective-permute-start | bytes 294920 | tf_op jit(solution)/shard_map/ppermute | solution.py:367
  5.4 9.2 %collective-permute-start.3 = (f32[96,256]{1,0:T(8,128)S(1)}, f32[96,256]{1,0:T(8,128)S(1)}, u32[]{:S(2)}, u32[]{:S(2)}) collective-permute-start(f32[96,256]{1,0:T(8,128)S(1)} %get-tuple-element.23.refs_1_), channel_id=1, source_target_pairs={{1,2},{3,4},{5,6},{9,10},{11,12},{13,14},{0,8},{7,15},{2,1},{4,3},... | collective-permute-start | bytes 294920 | tf_op jit(solution)/shard_map/ppermute | solution.py:370
  5.6 9.0 %collective-permute-start = (f32[96,256]{1,0:T(8,128)S(1)}, f32[96,256]{1,0:T(8,128)S(1)}, u32[]{:S(2)}, u32[]{:S(2)}) collective-permute-start(f32[96,256]{1,0:T(8,128)S(1)} %get-tuple-element.23.refs_1_), channel_id=1, source_target_pairs={{0,1},{2,3},{4,5},{6,7},{8,9},{10,11},{12,13},{14,15},{1,0},{3,2},... | collective-permute-start | bytes 294920 | tf_op jit(solution)/shard_map/ppermute | solution.py:369
  8.5 6.1 %collective-permute-start.2 = (f32[96,256]{1,0:T(8,128)S(1)}, f32[96,256]{1,0:T(8,128)S(1)}, u32[]{:S(2)}, u32[]{:S(2)}) collective-permute-start(f32[96,256]{1,0:T(8,128)S(1)} %collective-permute-done.1.refs_2_), channel_id=1, source_target_pairs={{0,2},{2,4},{4,6},{3,1},{5,3},{7,5},{6,7},{1,0},{8,10},{10,12},{12... | collective-permute-start | bytes 294920 | tf_op jit(solution)/shard_map/ppermute | solution.py:371
  10.0 1.2 %collective-permute-start.4 = (s32[1,4,7]{2,1,0:T(4,128)S(1)}, s32[1,4,7]{2,1,0:T(4,128)S(1)}, u32[]{:S(2)}, u32[]{:S(2)}) collective-permute-start(s32[1,4,7]{2,1,0:T(4,128)S(1)} %copy-done), channel_id=1, source_target_pairs={{0,8},{8,0},{1,9},{9,1},{2,10},{10,2},{3,11},{11,3},{4,12},{12,4},... | collective-permute-start | bytes 344 | tf_op jit(solution)/shard_map/ppermute | solution.py:375
  15.0 5.5 %collective-permute-start.7 = (f32[96,256]{1,0:T(8,128)S(1)}, f32[96,256]{1,0:T(8,128)S(1)}, u32[]{:S(2)}, u32[]{:S(2)}) collective-permute-start(f32[96,256]{1,0:T(8,128)S(1)} %get-tuple-element.34.refs_0_), channel_id=1, source_target_pairs={{0,1},{2,3},{4,5},{6,7},{8,9},{10,11},{12,13},{14,15},{1,0},{3,2},... | collective-permute-start | bytes 294920 | tf_op jit(solution)/shard_map/ppermute | solution.py:367
  15.7 11.4 %collective-permute-start.9 = (f32[96,256]{1,0:T(8,128)S(1)}, f32[96,256]{1,0:T(8,128)S(1)}, u32[]{:S(2)}, u32[]{:S(2)}) collective-permute-start(f32[96,256]{1,0:T(8,128)S(1)} %second_rows.1.refs_1_), channel_id=1, source_target_pairs={{1,2},{3,4},{5,6},{9,10},{11,12},{13,14},{0,8},{7,15},{2,1},{4,3},... | collective-permute-start | bytes 294920 | tf_op jit(solution)/shard_map/ppermute | solution.py:370
  15.8 11.4 %collective-permute-start.6 = (f32[96,256]{1,0:T(8,128)S(1)}, f32[96,256]{1,0:T(8,128)S(1)}, u32[]{:S(2)}, u32[]{:S(2)}) collective-permute-start(f32[96,256]{1,0:T(8,128)S(1)} %second_rows.1.refs_1_), channel_id=1, source_target_pairs={{0,1},{2,3},{4,5},{6,7},{8,9},{10,11},{12,13},{14,15},{1,0},{3,2},... | collective-permute-start | bytes 294920 | tf_op jit(solution)/shard_map/ppermute | solution.py:369
  20.5 6.7 %collective-permute-start.8 = (f32[96,256]{1,0:T(8,128)S(1)}, f32[96,256]{1,0:T(8,128)S(1)}, u32[]{:S(2)}, u32[]{:S(2)}) collective-permute-start(f32[96,256]{1,0:T(8,128)S(1)} %collective-permute-done.7.refs_2_), channel_id=1, source_target_pairs={{0,2},{2,4},{4,6},{3,1},{5,3},{7,5},{6,7},{1,0},{8,10},{10,12},{12... | collective-permute-start | bytes 294920 | tf_op jit(solution)/shard_map/ppermute | solution.py:371

commit v11 on v8

--- a/solution.py
+++ b/solution.py
@@ -53,14 +53,6 @@
     total[...] = entered(held, coef)
 
 
-def fetch_kernel(table, out, sems):
-    count = out.shape[1]
-    for i in range(count):
-        pltpu.make_async_copy(table.at[0, i], out.at[0, i], sems.at[i]).start()
-    for i in range(count):
-        pltpu.make_async_copy(table.at[0, i], out.at[0, i], sems.at[i]).wait()
-
-
 def head_and_tail(value):
     head = value.astype(jnp.bfloat16)
     return head, (value - head.astype(jnp.float32)).astype(jnp.bfloat16)
@@ -176,7 +168,7 @@
                     low[i, at[j], part] = tail
                 return carry
 
-            lax.fori_loop(0, size // 16, split, 0, unroll=2)
+            lax.fori_loop(0, size // 16, split, 0, unroll=4)
 
         direct = jnp.logical_not(copied)
 
@@ -401,20 +393,10 @@
     coefs = []
 
     def enter_second():
-        part_total, coef = enter(second_rows)
-        coefs.append(coef)
+        part_total, coef, near = enter(second_rows, (blocks, half))
+        coefs.extend((coef, near))
         return part_total
 
-    near = pl.pallas_call(
-        fetch_kernel,
-        out_shape=jax.ShapeDtypeStruct((1, half) + blocks.shape[2:], f32),
-        in_specs=[HBM],
-        out_specs=VMEM,
-        scratch_shapes=[pltpu.SemaphoreType.DMA((half,))],
-        compiler_params=params(8),
-        cost_estimate=cost(0, 2 * blocks.size),
-        name="fetch",
-    )(in_hbm(blocks))
     first_total, coef, own_cols = enter(first_rows, (block_cols, block_rows))
     coefs.append(coef)
     second_total, early, late = exchange(first_total, enter_second)
@@ -422,7 +404,7 @@
     macs = 6 * channels * points * 2 * size
 
     every_row = range(block_rows)
-    row_groups = ((every_row,), (every_row[:1], every_row[1:half], every_row[half:]))
+    row_groups = ((every_row,), (every_row[:1], every_row[1:]))
 
     def prepare(level, rows, fields, halo, ready):
         band = jax.ShapeDtypeStruct((len(rows), 2 * block_rows + 1, size, 2 * size), bf16)
@@ -443,7 +425,7 @@
             compiler_params=params(16),
             cost_estimate=cost(2 * macs, 4 * blocks.size),
             name="prepare",
-        )(own_cols, other_cols, in_hbm(blocks), near, other_blocks, *operands)
+        )(own_cols, other_cols, in_hbm(blocks), coefs[2], other_blocks, *operands)
 
     def early_products(level, halo, *fields):
         ready = []

time: 28.5 us -> 29.3 us (1.028)
  starting transfers between devices: 9.94 us -> 14 us
  Pallas kernels: 13.1 us -> 11.5 us
  waiting for transfers between devices: 5.15 us -> 3.57 us
    ppermute x2, starting transfers between devices: 2.08 us -> 5.28 us  [exchange(): second_swapped = lax.ppermute(second, axes, beside)]
    ppermute x2, waiting for transfers between devices: 5.13 us -> 2.39 us  [exchange(): first_swapped = lax.ppermute(first, axes, beside)]
    pallas_call x1 -> x0, Pallas kernels: 1.47 us -> none  [per_device(): pl.pallas_call(fetch_kernel, out_shape=jax.ShapeDtypeStruct((1, half) + b...]
    ppermute x1, waiting for transfers between devices: 0.01 us -> 1.16 us  [per_device(): other_cols = lax.ppermute(block_cols, 'depth', over_depth)]
    pallas_call x4 -> x3, Pallas kernels: 7.8 us -> 7.02 us  [prepare(): pl.pallas_call(functools.partial(prepare_kernel, level, rows, len(halo),...]
    pallas_call x2, Pallas kernels: 1.9 us -> 2.61 us  [enter(): pl.pallas_call(functools.partial(enter_kernel, rows[0] * size, len(tables...]
    ppermute x2, starting transfers between devices: 4.12 us -> 4.8 us  [exchange(): relayed = lax.ppermute(first_swapped, axes, onward)]
  transfers between devices with their start and end apart: 10 -> 10, of which waited for: 2 -> 2; matrix products, arithmetic and copies ran while one was open for 0% -> 0% of each run, Pallas kernels for 41% -> 34%
where the time goes in v11:
time: 29.3 us; the launch traced here: 29.2 us
  starting transfers between devices  14 us (48%)
  Pallas kernels  11.5 us (39%)
  waiting for transfers between devices  3.57 us (12%)
    pallas_call x3, Pallas kernels, prepare(): pl.pallas_call(functools.partial(prepare_kernel, level, rows, len(halo),...  7.02 us
    ppermute x2, starting transfers between devices, exchange(): second_swapped = lax.ppermute(second, axes, beside)  5.28 us
    ppermute x2, starting transfers between devices, exchange(): relayed = lax.ppermute(first_swapped, axes, onward)  4.8 us
    ppermute x2, starting transfers between devices, exchange(): first_swapped = lax.ppermute(first, axes, beside)  2.82 us
    pallas_call x2, Pallas kernels, enter(): pl.pallas_call(functools.partial(enter_kernel, rows[0] * size, len(tables...  2.61 us
    ppermute x2, waiting for transfers between devices, exchange(): first_swapped = lax.ppermute(first, axes, beside)  2.39 us
    pallas_call x1, Pallas kernels, per_device(): pl.pallas_call(functools.partial(bottom_kernel, len(row_groups[1])), out_...  1.2 us
    ppermute x1, waiting for transfers between devices, per_device(): other_cols = lax.ppermute(block_cols, 'depth', over_depth)  1.16 us
  transfers between devices with their start and end apart: 10, of which 2 were waited for; matrix products, arithmetic and copies ran while one was open for 0% of the time, Pallas kernels for 34%

profile of v11, /device:TPU:0, one launch (start us, length us, event | category | flops | bytes accessed | tf_op | source)
XLA Modules:
  0.0 29.2 jit_solution(12561556135664472519)
XLA Ops:
  0.0 0.0 copy-start
  0.0 0.5 %collective-permute-start.5 = (f32[1,4,7,2,128,128]{5,4,3,2,1,0:T(8,128)}, f32[1,4,7,2,128,128]{5,4,3,2,1,0:T(8,128)S(1)}, u32[]{:S(2)}, u32[]{:S(2)}) collective-permute-start(f32[1,4,7,2,128,128]{5,4,3,2,1,0:T(8,128)} %own.5), channel_id=1, source_target_pairs={{0,8},{8,0},{1,9},{9,1},{2,10},{10,2},{3,11},{11,3},{4,12},{12,4},... | collective-permute-start | bytes 11010056 | tf_op jit(solution)/shard_map/ppermute | solution.py:364
  0.5 1.0 %enter.3 = (f32[96,256]{1,0:T(8,128)S(1)}, f32[2,256]{1,0:T(2,128)S(1)}, s32[1,4,7]{2,1,0:T(4,128)S(1)}) custom-call(f32[3,2,16,512]{3,2,1,0:T(8,128)} %sources.3, s32[1,512]{1,0:T(1,128)} %bitcast.1, f32[2,512]{1,0:T(2,128)} %refl_coef.3, s32[1,4,7]{2,1,0:T(4,128)} %refs_0_.3), custom_call_target="tpu_custom_call" | custom-call | tf_op jit(solution)/shard_map/enter/pallas_call | solution.py:370
  1.5 2.6 %collective-permute-start.1 = (f32[96,256]{1,0:T(8,128)S(1)}, f32[96,256]{1,0:T(8,128)S(1)}, u32[]{:S(2)}, u32[]{:S(2)}) collective-permute-start(f32[96,256]{1,0:T(8,128)S(1)} %get-tuple-element.24.refs_0_), channel_id=1, source_target_pairs={{0,1},{2,3},{4,5},{6,7},{8,9},{10,11},{12,13},{14,15},{1,0},{3,2},... | collective-permute-start | bytes 294920 | tf_op jit(solution)/shard_map/ppermute | solution.py:357
  4.0 1.6 %enter.2 = (f32[96,256]{1,0:T(8,128)S(1)}, f32[2,256]{1,0:T(2,128)S(1)}, f32[1,2,7,2,128,128]{5,4,3,2,1,0:T(8,128)S(1)}) custom-call(f32[3,2,16,512]{3,2,1,0:T(8,128)} %sources.3, s32[1,512]{1,0:T(1,128)} %bitcast.2, f32[2,512]{1,0:T(2,128)} %refl_coef.3, f32[1,4,7,2,128,128]{5,4,3,2,1,0:T(8,128)} %own.5), custom_call_target="tpu_custom_call" | custom-call | tf_op jit(solution)/shard_map/enter/pallas_call | solution.py:370
  5.7 0.3 collective-permute-start.3
  6.0 2.8 %collective-permute-start = (f32[96,256]{1,0:T(8,128)S(1)}, f32[96,256]{1,0:T(8,128)S(1)}, u32[]{:S(2)}, u32[]{:S(2)}) collective-permute-start(f32[96,256]{1,0:T(8,128)S(1)} %get-tuple-element.23.refs_1_), channel_id=1, source_target_pairs={{0,1},{2,3},{4,5},{6,7},{8,9},{10,11},{12,13},{14,15},{1,0},{3,2},... | collective-permute-start | bytes 294920 | tf_op jit(solution)/shard_map/ppermute | solution.py:359
  8.8 0.0 collective-permute-done.1.refs_2_
  8.8 1.6 %collective-permute-start.2 = (f32[96,256]{1,0:T(8,128)S(1)}, f32[96,256]{1,0:T(8,128)S(1)}, u32[]{:S(2)}, u32[]{:S(2)}) collective-permute-start(f32[96,256]{1,0:T(8,128)S(1)} %collective-permute-done.1.refs_2_), channel_id=1, source_target_pairs={{0,2},{2,4},{4,6},{3,1},{5,3},{7,5},{6,7},{1,0},{8,10},{10,12},{12... | collective-permute-start | bytes 294920 | tf_op jit(solution)/shard_map/ppermute | solution.py:361
  10.4 0.0 copy-done
  10.4 0.0 collective-permute-start.4
  10.4 1.2 %collective-permute-done.4.other_cols = s32[1,4,7]{2,1,0:T(4,128)S(1)} collective-permute-done((s32[1,4,7]{2,1,0:T(4,128)S(1)}, s32[1,4,7]{2,1,0:T(4,128)S(1)}, u32[]{:S(2)}, u32[]{:S(2)}) %collective-permute-start.4) | collective-permute-done | bytes 144 | tf_op jit(solution)/shard_map/ppermute | solution.py:365
  11.5 0.0 collective-permute-done.5.received
  11.5 3.2 %prepare.3 = (bf16[4,9,128,256]{3,2,1,0:T(8,128)(2,1)S(1)}, bf16[4,9,128,256]{3,2,1,0:T(8,128)(2,1)S(1)}, f32[4,96,256]{2,1,0:T(8,128)S(1)}) custom-call(s32[1,4,7]{2,1,0:T(4,128)S(1)} %get-tuple-element.25.own_cols, s32[1,4,7]{2,1,0:T(4,128)S(1)} %collective-permute-done.4.other_cols, f32[1,4,7,2,128,128]{5,4,3,2,1,0:T(8,128)} %own.5, ...), custom_call_target="tpu_custom_call" | custom-call | flops 75497472 | bytes 3670016 | tf_op jit(solution)/shard_map/prepare/pallas_call | solution.py:414
  14.8 0.0 collective-permute-done.3.diagonal
  14.8 0.0 collective-permute-done.swapped
  14.8 0.0 collective-permute-done.2.relayed
  14.8 0.4 %first_rows.1 = (f32[96,256]{1,0:T(8,128)S(1)}, bf16[192,256]{1,0:T(8,128)(2,1)S(1)}, bf16[192,512]{1,0:T(8,128)(2,1)S(1)}) custom-call(f32[96,256]{1,0:T(8,128)S(1)} %collective-permute-done.swapped, f32[96,256]{1,0:T(8,128)S(1)} %collective-permute-done.2.relayed, f32[96,256]{1,0:T(8,128)S(1)} %collective-permute-done.3.diagonal, ...), custom_call_target="tpu_custom_call" | custom-call | flops 37748736 | bytes 917504 | tf_op jit(solution)/shard_map/first_rows/pallas_call | solution.py:442
  15.2 0.3 collective-permute-start.7
  15.4 0.3 %second_rows.1.refs_1_ = f32[96,256]{1,0:T(8,128)S(1)} custom-call(bf16[192,256]{1,0:T(8,128)(2,1)S(1)} %get-tuple-element.31.swapped, bf16[192,512]{1,0:T(8,128)(2,1)S(1)} %get-tuple-element.32.diagonal, bf16[4,9,128,256]{3,2,1,0:T(8,128)(2,1)S(1)} %get-tuple-element.27.refs_0_, bf16[4,9,128,256]{3,2,1,0:T(8,128)(2,1)S(1)} %get-tuple-element.28.refs_1_, ...), custom_call_target="tpu_custom_call" | custom-call | flops 37748736 | bytes 917504 | tf_op jit(solution)/shard_map/second_rows/pallas_call | solution.py:457
  15.8 0.3 collective-permute-start.9
  16.1 2.5 %collective-permute-start.6 = (f32[96,256]{1,0:T(8,128)S(1)}, f32[96,256]{1,0:T(8,128)S(1)}, u32[]{:S(2)}, u32[]{:S(2)}) collective-permute-start(f32[96,256]{1,0:T(8,128)S(1)} %second_rows.1.refs_1_), channel_id=1, source_target_pairs={{0,1},{2,3},{4,5},{6,7},{8,9},{10,11},{12,13},{14,15},{1,0},{3,2},... | collective-permute-start | bytes 294920 | tf_op jit(solution)/shard_map/ppermute | solution.py:359
  18.5 2.4 %collective-permute-done.7.refs_2_ = f32[96,256]{1,0:T(8,128)S(1)} collective-permute-done((f32[96,256]{1,0:T(8,128)S(1)}, f32[96,256]{1,0:T(8,128)S(1)}, u32[]{:S(2)}, u32[]{:S(2)}) %collective-permute-start.7) | collective-permute-done | bytes 98336 | tf_op jit(solution)/shard_map/ppermute | solution.py:357
  20.9 3.2 %collective-permute-start.8 = (f32[96,256]{1,0:T(8,128)S(1)}, f32[96,256]{1,0:T(8,128)S(1)}, u32[]{:S(2)}, u32[]{:S(2)}) collective-permute-start(f32[96,256]{1,0:T(8,128)S(1)} %collective-permute-done.7.refs_2_), channel_id=1, source_target_pairs={{0,2},{2,4},{4,6},{3,1},{5,3},{7,5},{6,7},{1,0},{8,10},{10,12},{12... | collective-permute-start | bytes 294920 | tf_op jit(solution)/shard_map/ppermute | solution.py:361
  24.1 1.4 %prepare.4 = (bf16[1,9,128,256]{3,2,1,0:T(8,128)(2,1)S(1)}, bf16[1,9,128,256]{3,2,1,0:T(8,128)(2,1)S(1)}, f32[1,96,256]{2,1,0:T(8,128)S(1)}) custom-call(s32[1,4,7]{2,1,0:T(4,128)S(1)} %get-tuple-element.25.own_cols, s32[1,4,7]{2,1,0:T(4,128)S(1)} %collective-permute-done.4.other_cols, f32[1,4,7,2,128,128]{5,4,3,2,1,0:T(8,128)} %own.5, ...), custom_call_target="tpu_custom_call" | custom-call | flops 75497472 | bytes 3670016 | tf_op jit(solution)/shard_map/prepare/pallas_call | solution.py:414
  25.6 2.3 %prepare.5 = (bf16[3,9,128,256]{3,2,1,0:T(8,128)(2,1)S(1)}, bf16[3,9,128,256]{3,2,1,0:T(8,128)(2,1)S(1)}, f32[4,96,256]{2,1,0:T(8,128)S(1)}) custom-call(s32[1,4,7]{2,1,0:T(4,128)S(1)} %get-tuple-element.25.own_cols, s32[1,4,7]{2,1,0:T(4,128)S(1)} %collective-permute-done.4.other_cols, f32[1,4,7,2,128,128]{5,4,3,2,1,0:T(8,128)} %own.5, ...), custom_call_target="tpu_custom_call" | custom-call | flops 75497472 | bytes 3670016 | tf_op jit(solution)/shard_map/prepare/pallas_call | solution.py:414
  27.9 0.0 collective-permute-done.9.diagonal
  28.0 0.0 collective-permute-done.6.swapped
  28.0 0.0 collective-permute-done.8.relayed
  28.0 1.2 %bottom.1 = f32[3,2,16,512]{3,2,1,0:T(8,128)} custom-call(f32[96,256]{1,0:T(8,128)S(1)} %collective-permute-done.6.swapped, f32[96,256]{1,0:T(8,128)S(1)} %collective-permute-done.8.relayed, f32[96,256]{1,0:T(8,128)S(1)} %collective-permute-done.9.diagonal, bf16[1,9,128,256]{3,2,1,0:T(8,128)(2,1)S(1)} %get-tuple-element.35.refs_3_.refs_0_, ...), custom_call_target="tpu_custom_call" | custom-call | flops 37748736 | bytes 917504 | tf_op jit(solution)/shard_map/bottom/pallas_call | solution.py:469
Async XLA Ops:
  0.0 10.4 %copy-start = (s32[1,4,7]{2,1,0:T(4,128)S(1)}, s32[1,4,7]{2,1,0:T(4,128)}, u32[]{:S(2)}) copy-start(s32[1,4,7]{2,1,0:T(4,128)} %refs_0_.3) | copy-start | bytes 340
  0.0 11.5 %collective-permute-start.5 = (f32[1,4,7,2,128,128]{5,4,3,2,1,0:T(8,128)}, f32[1,4,7,2,128,128]{5,4,3,2,1,0:T(8,128)S(1)}, u32[]{:S(2)}, u32[]{:S(2)}) collective-permute-start(f32[1,4,7,2,128,128]{5,4,3,2,1,0:T(8,128)} %own.5), channel_id=1, source_target_pairs={{0,8},{8,0},{1,9},{9,1},{2,10},{10,2},{3,11},{11,3},{4,12},{12,4},... | collective-permute-start | bytes 11010056 | tf_op jit(solution)/shard_map/ppermute | solution.py:364
  1.5 7.3 %collective-permute-start.1 = (f32[96,256]{1,0:T(8,128)S(1)}, f32[96,256]{1,0:T(8,128)S(1)}, u32[]{:S(2)}, u32[]{:S(2)}) collective-permute-start(f32[96,256]{1,0:T(8,128)S(1)} %get-tuple-element.24.refs_0_), channel_id=1, source_target_pairs={{0,1},{2,3},{4,5},{6,7},{8,9},{10,11},{12,13},{14,15},{1,0},{3,2},... | collective-permute-start | bytes 294920 | tf_op jit(solution)/shard_map/ppermute | solution.py:357
  5.7 9.1 %collective-permute-start.3 = (f32[96,256]{1,0:T(8,128)S(1)}, f32[96,256]{1,0:T(8,128)S(1)}, u32[]{:S(2)}, u32[]{:S(2)}) collective-permute-start(f32[96,256]{1,0:T(8,128)S(1)} %get-tuple-element.23.refs_1_), channel_id=1, source_target_pairs={{1,2},{3,4},{5,6},{9,10},{11,12},{13,14},{0,8},{7,15},{2,1},{4,3},... | collective-permute-start | bytes 294920 | tf_op jit(solution)/shard_map/ppermute | solution.py:360
  6.0 8.8 %collective-permute-start = (f32[96,256]{1,0:T(8,128)S(1)}, f32[96,256]{1,0:T(8,128)S(1)}, u32[]{:S(2)}, u32[]{:S(2)}) collective-permute-start(f32[96,256]{1,0:T(8,128)S(1)} %get-tuple-element.23.refs_1_), channel_id=1, source_target_pairs={{0,1},{2,3},{4,5},{6,7},{8,9},{10,11},{12,13},{14,15},{1,0},{3,2},... | collective-permute-start | bytes 294920 | tf_op jit(solution)/shard_map/ppermute | solution.py:359
  8.8 6.0 %collective-permute-start.2 = (f32[96,256]{1,0:T(8,128)S(1)}, f32[96,256]{1,0:T(8,128)S(1)}, u32[]{:S(2)}, u32[]{:S(2)}) collective-permute-start(f32[96,256]{1,0:T(8,128)S(1)} %collective-permute-done.1.refs_2_), channel_id=1, source_target_pairs={{0,2},{2,4},{4,6},{3,1},{5,3},{7,5},{6,7},{1,0},{8,10},{10,12},{12... | collective-permute-start | bytes 294920 | tf_op jit(solution)/shard_map/ppermute | solution.py:361
  10.4 1.2 %collective-permute-start.4 = (s32[1,4,7]{2,1,0:T(4,128)S(1)}, s32[1,4,7]{2,1,0:T(4,128)S(1)}, u32[]{:S(2)}, u32[]{:S(2)}) collective-permute-start(s32[1,4,7]{2,1,0:T(4,128)S(1)} %copy-done), channel_id=1, source_target_pairs={{0,8},{8,0},{1,9},{9,1},{2,10},{10,2},{3,11},{11,3},{4,12},{12,4},... | collective-permute-start | bytes 344 | tf_op jit(solution)/shard_map/ppermute | solution.py:365
  15.2 5.7 %collective-permute-start.7 = (f32[96,256]{1,0:T(8,128)S(1)}, f32[96,256]{1,0:T(8,128)S(1)}, u32[]{:S(2)}, u32[]{:S(2)}) collective-permute-start(f32[96,256]{1,0:T(8,128)S(1)} %get-tuple-element.34.refs_0_), channel_id=1, source_target_pairs={{0,1},{2,3},{4,5},{6,7},{8,9},{10,11},{12,13},{14,15},{1,0},{3,2},... | collective-permute-start | bytes 294920 | tf_op jit(solution)/shard_map/ppermute | solution.py:357
  15.8 12.2 %collective-permute-start.9 = (f32[96,256]{1,0:T(8,128)S(1)}, f32[96,256]{1,0:T(8,128)S(1)}, u32[]{:S(2)}, u32[]{:S(2)}) collective-permute-start(f32[96,256]{1,0:T(8,128)S(1)} %second_rows.1.refs_1_), channel_id=1, source_target_pairs={{1,2},{3,4},{5,6},{9,10},{11,12},{13,14},{0,8},{7,15},{2,1},{4,3},... | collective-permute-start | bytes 294920 | tf_op jit(solution)/shard_map/ppermute | solution.py:360
  16.1 11.9 %collective-permute-start.6 = (f32[96,256]{1,0:T(8,128)S(1)}, f32[96,256]{1,0:T(8,128)S(1)}, u32[]{:S(2)}, u32[]{:S(2)}) collective-permute-start(f32[96,256]{1,0:T(8,128)S(1)} %second_rows.1.refs_1_), channel_id=1, source_target_pairs={{0,1},{2,3},{4,5},{6,7},{8,9},{10,11},{12,13},{14,15},{1,0},{3,2},... | collective-permute-start | bytes 294920 | tf_op jit(solution)/shard_map/ppermute | solution.py:359
  20.9 7.0 %collective-permute-start.8 = (f32[96,256]{1,0:T(8,128)S(1)}, f32[96,256]{1,0:T(8,128)S(1)}, u32[]{:S(2)}, u32[]{:S(2)}) collective-permute-start(f32[96,256]{1,0:T(8,128)S(1)} %collective-permute-done.7.refs_2_), channel_id=1, source_target_pairs={{0,2},{2,4},{4,6},{3,1},{5,3},{7,5},{6,7},{1,0},{8,10},{10,12},{12... | collective-permute-start | bytes 294920 | tf_op jit(solution)/shard_map/ppermute | solution.py:361
